TPU v7x, 512 devices: a whole 4x8x8 slice. The times are simulated.
512 devices in a mesh: ep: 128 (over y, z, core), dp: 4 (over x).
Axes of the slice: x: 4, y: 8, z: 8, core: 2. Of those that a mesh axis runs over, the one named last changes fastest.
Arguments:
- activations: float32 [256, 256, 768], P('ep', 'dp'), may hold values from -6 to 6
- out_grads: float32 [256, 256, 512], P('ep', 'dp'), may hold values from -6 to 6
- counts: int32 [256, 4], P('ep', 'dp'), may hold values from 1 to 64
- slot_weights: float32 [256, 768, 512], P('ep', None, 'dp'), may hold values from -0.21875 to 0.21875
- master: float32 [128, 768, 512], P(None, 'ep', 'dp'), may hold values from -0.21875 to 0.21875
- moment_one: float32 [128, 768, 512], P(None, 'ep', 'dp'), may hold values from -6 to 6
- moment_two: float32 [128, 768, 512], P(None, 'ep', 'dp'), may hold values from 1 to 100
- old_table: int32 [256, 1], replicated, may hold values from 0 to 127
- new_table: int32 [256, 1], replicated, may hold values from 0 to 127
Outputs:
- outputs: float32 [256, 256, 512], P('ep', 'dp')
- input_grads: float32 [256, 256, 768], P('ep', 'dp')
- new_master: float32 [128, 768, 512], P(None, 'ep', 'dp')
- new_moment_one: float32 [128, 768, 512], P(None, 'ep', 'dp')
- new_moment_two: float32 [128, 768, 512], P(None, 'ep', 'dp')
- new_slots: float32 [256, 768, 512], P('ep', None, 'dp')
Inputs may be any that keep to these rules, and one draw needn't show every extreme that they name: `old_table`: every expert is named by at least one old slot. `new_table`: every expert is named by at least one new slot.
All inputs are finite; a program needn't handle non-finite values.
Results may differ from a plain program's by a relative error of at most 0.00007.
Values sent between devices are 32-bit elements; how exact they have to be, the bound alone decides.
No kernel may reach another device: no remote copies, remote signals or barrier semaphores. Data moves between devices by JAX's collectives and lax.ppermute only.
A program may use at most 64 MiB of HBM per device.

v0:
```python
import jax
import jax.numpy as jnp
from jax import lax
from jax.sharding import PartitionSpec as P

STEP = 100


beta_one = 0.9
beta_two = 0.999
learn_rate = 0.02
epsilon = 1e-08
decay_rate = 0.1


def adamw(master, moment_one, moment_two, expert_grad):
    first_new = beta_one * moment_one + (1.0 - beta_one) * expert_grad
    second_new = beta_two * moment_two + (1.0 - beta_two) * expert_grad * expert_grad
    first_hat = first_new / (1.0 - beta_one**STEP)
    second_hat = second_new / (1.0 - beta_two**STEP)
    updated = master - learn_rate * (
        first_hat / (jnp.sqrt(second_hat) + epsilon) + decay_rate * master
    )
    return (updated, first_new, second_new)


def local(
    activations,
    out_grads,
    counts,
    slot_weights,
    master,
    moment_one,
    moment_two,
    old_table,
    new_table,
):
    precise = lax.Precision.HIGHEST
    experts_ids = jnp.arange(master.shape[0], dtype=jnp.int32)
    old_onehot = (old_table[:, 0][None, :] == experts_ids[:, None]).astype(jnp.float32)
    positions = jnp.arange(activations.shape[1], dtype=jnp.int32)
    live_rows = (positions[None, :] < counts).astype(jnp.float32)
    masked_acts = activations * live_rows[:, :, None]
    masked_grads = out_grads * live_rows[:, :, None]
    whole_weights = lax.all_gather(slot_weights, "dp", axis=2, tiled=True)
    outputs = jnp.einsum("srf,sfd->srd", masked_acts, whole_weights, precision=precise)
    input_grads = jnp.einsum("srd,sfd->srf", masked_grads, whole_weights, precision=precise)
    every_act = lax.all_gather(masked_acts, "dp", axis=1, tiled=True)
    own_columns = lax.all_to_all(masked_grads, "dp", split_axis=2, concat_axis=1, tiled=True)
    column_grad = jnp.einsum("srf,srd->sfd", every_act, own_columns, precision=precise)
    arrived = lax.all_to_all(column_grad, "ep", split_axis=1, concat_axis=0, tiled=True)
    expert_grad = jnp.einsum("es,sfd->efd", old_onehot, arrived, precision=precise)
    new_master, new_moment_one, new_moment_two = adamw(master, moment_one, moment_two, expert_grad)
    new_onehot = (new_table[:, 0][:, None] == experts_ids[None, :]).astype(jnp.float32)
    picked = jnp.einsum("se,efd->sfd", new_onehot, new_master, precision=precise)
    new_slots = lax.all_to_all(picked, "ep", split_axis=0, concat_axis=1, tiled=True)
    return (outputs, input_grads, new_master, new_moment_one, new_moment_two, new_slots)


def solution(mesh):
    in_specs = (
        P("ep", "dp", None),
        P("ep", "dp", None),
        P("ep", "dp"),
        P("ep", None, "dp"),
        P(None, "ep", "dp"),
        P(None, "ep", "dp"),
        P(None, "ep", "dp"),
        P(),
        P(),
    )
    out_specs = (
        P("ep", "dp", None),
        P("ep", "dp", None),
        P(None, "ep", "dp"),
        P(None, "ep", "dp"),
        P(None, "ep", "dp"),
        P("ep", None, "dp"),
    )
    return jax.shard_map(local, mesh=mesh, in_specs=in_specs, out_specs=out_specs, check_vma=False)
```

profile of v0, /device:TPU:1, one launch (start us, length us, event | category | flops | bytes accessed | tf_op | source)
XLA Modules:
  0.0 141.3 jit_solution(7682760392878343886)
XLA Ops:
  7.2 0.0 all-gather.5.cloned.1.call-start
  7.2 0.7 compare_convert_fusion
  7.9 1.8 %broadcast_multiply_fusion = f32[2,64,768]{2,1,0:T(8,128)} fusion(f32[2,64,768]{2,1,0:T(8,128)} %param.9, f32[2,64]{1,0:T(2,128)S(1)} %compare_convert_fusion), kind=kLoop, calls=%fused_computation.4 | loop fusion | flops 98304 | bytes 786944 | tf_op jit(solution)/shard_map/mul | solution.py:43
  9.8 0.0 all-gather.5.cloned.1.call-update
  9.8 0.0 all-gather.3.cloned.1.call-start
  9.8 0.7 all-gather.3.cloned.1.call-update
  10.5 1.0 broadcast_multiply_fusion.1
  11.6 0.2 copy.31
  11.8 0.6 reshape.38
  12.4 10.2 %all_to_all.54 = f32[4,1,16384]{2,1,0:T(1,128)S(1)} all-to-all(f32[4,1,16384]{2,1,0:T(1,128)S(1)} %reshape.38), channel_id=1, replica_groups=mesh['ep'=128,'dp'=4] {'dp'}, dimensions={0} | all-to-all | bytes 524288 | tf_op jit(solution)/shard_map/all_to_all | solution.py:49
  22.6 0.5 broadcast.23
  23.1 1.4 reduce
  24.4 0.4 reshape.39
  24.9 0.2 copy.32
  25.1 23.0 %all-gather.5.cloned.1.call-done = f32[2,256,768]{2,1,0:T(8,128)} async-done(((f32[2,64,768]{2,1,0:T(8,128)}), f32[2,256,768]{2,1,0:T(8,128)}) %all-gather.5.cloned.1.call-update) | async-done | bytes 1572880 | tf_op jit(solution)/shard_map/all_gather | solution.py:48
  48.0 0.0 copy-start.3
  48.0 0.0 copy-start.4
  48.0 0.0 copy-start.5
  48.0 0.0 copy-start.6
  48.0 4.1 %fusion.12 = f32[2,768,128]{2,1,0:T(8,128)S(1)} fusion(f32[2,256,768]{2,1,0:T(8,128)} %all-gather.5.cloned.1.call-done, f32[2,256,128]{2,1,0:T(8,128)S(1)} %bitcast.39), kind=kOutput, calls=%fused_computation.17 | convolution fusion | flops 603979776 | bytes 2621440 | tf_op jit(solution)/shard_map/srf,srd->sfd/dot_general | solution.py:50
  52.2 0.6 copy.33
  52.8 0.0 copy-start.7
  52.8 39.2 %all_to_all.55 = f32[2,768,128]{2,0,1:T(2,128)S(1)} all-to-all(f32[2,768,128]{2,0,1:T(2,128)S(1)} %copy.33), channel_id=1, replica_groups=mesh['ep'=128,'dp'=4] {'ep'}, dimensions={1} | all-to-all | bytes 1572864 | tf_op jit(solution)/shard_map/all_to_all | solution.py:51
  92.0 0.3 copy.34
  92.3 0.0 copy-done.3
  92.3 0.0 copy-done.4
  92.3 0.0 copy-done.5
  92.3 0.0 copy-done.6
  92.4 1.5 %multiply_subtract_fusion = (f32[128,6,128]{2,0,1:T(8,128)S(1)}, f32[128,6,128]{2,0,1:T(8,128)}, f32[128,6,128]{2,0,1:T(8,128)}) fusion(f32[128,6,128]{2,0,1:T(8,128)S(1)} %copy-done.3, f32[128,6,128]{2,0,1:T(8,128)S(1)} %copy-done.4, f32[128,6,128]{2,0,1:T(8,128)S(1)} %copy-done.5, f32[256,6,128]{2,0,1:T(8,128)S(1)} %bitcast.36, s32[256]{0:T(256)S(1)} %bitcast.40), kind=kOutput, calls=%fused_computation.2 | convolution fusion | flops 303497216 | bytes 3146752 | tf_op jit(solution)/shard_map/es,sfd->efd/dot_general | solution.py:52
  93.9 0.0 copy-start.2
  93.9 0.0 copy-start.1
  93.9 0.0 copy-done.7
  93.9 0.5 fusion.5
  94.4 1.5 %copy.35 = f32[256,6,128]{2,1,0:T(8,128)} copy(f32[256,6,128]{2,0,1:T(8,128)S(1)} %fusion.5) | data formatting | bytes 1572864 | tf_op jit(solution)/shard_map/se,efd->sfd/dot_general | solution.py:55
  95.9 6.8 %all-to-all-start.2 = ((f32[256,6,128]{2,1,0:T(8,128)}), f32[256,6,128]{2,1,0:T(8,128)S(1)}, u32[]{:S(2)}, u32[]{:S(2)}) async-start(f32[256,6,128]{2,1,0:T(8,128)} %copy.35), calls=%async_computation.2 | async-start | bytes 2097152 | tf_op jit(solution)/shard_map/all_to_all | solution.py:56
  102.7 0.0 all-gather.3.cloned.1.call-done
  102.8 0.0 copy-done.1
  102.8 0.0 copy-start
  102.8 4.8 %fusion.10 = f32[2,64,512]{2,1,0:T(8,128)} fusion(f32[2,64,768]{2,1,0:T(8,128)S(1)} %copy-done.1, f32[2,768,512]{2,1,0:T(8,128)} %all-gather.3.cloned.1.call-done), kind=kOutput, calls=%fused_computation.15 | convolution fusion | flops 603979776 | bytes 3801088 | tf_op jit(solution)/shard_map/srf,sfd->srd/dot_general | solution.py:46
  107.5 0.0 copy-done.2
  107.5 0.0 copy-done
  107.5 3.9 %fusion.11 = f32[2,64,768]{2,1,0:T(8,128)} fusion(f32[2,64,512]{2,1,0:T(8,128)S(1)} %broadcast_multiply_fusion.1, f32[2,768,512]{2,1,0:T(8,128)S(1)} %copy-done), kind=kOutput, calls=%fused_computation.16 | convolution fusion | flops 603979776 | bytes 3801088 | tf_op jit(solution)/shard_map/srd,sfd->srf/dot_general | solution.py:47
  111.4 21.7 %all-to-all-done.2 = f32[256,6,128]{2,1,0:T(8,128)S(1)} async-done(((f32[256,6,128]{2,1,0:T(8,128)}), f32[256,6,128]{2,1,0:T(8,128)S(1)}, u32[]{:S(2)}, u32[]{:S(2)}) %all-to-all-start.2) | async-done | bytes 786464 | tf_op jit(solution)/shard_map/all_to_all | solution.py:56
  133.1 0.4 copy.36
  133.5 0.9 copy.37
Async XLA Ops:
  7.2 40.9 %all-gather.5.cloned.1.call-start = ((), (), s32[]{:S(2)}) async-start(), calls=%async_computation.4 | async-start | bytes 1966080 | tf_op jit(solution)/shard_map/all_gather | solution.py:48
  9.8 93.0 %all-gather.3.cloned.1.call-start = ((), (), s32[]{:S(2)}) async-start(), calls=%async_computation.3 | async-start | bytes 3932160 | tf_op jit(solution)/shard_map/all_gather | solution.py:45
  48.0 44.3 %copy-start.3 = (f32[128,6,128]{2,0,1:T(8,128)S(1)}, f32[128,6,128]{2,0,1:T(8,128)}, u32[]{:S(2)}) copy-start(f32[128,6,128]{2,0,1:T(8,128)} %param.13) | copy-start | bytes 1179652
  48.0 44.3 %copy-start.4 = (f32[128,6,128]{2,0,1:T(8,128)S(1)}, f32[128,6,128]{2,0,1:T(8,128)}, u32[]{:S(2)}) copy-start(f32[128,6,128]{2,0,1:T(8,128)} %param.14) | copy-start | bytes 1179652
  48.0 44.3 %copy-start.5 = (f32[128,6,128]{2,0,1:T(8,128)S(1)}, f32[128,6,128]{2,0,1:T(8,128)}, u32[]{:S(2)}) copy-start(f32[128,6,128]{2,0,1:T(8,128)} %param.15) | copy-start | bytes 1179652
  48.0 44.3 %copy-start.6 = (s32[256,1]{0,1:T(1,128)S(1)}, s32[256,1]{0,1:T(1,128)}, u32[]{:S(2)}) copy-start(s32[256,1]{0,1:T(1,128)} %param.16) | copy-start | bytes 3076
  52.8 41.1 %copy-start.7 = (s32[256,1]{0,1:T(1,128)S(1)}, s32[256,1]{0,1:T(1,128)}, u32[]{:S(2)}) copy-start(s32[256,1]{0,1:T(1,128)} %param.17) | copy-start | bytes 3076
  93.9 13.6 %copy-start.2 = (f32[128,6,128]{2,0,1:T(8,128)}, f32[128,6,128]{2,0,1:T(8,128)S(1)}, u32[]{:S(2)}) copy-start(f32[128,6,128]{2,0,1:T(8,128)S(1)} %get-tuple-element.24) | copy-start | bytes 1179652
  93.9 8.9 %copy-start.1 = (f32[2,64,768]{2,1,0:T(8,128)S(1)}, f32[2,64,768]{2,1,0:T(8,128)}, u32[]{:S(2)}) copy-start(f32[2,64,768]{2,1,0:T(8,128)} %broadcast_multiply_fusion) | copy-start | bytes 1179652
  95.9 37.2 %all-to-all-start.2 = ((f32[256,6,128]{2,1,0:T(8,128)}), f32[256,6,128]{2,1,0:T(8,128)S(1)}, u32[]{:S(2)}, u32[]{:S(2)}) async-start(f32[256,6,128]{2,1,0:T(8,128)} %copy.35), calls=%async_computation.2 | async-start | bytes 2097152 | tf_op jit(solution)/shard_map/all_to_all | solution.py:56
  102.8 4.8 %copy-start = (f32[2,768,512]{2,1,0:T(8,128)S(1)}, f32[2,768,512]{2,1,0:T(8,128)}, u32[]{:S(2)}) copy-start(f32[2,768,512]{2,1,0:T(8,128)} %all-gather.3.cloned.1.call-done) | copy-start | bytes 9437188
Sparse Core Ops, SparseCore 0:
  10.7 37.3 all-gather.4
  50.1 47.7 all-gather.2
where the time goes:
time: 142 us; the launch traced here: 141 us
  blocking collectives  49.4 us (35%)
  waiting for transfers between devices  45.4 us (32%)
  matrix products  14.8 us (10%)
  between operations  14.2 us (10%)
  starting transfers between devices  6.91 us (5%)
  local copies, waits for them, and re-layouts  5.63 us (4%)
  other arithmetic  4.96 us (3%)
    all_to_all x1, blocking collectives, local(): lax.all_to_all(column_grad, 'ep', split_axis=1, concat_axis=0, tiled=True)  39.2 us
    all_gather x1, waiting for transfers between devices, local(): every_act = lax.all_gather(masked_acts, 'dp', axis=1, tiled=True)  23 us
    all_to_all x1, waiting for transfers between devices, local(): lax.all_to_all(picked, 'ep', split_axis=0, concat_axis=1, tiled=True)  21.7 us
    all_to_all x1, blocking collectives, local(): lax.all_to_all(masked_grads, 'dp', split_axis=2, concat_axis=1, tiled=True)  10.2 us
    all_to_all x1, starting transfers between devices, local(): lax.all_to_all(picked, 'ep', split_axis=0, concat_axis=1, tiled=True)  6.83 us
    dot_general x1, matrix products, local(): jnp.einsum('srf,sfd->srd', masked_acts, whole_weights, precision=precise)  4.76 us
    dot_general x1, matrix products, local(): jnp.einsum('srf,srd->sfd', every_act, own_columns, precision=precise)  4.13 us
    dot_general x1, matrix products, local(): jnp.einsum('srd,sfd->srf', masked_grads, whole_weights, precision=precise)  3.89 us
  transfers between devices with their start and end apart: 3, of which 2 were waited for; matrix products, arithmetic and copies ran while one was open for 15% of the time, Pallas kernels for 0%

commit v1 on v0

v1 whole, which is shorter than its diff:
```python
import jax
import jax.numpy as jnp
from jax import lax
from jax.experimental import pallas as pl
from jax.experimental.pallas import tpu as pltpu
from jax.sharding import PartitionSpec as P

STEP = 100


beta_one = 0.9
beta_two = 0.999
learn_rate = 0.02
epsilon = 1e-08
decay_rate = 0.1

LANES = 128


def halves(x):
    high = x.astype(jnp.bfloat16)
    low = (x - high.astype(jnp.float32)).astype(jnp.bfloat16)
    return high, low


def thirds(x):
    high = x.astype(jnp.bfloat16)
    rest = x - high.astype(jnp.float32)
    middle = rest.astype(jnp.bfloat16)
    low = (rest - middle.astype(jnp.float32)).astype(jnp.bfloat16)
    return high, middle, low


def dot(a, b, dims):
    return lax.dot_general(a, b, (dims, ((), ())), preferred_element_type=jnp.float32)


def dot_split(a, b, dims):
    (ah, al), (bh, bl) = a, b
    return dot(ah, bh, dims) + (dot(ah, bl, dims) + dot(al, bh, dims))


def grad_kernel(*refs):
    n = (len(refs) - 1) // 2
    acts, grads, out = refs[:n], refs[n : 2 * n], refs[-1]
    slots, _, ff = acts[0].shape
    for s in range(slots):
        a = jnp.concatenate([r[s] for r in acts], axis=0)
        g = jnp.concatenate([r[s] for r in grads], axis=0)
        out[pl.ds(s, ff, stride=slots), :] = dot_split(halves(a), halves(g), ((0,), (0,)))


def adamw_kernel(arrived, old_table, new_table, master, moment_one, moment_two,
                 new_master, new_one, new_two, send):
    rows, experts, _ = master.shape
    slots, owners = old_table.shape
    step = rows * slots
    ids = lax.broadcasted_iota(jnp.int32, (experts, owners), 0)

    def onehot(table):
        return jnp.concatenate(
            [(ids == table[p : p + 1, :]).astype(jnp.float32).astype(jnp.bfloat16) for p in range(slots)], axis=1
        )

    got = jnp.concatenate(
        [
            jnp.concatenate([arrived[pl.ds(f * slots + p, owners, stride=step), :] for f in range(rows)], axis=1)
            for p in range(slots)
        ],
        axis=0,
    )
    old = onehot(old_table)
    grad = sum(dot(old, part, ((1,), (0,))) for part in reversed(thirds(got)))
    updated = []
    for f in range(rows):
        g = grad[:, f * LANES : (f + 1) * LANES]
        first = beta_one * moment_one[f] + (1.0 - beta_one) * g
        second = beta_two * moment_two[f] + (1.0 - beta_two) * g * g
        new_one[f] = first
        new_two[f] = second
        first_hat = first / (1.0 - beta_one**STEP)
        second_hat = second / (1.0 - beta_two**STEP)
        m = master[f]
        m = m - learn_rate * (first_hat / (jnp.sqrt(second_hat) + epsilon) + decay_rate * m)
        new_master[f] = m
        updated.append(m)
    new = onehot(new_table)
    parts = thirds(jnp.concatenate(updated, axis=1))
    picked = sum(dot(new, part, ((0,), (0,))) for part in reversed(parts))
    for f in range(rows):
        for p in range(slots):
            send[pl.ds(f * slots + p, owners, stride=step), :] = picked[
                p * owners : (p + 1) * owners, f * LANES : (f + 1) * LANES
            ]


def product_kernel(place, counts, acts, grads, *refs):
    weights, outputs, input_grads = refs[:-2], refs[-2], refs[-1]
    n = len(weights)
    slots, rows, ff = acts.shape
    for s in range(slots):
        live = lax.broadcasted_iota(jnp.int32, (rows, 1), 0) < counts[s]
        a = halves(jnp.where(live, acts[s], 0.0))
        total = jnp.zeros((rows, ff), jnp.float32)
        for k in range(n):
            block = lax.rem(place[0] + n - k, n)
            columns = pl.ds(pl.multiple_of(block * LANES, LANES), LANES)
            w = halves(weights[k][s])
            outputs[s, :, columns] = dot_split(a, w, ((1,), (0,)))
            g = halves(jnp.where(live, grads[s, :, columns], 0.0))
            total += dot_split(g, w, ((1,), (1,)))
        input_grads[s] = total


VMEM = pl.BlockSpec(memory_space=pltpu.VMEM)
SMEM = pl.BlockSpec(memory_space=pltpu.SMEM)
LIMIT = 40 * 1024 * 1024


def local(
    activations,
    out_grads,
    counts,
    slot_weights,
    master,
    moment_one,
    moment_two,
    old_table,
    new_table,
):
    f32 = jnp.float32
    n = lax.axis_size("dp")
    owners = lax.axis_size("ep")
    me = lax.axis_index("dp")
    slots, tokens, ff = activations.shape
    experts, rows, lanes = master.shape

    def shifted(x, k):
        return lax.ppermute(x, "dp", [(i, (i + k) % n) for i in range(n)])

    shifts = [2, 1, 3]
    acts = {k: shifted(activations, k) for k in shifts}
    positions = jnp.arange(tokens, dtype=jnp.int32)
    live = (positions[None, :] < counts).astype(f32)

    def columns(k):
        block = lax.dynamic_slice_in_dim(out_grads, lax.rem(me + k, n) * lanes, lanes, axis=2)
        return block * live[:, :, None]

    grads = {k: shifted(columns(k), k) for k in shifts}
    column_grad = pl.pallas_call(
        grad_kernel,
        out_shape=jax.ShapeDtypeStruct((slots * ff, lanes), f32),
        in_specs=[VMEM] * (2 * n),
        out_specs=VMEM,
        compiler_params=pltpu.CompilerParams(vmem_limit_bytes=LIMIT),
        name="slot_grads",
    )(activations, *[acts[k] for k in shifts], columns(0), *[grads[k] for k in shifts])
    held, column_grad = lax.optimization_barrier((slot_weights, column_grad))
    near = {k: shifted(held, k) for k in shifts[1:]}
    arrived = lax.all_to_all(
        column_grad.reshape(owners, 1, slots * rows * lanes), "ep", split_axis=0, concat_axis=0, tiled=True
    )
    arrived, near, held = lax.optimization_barrier((arrived, near, held))
    weights = {shifts[0]: shifted(held, shifts[0]), **near}

    plane = jax.ShapeDtypeStruct((rows, experts, lanes), f32)
    flip = lambda x: jnp.transpose(x, (1, 0, 2))
    new_master, new_one, new_two, send = pl.pallas_call(
        adamw_kernel,
        out_shape=(plane, plane, plane, jax.ShapeDtypeStruct((slots * rows * owners, lanes), f32)),
        in_specs=[VMEM] * 6,
        out_specs=(VMEM,) * 4,
        compiler_params=pltpu.CompilerParams(vmem_limit_bytes=LIMIT),
        name="adamw",
    )(
        arrived.reshape(slots * rows * owners, lanes),
        old_table.reshape(owners, slots).T,
        new_table.reshape(owners, slots).T,
        flip(master),
        flip(moment_one),
        flip(moment_two),
    )
    placed = lax.all_to_all(
        send.reshape(owners, 1, slots * rows * lanes), "ep", split_axis=0, concat_axis=0, tiled=True
    )
    outputs, input_grads = pl.pallas_call(
        product_kernel,
        out_shape=(
            jax.ShapeDtypeStruct(out_grads.shape, f32),
            jax.ShapeDtypeStruct(activations.shape, f32),
        ),
        in_specs=[SMEM, SMEM] + [VMEM] * (2 + n),
        out_specs=(VMEM, VMEM),
        compiler_params=pltpu.CompilerParams(vmem_limit_bytes=LIMIT),
        cost_estimate=pl.CostEstimate(flops=12 * slots * tokens * ff * n * lanes, bytes_accessed=8 << 20, transcendentals=0),
        name="products",
    )(
        me.astype(jnp.int32).reshape(1),
        counts[:, 0],
        activations,
        out_grads,
        slot_weights,
        *[weights[k] for k in range(1, n)],
    )
    new_slots = jnp.transpose(placed.reshape(ff, slots, lanes), (1, 0, 2))
    return (outputs, input_grads, flip(new_master), flip(new_one), flip(new_two), new_slots)


def solution(mesh):
    in_specs = (
        P("ep", "dp", None),
        P("ep", "dp", None),
        P("ep", "dp"),
        P("ep", None, "dp"),
        P(None, "ep", "dp"),
        P(None, "ep", "dp"),
        P(None, "ep", "dp"),
        P(),
        P(),
    )
    out_specs = (
        P("ep", "dp", None),
        P("ep", "dp", None),
        P(None, "ep", "dp"),
        P(None, "ep", "dp"),
        P(None, "ep", "dp"),
        P("ep", None, "dp"),
    )
    return jax.shard_map(local, mesh=mesh, in_specs=in_specs, out_specs=out_specs, check_vma=False)
```

time: 142 us -> 125 us (0.88)
  starting transfers between devices: 6.91 us -> 69.2 us
  blocking collectives: 49.4 us -> 0 us
  matrix products: 14.8 us -> 0 us
  between operations: 14.2 us -> 0.79 us
  waiting for transfers between devices: 45.4 us -> 34.2 us
  Pallas kernels: 0 us -> 7.37 us
  local copies, waits for them, and re-layouts: 5.63 us -> 8.94 us
  other arithmetic: 4.96 us -> 3.09 us
    all_to_all x2 -> x0, blocking collectives: 49.4 us -> none  [the longest x1 39.2 us: local(): lax.all_to_all(column_grad, 'ep', split_axis=1, concat_axis=0, tiled=True)]
    ppermute x0 -> x9, starting transfers between devices: none -> 34.7 us  [shifted(): return lax.ppermute(x, 'dp', [(i, (i + k) % n) for i in range(n)])]
    ppermute x0 -> x9, waiting for transfers between devices: none -> 32 us  [shifted(): return lax.ppermute(x, 'dp', [(i, (i + k) % n) for i in range(n)])]
    all_to_all x1 -> x2, starting transfers between devices: 6.83 us -> 34.4 us  [the longest x1 20.9 us: local(): lax.all_to_all(column_grad.reshape(owners, 1, slots * rows * lanes), 'ep'...]
    all_gather x2 -> x0, waiting for transfers between devices: 23 us -> none  [the longest x1 23 us: local(): every_act = lax.all_gather(masked_acts, 'dp', axis=1, tiled=True)]
    all_to_all x1 -> x2, waiting for transfers between devices: 21.7 us -> 2.18 us  [the longest x1 2.18 us: local(): lax.all_to_all(column_grad.reshape(owners, 1, slots * rows * lanes), 'ep'...]
    dot_general x5 -> x0, matrix products: 14.8 us -> none  [the longest x1 4.76 us: local(): jnp.einsum('srf,sfd->srd', masked_acts, whole_weights, precision=precise)]
    pallas_call x0 -> x3, Pallas kernels: none -> 7.37 us  [the longest x1 3.61 us: local(): pl.pallas_call(product_kernel, out_shape=(jax.ShapeDtypeStruct(out_grads....]
  transfers between devices with their start and end apart: 3 -> 11, of which waited for: 2 -> 6; matrix products, arithmetic and copies ran while one was open for 15% -> 6% of each run, Pallas kernels for 0% -> 3%
where the time goes in v1:
time: 125 us; the launch traced here: 124 us
  starting transfers between devices  69.2 us (55%)
  waiting for transfers between devices  34.2 us (27%)
  local copies, waits for them, and re-layouts  8.94 us (7%)
  Pallas kernels  7.37 us (6%)
  other arithmetic  3.09 us (2%)
    ppermute x9, starting transfers between devices, shifted(): return lax.ppermute(x, 'dp', [(i, (i + k) % n) for i in range(n)])  34.7 us
    ppermute x9, waiting for transfers between devices, shifted(): return lax.ppermute(x, 'dp', [(i, (i + k) % n) for i in range(n)])  32 us
    all_to_all x1, starting transfers between devices, local(): lax.all_to_all(column_grad.reshape(owners, 1, slots * rows * lanes), 'ep'...  20.9 us
    all_to_all x1, starting transfers between devices, local(): lax.all_to_all(send.reshape(owners, 1, slots * rows * lanes), 'ep', split...  13.5 us
    unnamed x20, local copies, waits for them, and re-layouts  5.59 us
    pallas_call x1, Pallas kernels, local(): pl.pallas_call(product_kernel, out_shape=(jax.ShapeDtypeStruct(out_grads....  3.61 us
  transfers between devices with their start and end apart: 11, of which 6 were waited for; matrix products, arithmetic and copies ran while one was open for 6% of the time, Pallas kernels for 3%

profile of v1, /device:TPU:1, one launch (start us, length us, event | category | flops | bytes accessed | tf_op | source)
XLA Modules:
  0.0 123.6 jit_solution(12562891249399569086)
XLA Ops:
  0.6 0.0 copy-start
  0.6 5.6 %collective-permute-start = (f32[2,64,768]{2,1,0:T(8,128)}, f32[2,64,768]{2,1,0:T(8,128)S(1)}, u32[]{:S(2)}, u32[]{:S(2)}) collective-permute-start(f32[2,64,768]{2,1,0:T(8,128)} %acts.1), channel_id=1, source_target_pairs={{0,2},{1,3},{2,0},{3,1},{4,6},{5,7},{6,4},{7,5},{8,10},{9,11},{10,... | collective-permute-start | bytes 1179656 | tf_op jit(solution)/shard_map/ppermute | solution.py:139
  6.3 2.2 %collective-permute-start.1 = (f32[2,64,768]{2,1,0:T(8,128)}, f32[2,64,768]{2,1,0:T(8,128)S(1)}, u32[]{:S(2)}, u32[]{:S(2)}) collective-permute-start(f32[2,64,768]{2,1,0:T(8,128)} %acts.1), channel_id=1, source_target_pairs={{0,1},{1,2},{2,3},{3,0},{4,5},{5,6},{6,7},{7,4},{8,9},{9,10},{10,1... | collective-permute-start | bytes 1179656 | tf_op jit(solution)/shard_map/ppermute | solution.py:139
  8.5 4.3 %collective-permute-start.2 = (f32[2,64,768]{2,1,0:T(8,128)}, f32[2,64,768]{2,1,0:T(8,128)S(1)}, u32[]{:S(2)}, u32[]{:S(2)}) collective-permute-start(f32[2,64,768]{2,1,0:T(8,128)} %acts.1), channel_id=1, source_target_pairs={{0,3},{1,0},{2,1},{3,2},{4,7},{5,4},{6,5},{7,6},{8,11},{9,8},{10,9... | collective-permute-start | bytes 1179656 | tf_op jit(solution)/shard_map/ppermute | solution.py:139
  12.8 0.7 compare_convert_fusion
  13.5 1.0 dynamic-slice_multiply_fusion
  14.5 1.9 %collective-permute-start.3 = (f32[2,64,128]{2,1,0:T(8,128)S(1)}, f32[2,64,128]{2,1,0:T(8,128)S(1)}, u32[]{:S(2)}, u32[]{:S(2)}) collective-permute-start(f32[2,64,128]{2,1,0:T(8,128)S(1)} %get-tuple-element.44), channel_id=1, source_target_pairs={{0,2},{1,3},{2,0},{3,1},{4,6},{5,7},{6,4},{7,5},{8,10},{9,11},{10,... | collective-permute-start | bytes 196616 | tf_op jit(solution)/shard_map/ppermute | solution.py:139
  16.5 2.5 %collective-permute-start.4 = (f32[2,64,128]{2,1,0:T(8,128)S(1)}, f32[2,64,128]{2,1,0:T(8,128)S(1)}, u32[]{:S(2)}, u32[]{:S(2)}) collective-permute-start(f32[2,64,128]{2,1,0:T(8,128)S(1)} %get-tuple-element.43), channel_id=1, source_target_pairs={{0,1},{1,2},{2,3},{3,0},{4,5},{5,6},{6,7},{7,4},{8,9},{9,10},{10,1... | collective-permute-start | bytes 196616 | tf_op jit(solution)/shard_map/ppermute | solution.py:139
  18.9 2.9 %collective-permute-done.3.refs_5_ = f32[2,64,128]{2,1,0:T(8,128)S(1)} collective-permute-done((f32[2,64,128]{2,1,0:T(8,128)S(1)}, f32[2,64,128]{2,1,0:T(8,128)S(1)}, u32[]{:S(2)}, u32[]{:S(2)}) %collective-permute-start.3) | collective-permute-done | bytes 65568 | tf_op jit(solution)/shard_map/ppermute | solution.py:139
  21.8 6.6 %collective-permute-start.5 = (f32[2,64,128]{2,1,0:T(8,128)S(1)}, f32[2,64,128]{2,1,0:T(8,128)S(1)}, u32[]{:S(2)}, u32[]{:S(2)}) collective-permute-start(f32[2,64,128]{2,1,0:T(8,128)S(1)} %get-tuple-element.42), channel_id=1, source_target_pairs={{0,3},{1,0},{2,1},{3,2},{4,7},{5,4},{6,5},{7,6},{8,11},{9,8},{10,9... | collective-permute-start | bytes 196616 | tf_op jit(solution)/shard_map/ppermute | solution.py:139
  28.4 0.0 collective-permute-done.4.refs_6_
  28.4 1.3 %collective-permute-done.5.refs_7_ = f32[2,64,128]{2,1,0:T(8,128)S(1)} collective-permute-done((f32[2,64,128]{2,1,0:T(8,128)S(1)}, f32[2,64,128]{2,1,0:T(8,128)S(1)}, u32[]{:S(2)}, u32[]{:S(2)}) %collective-permute-start.5) | collective-permute-done | bytes 65568 | tf_op jit(solution)/shard_map/ppermute | solution.py:139
  29.7 0.0 collective-permute-done.refs_1_
  29.7 0.0 collective-permute-done.1.refs_2_
  29.7 0.0 collective-permute-done.2.refs_3_
  29.7 0.0 copy-done
  29.7 1.7 %slot_grads.1 = f32[1536,128]{1,0:T(8,128)} custom-call(f32[2,64,768]{2,1,0:T(8,128)S(1)} %copy-done, f32[2,64,768]{2,1,0:T(8,128)S(1)} %collective-permute-done.refs_1_, f32[2,64,768]{2,1,0:T(8,128)S(1)} %collective-permute-done.1.refs_2_, f32[2,64,768]{2,1,0:T(8,128)S(1)} %collective-permute-done.2.refs_3_, f32[2,64,128]{2,1,0:T(8,128)S(1)} %get-tuple-element.45.refs_4_, ...), custom_call_target="tpu_custom_call" | custom-call | tf_op jit(solution)/shard_map/slot_grads/pallas_call | solution.py:151
  31.4 20.9 %all-to-all-start = ((f32[128,1,1536]{2,1,0:T(1,128)}), f32[128,1,1536]{2,1,0:T(1,128)S(1)}, u32[]{:S(2)}, u32[]{:S(2)}) async-start(f32[128,1,1536]{2,1,0:T(1,128)} %bitcast.2), calls=%async_computation | async-start | bytes 1572864 | tf_op jit(solution)/shard_map/all_to_all | solution.py:161
  52.4 0.0 copy-done.2
  52.4 0.0 copy-start.7
  52.4 2.6 %collective-permute-start.6 = (f32[2,768,128]{2,1,0:T(8,128)S(1)}, f32[2,768,128]{2,1,0:T(8,128)S(1)}, u32[]{:S(2)}, u32[]{:S(2)}) collective-permute-start(f32[2,768,128]{2,1,0:T(8,128)S(1)} %copy-done.2), channel_id=1, source_target_pairs={{0,1},{1,2},{2,3},{3,0},{4,5},{5,6},{6,7},{7,4},{8,9},{9,10},{10,1... | collective-permute-start | bytes 2359304 | tf_op jit(solution)/shard_map/ppermute | solution.py:139
  55.0 4.1 %collective-permute-start.7 = (f32[2,768,128]{2,1,0:T(8,128)S(1)}, f32[2,768,128]{2,1,0:T(8,128)S(1)}, u32[]{:S(2)}, u32[]{:S(2)}) collective-permute-start(f32[2,768,128]{2,1,0:T(8,128)S(1)} %copy-done.2), channel_id=1, source_target_pairs={{0,3},{1,0},{2,1},{3,2},{4,7},{5,4},{6,5},{7,6},{8,11},{9,8},{10,9... | collective-permute-start | bytes 2359304 | tf_op jit(solution)/shard_map/ppermute | solution.py:139
  59.1 0.5 broadcast.24
  59.6 0.0 copy-done.7
  59.6 0.7 reduce.6
  60.2 0.8 reshape.59
  61.0 0.0 copy-start.8
  61.0 0.9 copy.19
  61.9 0.0 copy-done.8
  61.9 0.7 reduce.7
  62.6 0.8 reshape.60
  63.4 0.9 copy.20
  64.3 9.7 %collective-permute-done.6.refs_1_ = f32[2,768,128]{2,1,0:T(8,128)S(1)} collective-permute-done((f32[2,768,128]{2,1,0:T(8,128)S(1)}, f32[2,768,128]{2,1,0:T(8,128)S(1)}, u32[]{:S(2)}, u32[]{:S(2)}) %collective-permute-start.6) | collective-permute-done | bytes 786464 | tf_op jit(solution)/shard_map/ppermute | solution.py:139
  74.0 1.3 %collective-permute-done.7.refs_3_ = f32[2,768,128]{2,1,0:T(8,128)S(1)} collective-permute-done((f32[2,768,128]{2,1,0:T(8,128)S(1)}, f32[2,768,128]{2,1,0:T(8,128)S(1)}, u32[]{:S(2)}, u32[]{:S(2)}) %collective-permute-start.7) | collective-permute-done | bytes 786464 | tf_op jit(solution)/shard_map/ppermute | solution.py:139
  75.3 2.2 %all-to-all-done = f32[128,1,1536]{2,1,0:T(1,128)S(1)} async-done(((f32[128,1,1536]{2,1,0:T(1,128)}), f32[128,1,1536]{2,1,0:T(1,128)S(1)}, u32[]{:S(2)}, u32[]{:S(2)}) %all-to-all-start) | async-done | bytes 786464 | tf_op jit(solution)/shard_map/all_to_all | solution.py:161
  77.5 1.0 copy-done.3
  78.5 1.0 copy-done.4
  79.5 1.0 copy-done.5
  80.5 2.1 %adamw.1 = (f32[6,128,128]{2,1,0:T(8,128)}, f32[6,128,128]{2,1,0:T(8,128)}, f32[6,128,128]{2,1,0:T(8,128)}, f32[1536,128]{1,0:T(8,128)}) custom-call(f32[1536,128]{1,0:T(8,128)S(1)} %bitcast.18, s32[2,128]{1,0:T(2,128)S(1)} %bitcast.22, s32[2,128]{1,0:T(2,128)S(1)} %bitcast.23, f32[6,128,128]{2,1,0:T(8,128)S(1)} %bitcast.19, f32[6,128,128]{2,1,0:T(8,128)S(1)} %bitcast.20, ...), custom_call_target="tpu_custom_call" | custom-call | tf_op jit(solution)/shard_map/adamw/pallas_call | solution.py:169
  82.5 13.5 %all-to-all-start.1 = ((f32[128,1,1536]{2,1,0:T(1,128)}), f32[128,1,1536]{2,1,0:T(1,128)}, u32[]{:S(2)}, u32[]{:S(2)}) async-start(f32[128,1,1536]{2,1,0:T(1,128)} %bitcast.12), calls=%async_computation.1 | async-start | bytes 1572864 | tf_op jit(solution)/shard_map/all_to_all | solution.py:184
  96.1 0.0 copy-start.6
  96.1 5.0 %collective-permute-start.8 = (f32[2,768,128]{2,1,0:T(8,128)S(1)}, f32[2,768,128]{2,1,0:T(8,128)S(1)}, u32[]{:S(2)}, u32[]{:S(2)}) collective-permute-start(f32[2,768,128]{2,1,0:T(8,128)S(1)} %copy-done.2), channel_id=1, source_target_pairs={{0,2},{1,3},{2,0},{3,1},{4,6},{5,7},{6,4},{7,5},{8,10},{9,11},{10,... | collective-permute-start | bytes 2359304 | tf_op jit(solution)/shard_map/ppermute | solution.py:139
  101.1 16.8 %collective-permute-done.8.refs_2_ = f32[2,768,128]{2,1,0:T(8,128)S(1)} collective-permute-done((f32[2,768,128]{2,1,0:T(8,128)S(1)}, f32[2,768,128]{2,1,0:T(8,128)S(1)}, u32[]{:S(2)}, u32[]{:S(2)}) %collective-permute-start.8) | collective-permute-done | bytes 786464 | tf_op jit(solution)/shard_map/ppermute | solution.py:139
  117.9 0.0 copy-done.1
  117.9 0.0 copy-done.6
  117.9 3.6 %products.1 = (f32[2,64,512]{2,1,0:T(8,128)}, f32[2,64,768]{2,1,0:T(8,128)}) custom-call(s32[1]{0:T(128)} %bitcast.place, s32[2]{0:T(128)S(1)} %bitcast.25, f32[2,64,768]{2,1,0:T(8,128)S(1)} %copy-done, f32[2,64,512]{2,1,0:T(8,128)S(1)} %copy-done.1, f32[2,768,128]{2,1,0:T(8,128)S(1)} %copy-done.2, f32[2,768,128]{2,1,0:T(8,128)S(1)} %collective-permute-done.6.refs_1_, ...), custom_call_target="tpu_custom_call" | custom-call | flops 603979776 | bytes 8388608 | tf_op jit(solution)/shard_map/products/pallas_call | solution.py:187
  121.5 0.0 all-to-all-done.1
  121.5 2.1 %copy.22 = f32[2,768,128]{2,1,0:T(8,128)} copy(f32[2,768,128]{2,0,1:T(2,128)} %bitcast.14) | data formatting | bytes 1572864
  (5 shorter events, 0.0 us)
Async XLA Ops:
  0.6 29.1 %copy-start = (f32[2,64,768]{2,1,0:T(8,128)S(1)}, f32[2,64,768]{2,1,0:T(8,128)}, u32[]{:S(2)}) copy-start(f32[2,64,768]{2,1,0:T(8,128)} %acts.1) | copy-start | bytes 1179652
  0.6 29.1 %collective-permute-start = (f32[2,64,768]{2,1,0:T(8,128)}, f32[2,64,768]{2,1,0:T(8,128)S(1)}, u32[]{:S(2)}, u32[]{:S(2)}) collective-permute-start(f32[2,64,768]{2,1,0:T(8,128)} %acts.1), channel_id=1, source_target_pairs={{0,2},{1,3},{2,0},{3,1},{4,6},{5,7},{6,4},{7,5},{8,10},{9,11},{10,... | collective-permute-start | bytes 1179656 | tf_op jit(solution)/shard_map/ppermute | solution.py:139
  6.3 23.5 %collective-permute-start.1 = (f32[2,64,768]{2,1,0:T(8,128)}, f32[2,64,768]{2,1,0:T(8,128)S(1)}, u32[]{:S(2)}, u32[]{:S(2)}) collective-permute-start(f32[2,64,768]{2,1,0:T(8,128)} %acts.1), channel_id=1, source_target_pairs={{0,1},{1,2},{2,3},{3,0},{4,5},{5,6},{6,7},{7,4},{8,9},{9,10},{10,1... | collective-permute-start | bytes 1179656 | tf_op jit(solution)/shard_map/ppermute | solution.py:139
  8.5 21.2 %collective-permute-start.2 = (f32[2,64,768]{2,1,0:T(8,128)}, f32[2,64,768]{2,1,0:T(8,128)S(1)}, u32[]{:S(2)}, u32[]{:S(2)}) collective-permute-start(f32[2,64,768]{2,1,0:T(8,128)} %acts.1), channel_id=1, source_target_pairs={{0,3},{1,0},{2,1},{3,2},{4,7},{5,4},{6,5},{7,6},{8,11},{9,8},{10,9... | collective-permute-start | bytes 1179656 | tf_op jit(solution)/shard_map/ppermute | solution.py:139
  14.5 7.3 %collective-permute-start.3 = (f32[2,64,128]{2,1,0:T(8,128)S(1)}, f32[2,64,128]{2,1,0:T(8,128)S(1)}, u32[]{:S(2)}, u32[]{:S(2)}) collective-permute-start(f32[2,64,128]{2,1,0:T(8,128)S(1)} %get-tuple-element.44), channel_id=1, source_target_pairs={{0,2},{1,3},{2,0},{3,1},{4,6},{5,7},{6,4},{7,5},{8,10},{9,11},{10,... | collective-permute-start | bytes 196616 | tf_op jit(solution)/shard_map/ppermute | solution.py:139
  16.5 12.0 %collective-permute-start.4 = (f32[2,64,128]{2,1,0:T(8,128)S(1)}, f32[2,64,128]{2,1,0:T(8,128)S(1)}, u32[]{:S(2)}, u32[]{:S(2)}) collective-permute-start(f32[2,64,128]{2,1,0:T(8,128)S(1)} %get-tuple-element.43), channel_id=1, source_target_pairs={{0,1},{1,2},{2,3},{3,0},{4,5},{5,6},{6,7},{7,4},{8,9},{9,10},{10,1... | collective-permute-start | bytes 196616 | tf_op jit(solution)/shard_map/ppermute | solution.py:139
  21.8 7.9 %collective-permute-start.5 = (f32[2,64,128]{2,1,0:T(8,128)S(1)}, f32[2,64,128]{2,1,0:T(8,128)S(1)}, u32[]{:S(2)}, u32[]{:S(2)}) collective-permute-start(f32[2,64,128]{2,1,0:T(8,128)S(1)} %get-tuple-element.42), channel_id=1, source_target_pairs={{0,3},{1,0},{2,1},{3,2},{4,7},{5,4},{6,5},{7,6},{8,11},{9,8},{10,9... | collective-permute-start | bytes 196616 | tf_op jit(solution)/shard_map/ppermute | solution.py:139
  31.4 20.9 %copy-start.2 = (f32[2,768,128]{2,1,0:T(8,128)S(1)}, f32[2,768,128]{2,1,0:T(8,128)}, u32[]{:S(2)}) copy-start(f32[2,768,128]{2,1,0:T(8,128)} %refs_0_.3) | copy-start | bytes 2359300
  31.4 46.1 %all-to-all-start = ((f32[128,1,1536]{2,1,0:T(1,128)}), f32[128,1,1536]{2,1,0:T(1,128)S(1)}, u32[]{:S(2)}, u32[]{:S(2)}) async-start(f32[128,1,1536]{2,1,0:T(1,128)} %bitcast.2), calls=%async_computation | async-start | bytes 1572864 | tf_op jit(solution)/shard_map/all_to_all | solution.py:161
  52.4 7.2 %copy-start.7 = (s32[256,1]{0,1:T(1,128)S(1)}, s32[256,1]{0,1:T(1,128)}, u32[]{:S(2)}) copy-start(s32[256,1]{0,1:T(1,128)} %param.16) | copy-start | bytes 3076
  52.4 21.6 %collective-permute-start.6 = (f32[2,768,128]{2,1,0:T(8,128)S(1)}, f32[2,768,128]{2,1,0:T(8,128)S(1)}, u32[]{:S(2)}, u32[]{:S(2)}) collective-permute-start(f32[2,768,128]{2,1,0:T(8,128)S(1)} %copy-done.2), channel_id=1, source_target_pairs={{0,1},{1,2},{2,3},{3,0},{4,5},{5,6},{6,7},{7,4},{8,9},{9,10},{10,1... | collective-permute-start | bytes 2359304 | tf_op jit(solution)/shard_map/ppermute | solution.py:139
  55.0 20.3 %collective-permute-start.7 = (f32[2,768,128]{2,1,0:T(8,128)S(1)}, f32[2,768,128]{2,1,0:T(8,128)S(1)}, u32[]{:S(2)}, u32[]{:S(2)}) collective-permute-start(f32[2,768,128]{2,1,0:T(8,128)S(1)} %copy-done.2), channel_id=1, source_target_pairs={{0,3},{1,0},{2,1},{3,2},{4,7},{5,4},{6,5},{7,6},{8,11},{9,8},{10,9... | collective-permute-start | bytes 2359304 | tf_op jit(solution)/shard_map/ppermute | solution.py:139
  61.0 0.9 copy-start.8
  77.5 1.0 copy-start.3
  78.5 1.0 copy-start.4
  79.5 1.0 copy-start.5
  82.5 35.3 %copy-start.1 = (f32[2,64,512]{2,1,0:T(8,128)S(1)}, f32[2,64,512]{2,1,0:T(8,128)}, u32[]{:S(2)}) copy-start(f32[2,64,512]{2,1,0:T(8,128)} %grads.1) | copy-start | bytes 786436
  82.5 39.0 %all-to-all-start.1 = ((f32[128,1,1536]{2,1,0:T(1,128)}), f32[128,1,1536]{2,1,0:T(1,128)}, u32[]{:S(2)}, u32[]{:S(2)}) async-start(f32[128,1,1536]{2,1,0:T(1,128)} %bitcast.12), calls=%async_computation.1 | async-start | bytes 1572864 | tf_op jit(solution)/shard_map/all_to_all | solution.py:184
  96.1 21.8 %copy-start.6 = (s32[2,1]{0,1:T(1,128)S(1)}, s32[2,1]{0,1:T(1,128)}, u32[]{:S(2)}) copy-start(s32[2,1]{0,1:T(1,128)} %param.11) | copy-start | bytes 28
  96.1 21.8 %collective-permute-start.8 = (f32[2,768,128]{2,1,0:T(8,128)S(1)}, f32[2,768,128]{2,1,0:T(8,128)S(1)}, u32[]{:S(2)}, u32[]{:S(2)}) collective-permute-start(f32[2,768,128]{2,1,0:T(8,128)S(1)} %copy-done.2), channel_id=1, source_target_pairs={{0,2},{1,3},{2,0},{3,1},{4,6},{5,7},{6,4},{7,5},{8,10},{9,11},{10,... | collective-permute-start | bytes 2359304 | tf_op jit(solution)/shard_map/ppermute | solution.py:139

commit v2 on v1

v2 whole, which is shorter than its diff:
```python
import jax
import jax.numpy as jnp
from jax import lax
from jax.experimental import pallas as pl
from jax.experimental.pallas import tpu as pltpu
from jax.sharding import PartitionSpec as P

STEP = 100


beta_one = 0.9
beta_two = 0.999
learn_rate = 0.02
epsilon = 1e-08
decay_rate = 0.1

LANES = 128


def halves(x):
    high = x.astype(jnp.bfloat16)
    low = (x - high.astype(jnp.float32)).astype(jnp.bfloat16)
    return high, low


def thirds(x):
    high = x.astype(jnp.bfloat16)
    rest = x - high.astype(jnp.float32)
    middle = rest.astype(jnp.bfloat16)
    low = (rest - middle.astype(jnp.float32)).astype(jnp.bfloat16)
    return high, middle, low


def dot(a, b, dims):
    return lax.dot_general(a, b, (dims, ((), ())), preferred_element_type=jnp.float32)


def dot_split(a, b, dims):
    (ah, al), (bh, bl) = a, b
    return dot(ah, bh, dims) + (dot(ah, bl, dims) + dot(al, bh, dims))


def pack_kernel(place, counts, acts, grads, *outs):
    n = len(outs)
    slots, rows, ff = acts.shape
    for s in range(slots):
        live = lax.broadcasted_iota(jnp.int32, (rows, 1), 0) < counts[s]
        for k in range(n):
            block = lax.rem(place[0] + k, n)
            columns = pl.ds(pl.multiple_of(block * LANES, LANES), LANES)
            g = jnp.where(live, grads[s, :, columns], 0.0)
            if k:
                outs[k][s, :, :ff] = acts[s]
                outs[k][s, :, ff:] = g
            else:
                outs[k][s] = g


def stacked(acts, grads, others, s):
    ff = acts.shape[2]
    a = jnp.concatenate([acts[s]] + [r[s, :, :ff] for r in others], axis=0)
    g = jnp.concatenate([grads[s]] + [r[s, :, ff:] for r in others], axis=0)
    return halves(a), halves(g)


def grad_kernel(acts, grads, *refs):
    others, out = refs[:-1], refs[-1]
    slots, _, ff = acts.shape
    for s in range(slots):
        a, g = stacked(acts, grads, others, s)
        out[pl.ds(s, ff, stride=slots), :] = dot_split(a, g, ((0,), (0,)))


def product_kernel(after, weights, acts, grads, *refs):
    n = len(refs) // 2 + 1
    others, outs = refs[: n - 1], refs[n - 1 :]
    slots, rows, ff = acts.shape
    for s in range(slots):
        a, g = stacked(acts, grads, others, s)
        w = halves(weights[s])
        columns = dot_split(a, w, ((1,), (0,)))
        part = dot_split(g, w, ((1,), (1,)))
        for k in range(n):
            outs[k][s, :, :ff] = part[k * rows : (k + 1) * rows]
            outs[k][s, :, ff:] = columns[k * rows : (k + 1) * rows]


def combine_kernel(place, counts, *refs):
    n = len(refs) - 2
    parts, outputs, input_grads = refs[:n], refs[-2], refs[-1]
    slots, rows, ff = input_grads.shape
    for s in range(slots):
        live = lax.broadcasted_iota(jnp.int32, (rows, 1), 0) < counts[s]
        total = parts[0][s, :, :ff]
        for k in range(1, n):
            total += parts[k][s, :, :ff]
        input_grads[s] = total
        for k in range(n):
            block = lax.rem(place[0] + k, n)
            columns = pl.ds(pl.multiple_of(block * LANES, LANES), LANES)
            outputs[s, :, columns] = jnp.where(live, parts[k][s, :, ff:], 0.0)


def place_kernel(rows, out):
    slots, ff, _ = out.shape
    for s in range(slots):
        out[s] = rows[pl.ds(s, ff, stride=slots), :]


def adamw_kernel(after, arrived, old_table, new_table, master_in, one_in, two_in,
                 new_master, new_one, new_two, send, master, moment_one, moment_two, arrivals):
    copies = [
        pltpu.make_async_copy(there, here, arrivals.at[i])
        for i, (there, here) in enumerate([(master_in, master), (one_in, moment_one), (two_in, moment_two)])
    ]
    for copy in copies:
        copy.start()
    rows, experts, _ = master.shape
    slots, owners = old_table.shape
    step = rows * slots
    ids = lax.broadcasted_iota(jnp.int32, (experts, owners), 0)

    def onehot(table):
        return jnp.concatenate(
            [(ids == table[p : p + 1, :]).astype(jnp.float32).astype(jnp.bfloat16) for p in range(slots)], axis=1
        )

    got = jnp.concatenate(
        [
            jnp.concatenate([arrived[pl.ds(f * slots + p, owners, stride=step), :] for f in range(rows)], axis=1)
            for p in range(slots)
        ],
        axis=0,
    )
    old = onehot(old_table)
    grad = sum(dot(old, part, ((1,), (0,))) for part in reversed(thirds(got)))
    for copy in copies:
        copy.wait()
    updated = []
    for f in range(rows):
        g = grad[:, f * LANES : (f + 1) * LANES]
        first = beta_one * moment_one[f] + (1.0 - beta_one) * g
        second = beta_two * moment_two[f] + (1.0 - beta_two) * g * g
        new_one[f] = first
        new_two[f] = second
        first_hat = first / (1.0 - beta_one**STEP)
        second_hat = second / (1.0 - beta_two**STEP)
        m = master[f]
        m = m - learn_rate * (first_hat / (jnp.sqrt(second_hat) + epsilon) + decay_rate * m)
        new_master[f] = m
        updated.append(m)
    new = onehot(new_table)
    parts = thirds(jnp.concatenate(updated, axis=1))
    picked = sum(dot(new, part, ((0,), (0,))) for part in reversed(parts))
    for f in range(rows):
        for p in range(slots):
            send[pl.ds(f * slots + p, owners, stride=step), :] = picked[
                p * owners : (p + 1) * owners, f * LANES : (f + 1) * LANES
            ]


VMEM = pl.BlockSpec(memory_space=pltpu.VMEM)
SMEM = pl.BlockSpec(memory_space=pltpu.SMEM)
ANY = pl.BlockSpec(memory_space=pl.ANY)
SOME = 24 * 1024 * 1024
MOST = 60 * 1024 * 1024


def kernel(body, out_shape, in_specs, name, scratch=(), flops=0, limit=SOME):
    alone = not isinstance(out_shape, tuple)
    return pl.pallas_call(
        body,
        out_shape=out_shape,
        in_specs=in_specs,
        out_specs=VMEM if alone else (VMEM,) * len(out_shape),
        scratch_shapes=scratch,
        compiler_params=pltpu.CompilerParams(vmem_limit_bytes=limit),
        cost_estimate=pl.CostEstimate(flops=flops, bytes_accessed=4 << 20, transcendentals=0),
        name=name,
    )


def local(
    activations,
    out_grads,
    counts,
    slot_weights,
    master,
    moment_one,
    moment_two,
    old_table,
    new_table,
):
    f32 = jnp.float32
    n = lax.axis_size("dp")
    owners = lax.axis_size("ep")
    me = lax.axis_index("dp")
    slots, tokens, ff = activations.shape
    experts, rows, lanes = master.shape

    def shifted(x, k):
        return lax.ppermute(x, "dp", [(i, (i + k) % n) for i in range(n)])

    def shape(*dims):
        return jax.ShapeDtypeStruct(dims, f32)

    place = me.astype(jnp.int32).reshape(1)
    limits = counts[:, 0]
    far = n // 2
    shifts = [far] + [k for k in range(1, n) if k != far]
    packet = shape(slots, tokens, ff + lanes)
    work = 6 * slots * tokens * n * ff * lanes

    own, *packed = kernel(
        pack_kernel, (shape(slots, tokens, lanes),) + (packet,) * (n - 1), [SMEM, SMEM, VMEM, VMEM], "pack", limit=MOST
    )(place, limits, activations, out_grads)
    came = {k: shifted(packed[k - 1], k) for k in shifts}
    others = [came[k] for k in range(1, n)]
    column_grad = kernel(grad_kernel, shape(slots * ff, lanes), [VMEM] * (n + 1), "slot_grads", flops=work)(
        activations, own, *others
    )
    arrived = lax.all_to_all(
        column_grad.reshape(owners, 1, slots * rows * lanes), "ep", split_axis=0, concat_axis=0, tiled=True
    )
    kept, *parts = kernel(product_kernel, (packet,) * n, [ANY] + [VMEM] * (n + 2), "products", flops=2 * work)(
        column_grad, slot_weights, activations, own, *others
    )
    back = {k: shifted(parts[k - 1], n - k) for k in shifts}

    plane = shape(rows, experts, lanes)
    flip = lambda x: jnp.transpose(x, (1, 0, 2))
    new_master, new_one, new_two, send = kernel(
        adamw_kernel,
        (plane, plane, plane, shape(slots * rows * owners, lanes)),
        [ANY] + [VMEM] * 3 + [ANY] * 3,
        "adamw",
        scratch=[pltpu.VMEM(plane.shape, f32)] * 3 + [pltpu.SemaphoreType.DMA((3,))],
        flops=work,
        limit=MOST,
    )(
        back[far],
        arrived.reshape(slots * rows * owners, lanes),
        old_table.reshape(owners, slots).T,
        new_table.reshape(owners, slots).T,
        flip(master),
        flip(moment_one),
        flip(moment_two),
    )
    placed = lax.all_to_all(
        send.reshape(owners, 1, slots * rows * lanes), "ep", split_axis=0, concat_axis=0, tiled=True
    )
    outputs, input_grads = kernel(
        combine_kernel, (shape(*out_grads.shape), shape(*activations.shape)), [SMEM, SMEM] + [VMEM] * n, "combine"
    )(place, limits, kept, *[back[k] for k in range(1, n)])
    new_slots = kernel(place_kernel, shape(*slot_weights.shape), [VMEM], "new_slots")(
        placed.reshape(ff * slots, lanes)
    )
    return (outputs, input_grads, flip(new_master), flip(new_one), flip(new_two), new_slots)


def solution(mesh):
    in_specs = (
        P("ep", "dp", None),
        P("ep", "dp", None),
        P("ep", "dp"),
        P("ep", None, "dp"),
        P(None, "ep", "dp"),
        P(None, "ep", "dp"),
        P(None, "ep", "dp"),
        P(),
        P(),
    )
    out_specs = (
        P("ep", "dp", None),
        P("ep", "dp", None),
        P(None, "ep", "dp"),
        P(None, "ep", "dp"),
        P(None, "ep", "dp"),
        P("ep", None, "dp"),
    )
    return jax.shard_map(local, mesh=mesh, in_specs=in_specs, out_specs=out_specs, check_vma=False)
```

time: 125 us -> 118 us (0.944)
  starting transfers between devices: 69.2 us -> 51.9 us
  waiting for transfers between devices: 34.2 us -> 46.1 us
  Pallas kernels: 7.37 us -> 12.6 us
  local copies, waits for them, and re-layouts: 8.94 us -> 3.76 us
  other arithmetic: 3.09 us -> 1.33 us
    ppermute x9 -> x6, starting transfers between devices: 34.7 us -> 22.3 us  [shifted(): return lax.ppermute(x, 'dp', [(i, (i + k) % n) for i in range(n)])]
    all_to_all x1, waiting for transfers between devices: 0.01 us -> 5.44 us  [local(): lax.all_to_all(send.reshape(owners, 1, slots * rows * lanes), 'ep', split...]
    pallas_call x3 -> x6, Pallas kernels: 7.37 us -> 12.6 us  [the longest x1 4.11 us: local(): kernel(adamw_kernel, (plane, plane, plane, shape(slots * rows * owners, l...]
    all_to_all x1, waiting for transfers between devices: 2.18 us -> 6.98 us  [local(): lax.all_to_all(column_grad.reshape(owners, 1, slots * rows * lanes), 'ep'...]
    all_to_all x1, starting transfers between devices: 13.5 us -> 9.07 us  [local(): lax.all_to_all(send.reshape(owners, 1, slots * rows * lanes), 'ep', split...]
    unnamed x20 -> x23, local copies, waits for them, and re-layouts: 5.59 us -> 2.21 us
    ppermute x9 -> x6, waiting for transfers between devices: 32 us -> 33.7 us  [shifted(): return lax.ppermute(x, 'dp', [(i, (i + k) % n) for i in range(n)])]
  transfers between devices with their start and end apart: 11 -> 8, of which waited for: 6 -> 6; matrix products, arithmetic and copies ran while one was open for 6% -> 3% of each run, Pallas kernels for 3% -> 3%
where the time goes in v2:
time: 118 us; the launch traced here: 116 us
  starting transfers between devices  51.9 us (44%)
  waiting for transfers between devices  46.1 us (39%)
  Pallas kernels  12.6 us (11%)
  local copies, waits for them, and re-layouts  3.76 us (3%)
  other arithmetic  1.33 us (1%)
    ppermute x6, waiting for transfers between devices, shifted(): return lax.ppermute(x, 'dp', [(i, (i + k) % n) for i in range(n)])  33.7 us
    ppermute x6, starting transfers between devices, shifted(): return lax.ppermute(x, 'dp', [(i, (i + k) % n) for i in range(n)])  22.3 us
    all_to_all x1, starting transfers between devices, local(): lax.all_to_all(column_grad.reshape(owners, 1, slots * rows * lanes), 'ep'...  20.5 us
    all_to_all x1, starting transfers between devices, local(): lax.all_to_all(send.reshape(owners, 1, slots * rows * lanes), 'ep', split...  9.07 us
    all_to_all x1, waiting for transfers between devices, local(): lax.all_to_all(column_grad.reshape(owners, 1, slots * rows * lanes), 'ep'...  6.98 us
    all_to_all x1, waiting for transfers between devices, local(): lax.all_to_all(send.reshape(owners, 1, slots * rows * lanes), 'ep', split...  5.44 us
    pallas_call x1, Pallas kernels, local(): kernel(adamw_kernel, (plane, plane, plane, shape(slots * rows * owners, l...  4.11 us
  transfers between devices with their start and end apart: 8, of which 6 were waited for; matrix products, arithmetic and copies ran while one was open for 3% of the time, Pallas kernels for 3%

profile of v2, /device:TPU:1, one launch (start us, length us, event | category | flops | bytes accessed | tf_op | source)
XLA Modules:
  0.0 116.5 jit_solution(16901480772312515904)
XLA Ops:
  0.6 0.0 copy-start
  0.6 2.3 %pack.1 = (f32[2,64,128]{2,1,0:T(8,128)}, f32[2,64,896]{2,1,0:T(8,128)}, f32[2,64,896]{2,1,0:T(8,128)}, f32[2,64,896]{2,1,0:T(8,128)}) custom-call(s32[1]{0:T(128)} %bitcast.place, s32[2]{0:T(128)} %bitcast.17, f32[2,64,768]{2,1,0:T(8,128)} %acts.5, f32[2,64,512]{2,1,0:T(8,128)} %grads.1), custom_call_target="tpu_custom_call" | custom-call | bytes 4194304 | tf_op jit(solution)/shard_map/pack/pallas_call | solution.py:214
  2.9 3.9 %collective-permute-start = (f32[2,64,896]{2,1,0:T(8,128)}, f32[2,64,896]{2,1,0:T(8,128)S(1)}, u32[]{:S(2)}, u32[]{:S(2)}) collective-permute-start(f32[2,64,896]{2,1,0:T(8,128)} %get-tuple-element.21), channel_id=1, source_target_pairs={{0,1},{1,2},{2,3},{3,0},{4,5},{5,6},{6,7},{7,4},{8,9},{9,10},{10,1... | collective-permute-start | bytes 1376264 | tf_op jit(solution)/shard_map/ppermute | solution.py:202
  6.9 4.4 %collective-permute-start.1 = (f32[2,64,896]{2,1,0:T(8,128)}, f32[2,64,896]{2,1,0:T(8,128)S(1)}, u32[]{:S(2)}, u32[]{:S(2)}) collective-permute-start(f32[2,64,896]{2,1,0:T(8,128)} %get-tuple-element.22), channel_id=1, source_target_pairs={{0,2},{1,3},{2,0},{3,1},{4,6},{5,7},{6,4},{7,5},{8,10},{9,11},{10,... | collective-permute-start | bytes 1376264 | tf_op jit(solution)/shard_map/ppermute | solution.py:202
  11.2 3.1 %collective-permute-start.2 = (f32[2,64,896]{2,1,0:T(8,128)}, f32[2,64,896]{2,1,0:T(8,128)S(1)}, u32[]{:S(2)}, u32[]{:S(2)}) collective-permute-start(f32[2,64,896]{2,1,0:T(8,128)} %get-tuple-element.23), channel_id=1, source_target_pairs={{0,3},{1,0},{2,1},{3,2},{4,7},{5,4},{6,5},{7,6},{8,11},{9,8},{10,9... | collective-permute-start | bytes 1376264 | tf_op jit(solution)/shard_map/ppermute | solution.py:202
  14.3 0.0 collective-permute-done.refs_0_
  14.3 15.0 %collective-permute-done.1.refs_1_ = f32[2,64,896]{2,1,0:T(8,128)S(1)} collective-permute-done((f32[2,64,896]{2,1,0:T(8,128)}, f32[2,64,896]{2,1,0:T(8,128)S(1)}, u32[]{:S(2)}, u32[]{:S(2)}) %collective-permute-start.1) | collective-permute-done | bytes 458784 | tf_op jit(solution)/shard_map/ppermute | solution.py:202
  29.3 0.0 collective-permute-done.2.refs_2_
  29.3 0.0 copy-done
  29.3 0.0 copy-start.4
  29.3 0.8 copy-done.4
  30.2 1.7 %slot_grads.1.after = f32[1536,128]{1,0:T(8,128)} custom-call(f32[2,64,768]{2,1,0:T(8,128)S(1)} %copy-done, f32[2,64,128]{2,1,0:T(8,128)S(1)} %copy-done.4, f32[2,64,896]{2,1,0:T(8,128)S(1)} %collective-permute-done.refs_0_, f32[2,64,896]{2,1,0:T(8,128)S(1)} %collective-permute-done.1.refs_1_, f32[2,64,896]{2,1,0:T(8,128)S(1)} %collective-permute-done.2.refs_2_), custom_call_target="tpu_custom_call" | custom-call | flops 301989888 | bytes 4194304 | tf_op jit(solution)/shard_map/slot_grads/pallas_call | solution.py:219
  31.9 0.0 copy-start.3
  31.9 0.0 copy-start.5
  31.9 20.5 %all-to-all-start = ((f32[128,1,1536]{2,1,0:T(1,128)}), f32[128,1,1536]{2,1,0:T(1,128)}, u32[]{:S(2)}, u32[]{:S(2)}) async-start(f32[128,1,1536]{2,1,0:T(1,128)} %bitcast.2), calls=%async_computation | async-start | bytes 1572864 | tf_op jit(solution)/shard_map/all_to_all | solution.py:222
  52.4 0.0 copy-done.3
  52.4 0.0 copy-done.5
  52.4 2.1 %products.1 = (f32[2,64,896]{2,1,0:T(8,128)S(1)}, f32[2,64,896]{2,1,0:T(8,128)S(1)}, f32[2,64,896]{2,1,0:T(8,128)}, f32[2,64,896]{2,1,0:T(8,128)S(1)}) custom-call(f32[1536,128]{1,0:T(8,128)} %slot_grads.1.after, f32[2,768,128]{2,1,0:T(8,128)S(1)} %copy-done.3, f32[2,64,768]{2,1,0:T(8,128)S(1)} %copy-done, f32[2,64,128]{2,1,0:T(8,128)S(1)} %copy-done.5, ...), custom_call_target="tpu_custom_call" | custom-call | flops 603979776 | bytes 4194304 | tf_op jit(solution)/shard_map/products/pallas_call | solution.py:225
  54.5 0.8 copy-done.7
  55.3 4.8 %collective-permute-start.4 = (f32[2,64,896]{2,1,0:T(8,128)}, f32[2,64,896]{2,1,0:T(8,128)S(1)}, u32[]{:S(2)}, u32[]{:S(2)}) collective-permute-start(f32[2,64,896]{2,1,0:T(8,128)} %get-tuple-element.26), channel_id=1, source_target_pairs={{0,2},{1,3},{2,0},{3,1},{4,6},{5,7},{6,4},{7,5},{8,10},{9,11},{10,... | collective-permute-start | bytes 1376264 | tf_op jit(solution)/shard_map/ppermute | solution.py:202
  60.1 0.5 broadcast.6
  60.6 0.0 copy-done.9
  60.6 0.7 reduce.6
  61.3 0.1 reshape.36
  61.4 0.0 copy-start.10
  61.5 0.6 copy.18
  62.1 0.0 copy-done.10
  62.1 0.7 reduce.7
  62.8 0.1 reshape.37
  62.9 0.6 copy.19
  63.6 6.7 %collective-permute-done.4.refs_2_.after = f32[2,64,896]{2,1,0:T(8,128)S(1)} collective-permute-done((f32[2,64,896]{2,1,0:T(8,128)}, f32[2,64,896]{2,1,0:T(8,128)S(1)}, u32[]{:S(2)}, u32[]{:S(2)}) %collective-permute-start.4) | collective-permute-done | bytes 458784 | tf_op jit(solution)/shard_map/ppermute | solution.py:202
  70.2 7.0 %all-to-all-done = f32[128,1,1536]{2,1,0:T(1,128)} async-done(((f32[128,1,1536]{2,1,0:T(1,128)}), f32[128,1,1536]{2,1,0:T(1,128)}, u32[]{:S(2)}, u32[]{:S(2)}) %all-to-all-start) | async-done | bytes 786464 | tf_op jit(solution)/shard_map/all_to_all | solution.py:222
  77.2 0.0 copy-done.1
  77.2 4.1 %adamw.1 = (f32[6,128,128]{2,1,0:T(8,128)}, f32[6,128,128]{2,1,0:T(8,128)}, f32[6,128,128]{2,1,0:T(8,128)}, f32[1536,128]{1,0:T(8,128)}) custom-call(f32[2,64,896]{2,1,0:T(8,128)} %copy-done.1, f32[1536,128]{1,0:T(8,128)} %bitcast.3.arrived, s32[2,128]{1,0:T(2,128)} %bitcast.23, s32[2,128]{1,0:T(2,128)} %bitcast.24, f32[6,128,128]{2,1,0:T(8,128)} %bitcast.20, ...), custom_call_target="tpu_custom_call" | custom-call | flops 301989888 | bytes 4194304 | tf_op jit(solution)/shard_map/adamw/pallas_call | solution.py:232
  81.3 0.0 copy-start.8
  81.3 0.0 copy-start.2
  81.4 9.1 %all-to-all-start.1 = ((f32[128,1,1536]{2,1,0:T(1,128)}), f32[128,1,1536]{2,1,0:T(1,128)S(1)}, u32[]{:S(2)}, u32[]{:S(2)}) async-start(f32[128,1,1536]{2,1,0:T(1,128)} %bitcast.19), calls=%async_computation.1 | async-start | bytes 1572864 | tf_op jit(solution)/shard_map/all_to_all | solution.py:249
  90.4 0.0 copy-done.8
  90.4 4.3 %collective-permute-start.3 = (f32[2,64,896]{2,1,0:T(8,128)S(1)}, f32[2,64,896]{2,1,0:T(8,128)S(1)}, u32[]{:S(2)}, u32[]{:S(2)}) collective-permute-start(f32[2,64,896]{2,1,0:T(8,128)S(1)} %copy-done.8), channel_id=1, source_target_pairs={{0,3},{1,0},{2,1},{3,2},{4,7},{5,4},{6,5},{7,6},{8,11},{9,8},{10,9... | collective-permute-start | bytes 1376264 | tf_op jit(solution)/shard_map/ppermute | solution.py:202
  94.7 0.0 copy-start.6
  94.7 1.9 %collective-permute-start.5 = (f32[2,64,896]{2,1,0:T(8,128)S(1)}, f32[2,64,896]{2,1,0:T(8,128)S(1)}, u32[]{:S(2)}, u32[]{:S(2)}) collective-permute-start(f32[2,64,896]{2,1,0:T(8,128)S(1)} %get-tuple-element.27), channel_id=1, source_target_pairs={{0,1},{1,2},{2,3},{3,0},{4,5},{5,6},{6,7},{7,4},{8,9},{9,10},{10,1... | collective-permute-start | bytes 1376264 | tf_op jit(solution)/shard_map/ppermute | solution.py:202
  96.6 7.8 %collective-permute-done.3.refs_1_ = f32[2,64,896]{2,1,0:T(8,128)S(1)} collective-permute-done((f32[2,64,896]{2,1,0:T(8,128)S(1)}, f32[2,64,896]{2,1,0:T(8,128)S(1)}, u32[]{:S(2)}, u32[]{:S(2)}) %collective-permute-start.3) | collective-permute-done | bytes 458784 | tf_op jit(solution)/shard_map/ppermute | solution.py:202
  104.4 4.2 %collective-permute-done.5.refs_3_ = f32[2,64,896]{2,1,0:T(8,128)S(1)} collective-permute-done((f32[2,64,896]{2,1,0:T(8,128)S(1)}, f32[2,64,896]{2,1,0:T(8,128)S(1)}, u32[]{:S(2)}, u32[]{:S(2)}) %collective-permute-start.5) | collective-permute-done | bytes 458784 | tf_op jit(solution)/shard_map/ppermute | solution.py:202
  108.7 0.0 copy-done.2
  108.7 0.0 copy-done.6
  108.7 1.5 %combine.1 = (f32[2,64,512]{2,1,0:T(8,128)}, f32[2,64,768]{2,1,0:T(8,128)}) custom-call(s32[1]{0:T(128)} %bitcast.place, s32[2]{0:T(128)S(1)} %bitcast.18, f32[2,64,896]{2,1,0:T(8,128)S(1)} %get-tuple-element.24.refs_0_, f32[2,64,896]{2,1,0:T(8,128)S(1)} %collective-permute-done.3.refs_1_, f32[2,64,896]{2,1,0:T(8,128)S(1)} %copy-done.2, ...), custom_call_target="tpu_custom_call" | custom-call | bytes 4194304 | tf_op jit(solution)/shard_map/combine/pallas_call | solution.py:252
  110.1 5.4 %all-to-all-done.1 = f32[128,1,1536]{2,1,0:T(1,128)S(1)} async-done(((f32[128,1,1536]{2,1,0:T(1,128)}), f32[128,1,1536]{2,1,0:T(1,128)S(1)}, u32[]{:S(2)}, u32[]{:S(2)}) %all-to-all-start.1) | async-done | bytes 786464 | tf_op jit(solution)/shard_map/all_to_all | solution.py:249
  115.6 0.9 new_slots.1
  (3 shorter events, 0.0 us)
Async XLA Ops:
  0.6 28.7 %copy-start = (f32[2,64,768]{2,1,0:T(8,128)S(1)}, f32[2,64,768]{2,1,0:T(8,128)}, u32[]{:S(2)}) copy-start(f32[2,64,768]{2,1,0:T(8,128)} %acts.5) | copy-start | bytes 1179652
  2.9 11.4 %collective-permute-start = (f32[2,64,896]{2,1,0:T(8,128)}, f32[2,64,896]{2,1,0:T(8,128)S(1)}, u32[]{:S(2)}, u32[]{:S(2)}) collective-permute-start(f32[2,64,896]{2,1,0:T(8,128)} %get-tuple-element.21), channel_id=1, source_target_pairs={{0,1},{1,2},{2,3},{3,0},{4,5},{5,6},{6,7},{7,4},{8,9},{9,10},{10,1... | collective-permute-start | bytes 1376264 | tf_op jit(solution)/shard_map/ppermute | solution.py:202
  6.9 22.4 %collective-permute-start.1 = (f32[2,64,896]{2,1,0:T(8,128)}, f32[2,64,896]{2,1,0:T(8,128)S(1)}, u32[]{:S(2)}, u32[]{:S(2)}) collective-permute-start(f32[2,64,896]{2,1,0:T(8,128)} %get-tuple-element.22), channel_id=1, source_target_pairs={{0,2},{1,3},{2,0},{3,1},{4,6},{5,7},{6,4},{7,5},{8,10},{9,11},{10,... | collective-permute-start | bytes 1376264 | tf_op jit(solution)/shard_map/ppermute | solution.py:202
  11.2 18.1 %collective-permute-start.2 = (f32[2,64,896]{2,1,0:T(8,128)}, f32[2,64,896]{2,1,0:T(8,128)S(1)}, u32[]{:S(2)}, u32[]{:S(2)}) collective-permute-start(f32[2,64,896]{2,1,0:T(8,128)} %get-tuple-element.23), channel_id=1, source_target_pairs={{0,3},{1,0},{2,1},{3,2},{4,7},{5,4},{6,5},{7,6},{8,11},{9,8},{10,9... | collective-permute-start | bytes 1376264 | tf_op jit(solution)/shard_map/ppermute | solution.py:202
  29.3 0.8 copy-start.4
  31.9 20.5 %copy-start.3 = (f32[2,768,128]{2,1,0:T(8,128)S(1)}, f32[2,768,128]{2,1,0:T(8,128)}, u32[]{:S(2)}) copy-start(f32[2,768,128]{2,1,0:T(8,128)} %weights.1) | copy-start | bytes 2359300
  31.9 20.5 %copy-start.5 = (f32[2,64,128]{2,1,0:T(8,128)S(1)}, f32[2,64,128]{2,1,0:T(8,128)}, u32[]{:S(2)}) copy-start(f32[2,64,128]{2,1,0:T(8,128)} %get-tuple-element.20.grads) | copy-start | bytes 196612
  31.9 45.3 %all-to-all-start = ((f32[128,1,1536]{2,1,0:T(1,128)}), f32[128,1,1536]{2,1,0:T(1,128)}, u32[]{:S(2)}, u32[]{:S(2)}) async-start(f32[128,1,1536]{2,1,0:T(1,128)} %bitcast.2), calls=%async_computation | async-start | bytes 1572864 | tf_op jit(solution)/shard_map/all_to_all | solution.py:222
  54.5 0.8 copy-start.7
  55.3 5.3 %copy-start.9 = (s32[256,1]{0,1:T(1,128)S(1)}, s32[256,1]{0,1:T(1,128)}, u32[]{:S(2)}) copy-start(s32[256,1]{0,1:T(1,128)} %param.16) | copy-start | bytes 3076
  55.3 14.9 %collective-permute-start.4 = (f32[2,64,896]{2,1,0:T(8,128)}, f32[2,64,896]{2,1,0:T(8,128)S(1)}, u32[]{:S(2)}, u32[]{:S(2)}) collective-permute-start(f32[2,64,896]{2,1,0:T(8,128)} %get-tuple-element.26), channel_id=1, source_target_pairs={{0,2},{1,3},{2,0},{3,1},{4,6},{5,7},{6,4},{7,5},{8,10},{9,11},{10,... | collective-permute-start | bytes 1376264 | tf_op jit(solution)/shard_map/ppermute | solution.py:202
  61.4 0.7 copy-start.10
  70.2 7.0 %copy-start.1 = (f32[2,64,896]{2,1,0:T(8,128)}, f32[2,64,896]{2,1,0:T(8,128)S(1)}, u32[]{:S(2)}) copy-start(f32[2,64,896]{2,1,0:T(8,128)S(1)} %collective-permute-done.4.refs_2_.after) | copy-start | bytes 1376260
  81.3 9.1 %copy-start.8 = (f32[2,64,896]{2,1,0:T(8,128)S(1)}, f32[2,64,896]{2,1,0:T(8,128)}, u32[]{:S(2)}) copy-start(f32[2,64,896]{2,1,0:T(8,128)} %copy-done.7) | copy-start | bytes 1376260
  81.3 27.3 %copy-start.2 = (f32[2,64,896]{2,1,0:T(8,128)S(1)}, f32[2,64,896]{2,1,0:T(8,128)}, u32[]{:S(2)}) copy-start(f32[2,64,896]{2,1,0:T(8,128)} %copy-done.1) | copy-start | bytes 1376260
  81.4 34.2 %all-to-all-start.1 = ((f32[128,1,1536]{2,1,0:T(1,128)}), f32[128,1,1536]{2,1,0:T(1,128)S(1)}, u32[]{:S(2)}, u32[]{:S(2)}) async-start(f32[128,1,1536]{2,1,0:T(1,128)} %bitcast.19), calls=%async_computation.1 | async-start | bytes 1572864 | tf_op jit(solution)/shard_map/all_to_all | solution.py:249
  90.4 14.0 %collective-permute-start.3 = (f32[2,64,896]{2,1,0:T(8,128)S(1)}, f32[2,64,896]{2,1,0:T(8,128)S(1)}, u32[]{:S(2)}, u32[]{:S(2)}) collective-permute-start(f32[2,64,896]{2,1,0:T(8,128)S(1)} %copy-done.8), channel_id=1, source_target_pairs={{0,3},{1,0},{2,1},{3,2},{4,7},{5,4},{6,5},{7,6},{8,11},{9,8},{10,9... | collective-permute-start | bytes 1376264 | tf_op jit(solution)/shard_map/ppermute | solution.py:202
  94.7 14.0 %copy-start.6 = (s32[2,1]{0,1:T(1,128)S(1)}, s32[2,1]{0,1:T(1,128)}, u32[]{:S(2)}) copy-start(s32[2,1]{0,1:T(1,128)} %param.11) | copy-start | bytes 28
  94.7 13.9 %collective-permute-start.5 = (f32[2,64,896]{2,1,0:T(8,128)S(1)}, f32[2,64,896]{2,1,0:T(8,128)S(1)}, u32[]{:S(2)}, u32[]{:S(2)}) collective-permute-start(f32[2,64,896]{2,1,0:T(8,128)S(1)} %get-tuple-element.27), channel_id=1, source_target_pairs={{0,1},{1,2},{2,3},{3,0},{4,5},{5,6},{6,7},{7,4},{8,9},{9,10},{10,1... | collective-permute-start | bytes 1376264 | tf_op jit(solution)/shard_map/ppermute | solution.py:202

commit v3 on v2

--- a/solution.py
+++ b/solution.py
@@ -40,49 +40,57 @@
     return dot(ah, bh, dims) + (dot(ah, bl, dims) + dot(al, bh, dims))
 
 
-def pack_kernel(place, counts, acts, grads, *outs):
-    n = len(outs)
-    slots, rows, ff = acts.shape
-    for s in range(slots):
-        live = lax.broadcasted_iota(jnp.int32, (rows, 1), 0) < counts[s]
-        for k in range(n):
-            block = lax.rem(place[0] + k, n)
-            columns = pl.ds(pl.multiple_of(block * LANES, LANES), LANES)
-            g = jnp.where(live, grads[s, :, columns], 0.0)
-            if k:
-                outs[k][s, :, :ff] = acts[s]
-                outs[k][s, :, ff:] = g
-            else:
-                outs[k][s] = g
-
-
-def stacked(acts, grads, others, s):
+CUT = LANES
+
+
+def own_columns(place, counts, grads, s, k=0):
+    n = grads.shape[2] // LANES
+    live = lax.broadcasted_iota(jnp.int32, (grads.shape[1], 1), 0) < counts[s]
+    block = lax.rem(place[0] + k, n)
+    columns = pl.ds(pl.multiple_of(block * LANES, LANES), LANES)
+    return jnp.where(live, grads[s, :, columns], 0.0)
+
+
+def pack_kernel(place, counts, acts, grads, ahead, behind, opposite):
+    slots, _, ff = acts.shape
+    for s in range(slots):
+        ahead[s, :, :ff] = acts[s]
+        ahead[s, :, ff:] = own_columns(place, counts, grads, s, 1)
+        behind[s, :, :ff] = acts[s]
+        behind[s, :, ff:] = own_columns(place, counts, grads, s, 3)
+        opposite[s, :, :CUT] = acts[s, :, :CUT]
+        opposite[s, :, CUT:] = own_columns(place, counts, grads, s, 2)
+
+
+def stacked(place, counts, acts, grads, ahead, behind, opposite, relayed, s):
     ff = acts.shape[2]
-    a = jnp.concatenate([acts[s]] + [r[s, :, :ff] for r in others], axis=0)
-    g = jnp.concatenate([grads[s]] + [r[s, :, ff:] for r in others], axis=0)
+    far = jnp.concatenate([opposite[s, :, :CUT], relayed[s]], axis=1)
+    a = jnp.concatenate([acts[s], ahead[s, :, :ff], far, behind[s, :, :ff]], axis=0)
+    g = jnp.concatenate(
+        [own_columns(place, counts, grads, s), ahead[s, :, ff:], opposite[s, :, CUT:], behind[s, :, ff:]], axis=0
+    )
     return halves(a), halves(g)
 
 
-def grad_kernel(acts, grads, *refs):
-    others, out = refs[:-1], refs[-1]
-    slots, _, ff = acts.shape
-    for s in range(slots):
-        a, g = stacked(acts, grads, others, s)
+def grad_kernel(*refs):
+    given, out = refs[:-1], refs[-1]
+    slots, _, ff = given[2].shape
+    for s in range(slots):
+        a, g = stacked(*given, s)
         out[pl.ds(s, ff, stride=slots), :] = dot_split(a, g, ((0,), (0,)))
 
 
-def product_kernel(after, weights, acts, grads, *refs):
-    n = len(refs) // 2 + 1
-    others, outs = refs[: n - 1], refs[n - 1 :]
-    slots, rows, ff = acts.shape
-    for s in range(slots):
-        a, g = stacked(acts, grads, others, s)
+def product_kernel(after, weights, *refs):
+    given, outs = refs[:8], refs[8:]
+    slots, rows, ff = given[2].shape
+    for s in range(slots):
+        a, g = stacked(*given, s)
         w = halves(weights[s])
         columns = dot_split(a, w, ((1,), (0,)))
         part = dot_split(g, w, ((1,), (1,)))
-        for k in range(n):
-            outs[k][s, :, :ff] = part[k * rows : (k + 1) * rows]
-            outs[k][s, :, ff:] = columns[k * rows : (k + 1) * rows]
+        for k, out in enumerate(outs):
+            out[s, :, :ff] = part[k * rows : (k + 1) * rows]
+            out[s, :, ff:] = columns[k * rows : (k + 1) * rows]
 
 
 def combine_kernel(place, counts, *refs):
@@ -107,13 +115,22 @@
         out[s] = rows[pl.ds(s, ff, stride=slots), :]
 
 
-def adamw_kernel(after, arrived, old_table, new_table, master_in, one_in, two_in,
-                 new_master, new_one, new_two, send, master, moment_one, moment_two, arrivals):
-    copies = [
-        pltpu.make_async_copy(there, here, arrivals.at[i])
-        for i, (there, here) in enumerate([(master_in, master), (one_in, moment_one), (two_in, moment_two)])
-    ]
-    for copy in copies:
+PIECES = 4
+
+
+def adamw_kernel(after, arrived_in, old_table, new_table, master_in, one_in, two_in,
+                 master_out, one_out, two_out, send_out,
+                 arrived, master, moment_one, moment_two, new_master, new_one, new_two, send, landed, left):
+    def moves(pairs, signals, first=0):
+        return [pltpu.make_async_copy(a, b, signals.at[first + i]) for i, (a, b) in enumerate(pairs)]
+
+    def split(a, b):
+        part = a.shape[0] // PIECES
+        return [(a.at[pl.ds(i * part, part)], b.at[pl.ds(i * part, part)]) for i in range(PIECES)]
+
+    early = moves(split(arrived_in, arrived), landed)
+    later = moves([(master_in, master), (one_in, moment_one), (two_in, moment_two)], landed, PIECES)
+    for copy in early + later:
         copy.start()
     rows, experts, _ = master.shape
     slots, owners = old_table.shape
@@ -125,6 +142,10 @@
             [(ids == table[p : p + 1, :]).astype(jnp.float32).astype(jnp.bfloat16) for p in range(slots)], axis=1
         )
 
+    old = onehot(old_table)
+    new = onehot(new_table)
+    for copy in early:
+        copy.wait()
     got = jnp.concatenate(
         [
             jnp.concatenate([arrived[pl.ds(f * slots + p, owners, stride=step), :] for f in range(rows)], axis=1)
@@ -132,9 +153,8 @@
         ],
         axis=0,
     )
-    old = onehot(old_table)
     grad = sum(dot(old, part, ((1,), (0,))) for part in reversed(thirds(got)))
-    for copy in copies:
+    for copy in later:
         copy.wait()
     updated = []
     for f in range(rows):
@@ -149,7 +169,9 @@
         m = m - learn_rate * (first_hat / (jnp.sqrt(second_hat) + epsilon) + decay_rate * m)
         new_master[f] = m
         updated.append(m)
-    new = onehot(new_table)
+    results = moves([(new_master, master_out), (new_one, one_out), (new_two, two_out)], left, PIECES)
+    for copy in results:
+        copy.start()
     parts = thirds(jnp.concatenate(updated, axis=1))
     picked = sum(dot(new, part, ((0,), (0,))) for part in reversed(parts))
     for f in range(rows):
@@ -157,6 +179,11 @@
             send[pl.ds(f * slots + p, owners, stride=step), :] = picked[
                 p * owners : (p + 1) * owners, f * LANES : (f + 1) * LANES
             ]
+    sent = moves(split(send, send_out), left)
+    for copy in sent:
+        copy.start()
+    for copy in results + sent:
+        copy.wait()
 
 
 VMEM = pl.BlockSpec(memory_space=pltpu.VMEM)
@@ -166,13 +193,13 @@
 MOST = 60 * 1024 * 1024
 
 
-def kernel(body, out_shape, in_specs, name, scratch=(), flops=0, limit=SOME):
+def kernel(body, out_shape, in_specs, name, flops=0, limit=SOME, spec=VMEM, scratch=()):
     alone = not isinstance(out_shape, tuple)
     return pl.pallas_call(
         body,
         out_shape=out_shape,
         in_specs=in_specs,
-        out_specs=VMEM if alone else (VMEM,) * len(out_shape),
+        out_specs=spec if alone else (spec,) * len(out_shape),
         scratch_shapes=scratch,
         compiler_params=pltpu.CompilerParams(vmem_limit_bytes=limit),
         cost_estimate=pl.CostEstimate(flops=flops, bytes_accessed=4 << 20, transcendentals=0),
@@ -211,20 +238,27 @@
     packet = shape(slots, tokens, ff + lanes)
     work = 6 * slots * tokens * n * ff * lanes
 
-    own, *packed = kernel(
-        pack_kernel, (shape(slots, tokens, lanes),) + (packet,) * (n - 1), [SMEM, SMEM, VMEM, VMEM], "pack", limit=MOST
+    ahead, behind, opposite = kernel(
+        pack_kernel,
+        (packet, packet, shape(slots, tokens, CUT + lanes)),
+        [SMEM, SMEM, VMEM, VMEM],
+        "pack",
+        limit=MOST,
     )(place, limits, activations, out_grads)
-    came = {k: shifted(packed[k - 1], k) for k in shifts}
-    others = [came[k] for k in range(1, n)]
-    column_grad = kernel(grad_kernel, shape(slots * ff, lanes), [VMEM] * (n + 1), "slot_grads", flops=work)(
-        activations, own, *others
+    ahead = shifted(ahead, 1)
+    behind = shifted(behind, n - 1)
+    opposite = shifted(opposite, far)
+    relayed = shifted(ahead[:, :, CUT:ff], 1)
+    given = (place, limits, activations, out_grads, ahead, behind, opposite, relayed)
+    column_grad = kernel(grad_kernel, shape(slots * ff, lanes), [SMEM] * 2 + [VMEM] * 6, "slot_grads", flops=work)(
+        *given
     )
     arrived = lax.all_to_all(
         column_grad.reshape(owners, 1, slots * rows * lanes), "ep", split_axis=0, concat_axis=0, tiled=True
     )
-    kept, *parts = kernel(product_kernel, (packet,) * n, [ANY] + [VMEM] * (n + 2), "products", flops=2 * work)(
-        column_grad, slot_weights, activations, own, *others
-    )
+    kept, *parts = kernel(
+        product_kernel, (packet,) * n, [ANY, VMEM, SMEM, SMEM] + [VMEM] * 6, "products", flops=2 * work
+    )(column_grad, slot_weights, *given)
     back = {k: shifted(parts[k - 1], n - k) for k in shifts}
 
     plane = shape(rows, experts, lanes)
@@ -232,11 +266,15 @@
     new_master, new_one, new_two, send = kernel(
         adamw_kernel,
         (plane, plane, plane, shape(slots * rows * owners, lanes)),
-        [ANY] + [VMEM] * 3 + [ANY] * 3,
+        [ANY, ANY, VMEM, VMEM, ANY, ANY, ANY],
         "adamw",
-        scratch=[pltpu.VMEM(plane.shape, f32)] * 3 + [pltpu.SemaphoreType.DMA((3,))],
         flops=work,
         limit=MOST,
+        spec=ANY,
+        scratch=[pltpu.VMEM((slots * rows * owners, lanes), f32)]
+        + [pltpu.VMEM(plane.shape, f32)] * 6
+        + [pltpu.VMEM((slots * rows * owners, lanes), f32)]
+        + [pltpu.SemaphoreType.DMA((PIECES + 3,))] * 2,
     )(
         back[far],
         arrived.reshape(slots * rows * owners, lanes),

time: 118 us -> 120 us (1.017); the launches traced: 116 us -> 120 us
  starting transfers between devices: 51.9 us -> 56.3 us
  waiting for transfers between devices: 46.1 us -> 43.8 us
    ppermute x6 -> x7, starting transfers between devices: 22.3 us -> 25.6 us  [shifted(): return lax.ppermute(x, 'dp', [(i, (i + k) % n) for i in range(n)])]
    ppermute x6 -> x7, waiting for transfers between devices: 33.7 us -> 30.7 us  [shifted(): return lax.ppermute(x, 'dp', [(i, (i + k) % n) for i in range(n)])]
    all_to_all x1, waiting for transfers between devices: 5.44 us -> 7.49 us  [local(): lax.all_to_all(send.reshape(owners, 1, slots * rows * lanes), 'ep', split...]
    all_to_all x1, waiting for transfers between devices: 6.98 us -> 5.65 us  [local(): lax.all_to_all(column_grad.reshape(owners, 1, slots * rows * lanes), 'ep'...]
    all_to_all x1, starting transfers between devices: 9.07 us -> 10.4 us  [local(): lax.all_to_all(send.reshape(owners, 1, slots * rows * lanes), 'ep', split...]
  transfers between devices with their start and end apart: 8 -> 9, of which waited for: 6 -> 7; matrix products, arithmetic and copies ran while one was open for 3% -> 3% of each run, Pallas kernels for 3% -> 3%
where the time goes in v3:
time: 120 us
  starting transfers between devices  56.3 us (47%)
  waiting for transfers between devices  43.8 us (36%)
  Pallas kernels  13.6 us (11%)
  local copies, waits for them, and re-layouts  3.72 us (3%)
  other arithmetic  1.33 us (1%)
    ppermute x7, waiting for transfers between devices, shifted(): return lax.ppermute(x, 'dp', [(i, (i + k) % n) for i in range(n)])  30.7 us
    ppermute x7, starting transfers between devices, shifted(): return lax.ppermute(x, 'dp', [(i, (i + k) % n) for i in range(n)])  25.6 us
    all_to_all x1, starting transfers between devices, local(): lax.all_to_all(column_grad.reshape(owners, 1, slots * rows * lanes), 'ep'...  20.4 us
    all_to_all x1, starting transfers between devices, local(): lax.all_to_all(send.reshape(owners, 1, slots * rows * lanes), 'ep', split...  10.4 us
    all_to_all x1, waiting for transfers between devices, local(): lax.all_to_all(send.reshape(owners, 1, slots * rows * lanes), 'ep', split...  7.49 us
    all_to_all x1, waiting for transfers between devices, local(): lax.all_to_all(column_grad.reshape(owners, 1, slots * rows * lanes), 'ep'...  5.65 us
    pallas_call x1, Pallas kernels, local(): kernel(adamw_kernel, (plane, plane, plane, shape(slots * rows * owners, l...  4.15 us
    pallas_call x1, Pallas kernels, local(): kernel(product_kernel, (packet,) * n, [ANY, VMEM, SMEM, SMEM] + [VMEM] *...  2.71 us
  transfers between devices with their start and end apart: 9, of which 7 were waited for; matrix products, arithmetic and copies ran while one was open for 3% of the time, Pallas kernels for 3%

profile of v3, /device:TPU:1, one launch (start us, length us, event | category | flops | bytes accessed | tf_op | source)
XLA Modules:
  0.0 119.7 jit_solution(6792277404312638229)
XLA Ops:
  0.6 2.1 %pack.1 = (f32[2,64,896]{2,1,0:T(8,128)}, f32[2,64,896]{2,1,0:T(8,128)}, f32[2,64,256]{2,1,0:T(8,128)}) custom-call(s32[1]{0:T(128)} %bitcast.place.refs_0_, s32[2]{0:T(128)} %bitcast.17, f32[2,64,768]{2,1,0:T(8,128)} %refs_2_.3, f32[2,64,512]{2,1,0:T(8,128)} %refs_3_.3), custom_call_target="tpu_custom_call" | custom-call | bytes 4194304 | tf_op jit(solution)/shard_map/pack/pallas_call | solution.py:241
  2.7 4.1 %collective-permute-start = (f32[2,64,896]{2,1,0:T(8,128)}, f32[2,64,896]{2,1,0:T(8,128)S(1)}, u32[]{:S(2)}, u32[]{:S(2)}) collective-permute-start(f32[2,64,896]{2,1,0:T(8,128)} %get-tuple-element.19), channel_id=1, source_target_pairs={{0,1},{1,2},{2,3},{3,0},{4,5},{5,6},{6,7},{7,4},{8,9},{9,10},{10,1... | collective-permute-start | bytes 1376264 | tf_op jit(solution)/shard_map/ppermute | solution.py:229
  6.8 0.0 copy-start.1
  6.8 3.3 %collective-permute-start.1 = (f32[2,64,896]{2,1,0:T(8,128)}, f32[2,64,896]{2,1,0:T(8,128)S(1)}, u32[]{:S(2)}, u32[]{:S(2)}) collective-permute-start(f32[2,64,896]{2,1,0:T(8,128)} %get-tuple-element.20), channel_id=1, source_target_pairs={{0,3},{1,0},{2,1},{3,2},{4,7},{5,4},{6,5},{7,6},{8,11},{9,8},{10,9... | collective-permute-start | bytes 1376264 | tf_op jit(solution)/shard_map/ppermute | solution.py:229
  10.2 4.0 %collective-permute-done.refs_4_ = f32[2,64,896]{2,1,0:T(8,128)S(1)} collective-permute-done((f32[2,64,896]{2,1,0:T(8,128)}, f32[2,64,896]{2,1,0:T(8,128)S(1)}, u32[]{:S(2)}, u32[]{:S(2)}) %collective-permute-start) | collective-permute-done | bytes 458784 | tf_op jit(solution)/shard_map/ppermute | solution.py:229
  14.2 0.0 copy-start.5
  14.2 5.3 %collective-permute-start.3 = (f32[2,64,640]{2,1,0:T(8,128)S(1)}, f32[2,64,640]{2,1,0:T(8,128)S(1)}, u32[]{:S(2)}, u32[]{:S(2)}) collective-permute-start(f32[2,64,640]{2,1,0:T(8,128)S(1)} %slice.4), channel_id=1, source_target_pairs={{0,1},{1,2},{2,3},{3,0},{4,5},{5,6},{6,7},{7,4},{8,9},{9,10},{10,1... | collective-permute-start | bytes 983048 | tf_op jit(solution)/shard_map/ppermute | solution.py:229
  19.5 5.2 %collective-permute-start.2 = (f32[2,64,256]{2,1,0:T(8,128)}, f32[2,64,256]{2,1,0:T(8,128)S(1)}, u32[]{:S(2)}, u32[]{:S(2)}) collective-permute-start(f32[2,64,256]{2,1,0:T(8,128)} %get-tuple-element.21), channel_id=1, source_target_pairs={{0,2},{1,3},{2,0},{3,1},{4,6},{5,7},{6,4},{7,5},{8,10},{9,11},{10,... | collective-permute-start | bytes 393224 | tf_op jit(solution)/shard_map/ppermute | solution.py:229
  24.7 6.8 %collective-permute-done.2.refs_6_ = f32[2,64,256]{2,1,0:T(8,128)S(1)} collective-permute-done((f32[2,64,256]{2,1,0:T(8,128)}, f32[2,64,256]{2,1,0:T(8,128)S(1)}, u32[]{:S(2)}, u32[]{:S(2)}) %collective-permute-start.2) | collective-permute-done | bytes 131104 | tf_op jit(solution)/shard_map/ppermute | solution.py:229
  31.5 0.0 collective-permute-done.1.refs_5_
  31.5 0.0 collective-permute-done.3.refs_7_
  31.5 0.0 copy-done
  31.5 0.0 copy-done.1
  31.5 0.0 copy-done.5
  31.5 2.3 %slot_grads.1.after = f32[1536,128]{1,0:T(8,128)} custom-call(s32[1]{0:T(128)} %bitcast.place.refs_0_, s32[2]{0:T(128)S(1)} %bitcast.18, f32[2,64,768]{2,1,0:T(8,128)S(1)} %copy-done, f32[2,64,512]{2,1,0:T(8,128)S(1)} %copy-done.1, f32[2,64,896]{2,1,0:T(8,128)S(1)} %collective-permute-done.refs_4_, f32[2,64,896]{2,1,0:T(8,128)S(1)} %collective-permute-done.1.refs_5_, ...), custom_call_target="tpu_custom_call" | custom-call | flops 301989888 | bytes 4194304 | tf_op jit(solution)/shard_map/slot_grads/pallas_call | solution.py:253
  33.8 20.4 %all-to-all-start = ((f32[128,1,1536]{2,1,0:T(1,128)}), f32[128,1,1536]{2,1,0:T(1,128)}, u32[]{:S(2)}, u32[]{:S(2)}) async-start(f32[128,1,1536]{2,1,0:T(1,128)} %bitcast.2), calls=%async_computation | async-start | bytes 1572864 | tf_op jit(solution)/shard_map/all_to_all | solution.py:256
  54.2 0.0 copy-done.4
  54.2 2.7 %products.1 = (f32[2,64,896]{2,1,0:T(8,128)S(1)}, f32[2,64,896]{2,1,0:T(8,128)S(1)}, f32[2,64,896]{2,1,0:T(8,128)}, f32[2,64,896]{2,1,0:T(8,128)S(1)}) custom-call(f32[1536,128]{1,0:T(8,128)} %slot_grads.1.after, f32[2,768,128]{2,1,0:T(8,128)S(1)} %copy-done.4, s32[1]{0:T(128)} %bitcast.place.refs_0_, s32[2]{0:T(128)S(1)} %bitcast.19, ...), custom_call_target="tpu_custom_call" | custom-call | flops 603979776 | bytes 4194304 | tf_op jit(solution)/shard_map/products/pallas_call | solution.py:259
  56.9 0.8 copy-done.6
  57.7 0.8 copy-done.8
  58.5 2.4 %collective-permute-start.5 = (f32[2,64,896]{2,1,0:T(8,128)}, f32[2,64,896]{2,1,0:T(8,128)S(1)}, u32[]{:S(2)}, u32[]{:S(2)}) collective-permute-start(f32[2,64,896]{2,1,0:T(8,128)} %get-tuple-element.24), channel_id=1, source_target_pairs={{0,2},{1,3},{2,0},{3,1},{4,6},{5,7},{6,4},{7,5},{8,10},{9,11},{10,... | collective-permute-start | bytes 1376264 | tf_op jit(solution)/shard_map/ppermute | solution.py:229
  60.9 0.5 broadcast.6
  61.4 0.0 copy-done.10
  61.4 0.7 reduce.6
  62.1 0.1 reshape.36
  62.2 0.0 copy-start.11
  62.2 0.6 copy.18
  62.8 0.0 copy-done.11
  62.9 0.7 reduce.7
  63.5 0.1 reshape.37
  63.7 0.6 copy.19
  64.3 9.1 %collective-permute-done.5.refs_2_.after = f32[2,64,896]{2,1,0:T(8,128)S(1)} collective-permute-done((f32[2,64,896]{2,1,0:T(8,128)}, f32[2,64,896]{2,1,0:T(8,128)S(1)}, u32[]{:S(2)}, u32[]{:S(2)}) %collective-permute-start.5) | collective-permute-done | bytes 458784 | tf_op jit(solution)/shard_map/ppermute | solution.py:229
  73.4 5.7 %all-to-all-done = f32[128,1,1536]{2,1,0:T(1,128)} async-done(((f32[128,1,1536]{2,1,0:T(1,128)}), f32[128,1,1536]{2,1,0:T(1,128)}, u32[]{:S(2)}, u32[]{:S(2)}) %all-to-all-start) | async-done | bytes 786464 | tf_op jit(solution)/shard_map/all_to_all | solution.py:256
  79.0 0.0 copy-done.2
  79.0 4.2 %adamw.1 = (f32[6,128,128]{2,1,0:T(8,128)}, f32[6,128,128]{2,1,0:T(8,128)}, f32[6,128,128]{2,1,0:T(8,128)}, f32[1536,128]{1,0:T(8,128)}) custom-call(f32[2,64,896]{2,1,0:T(8,128)} %copy-done.2, f32[1536,128]{1,0:T(8,128)} %bitcast.3.arrived_in, s32[2,128]{1,0:T(2,128)} %bitcast.25, s32[2,128]{1,0:T(2,128)} %bitcast.26, f32[6,128,128]{2,1,0:T(8,128)} %bitcast.22, ...), custom_call_target="tpu_custom_call" | custom-call | flops 301989888 | bytes 4194304 | tf_op jit(solution)/shard_map/adamw/pallas_call | solution.py:266
  83.2 0.0 copy-start.9
  83.2 0.0 copy-start.7
  83.2 0.0 copy-start.3
  83.2 10.4 %all-to-all-start.1 = ((f32[128,1,1536]{2,1,0:T(1,128)}), f32[128,1,1536]{2,1,0:T(1,128)S(1)}, u32[]{:S(2)}, u32[]{:S(2)}) async-start(f32[128,1,1536]{2,1,0:T(1,128)} %bitcast.21), calls=%async_computation.1 | async-start | bytes 1572864 | tf_op jit(solution)/shard_map/all_to_all | solution.py:287
  93.6 0.0 copy-done.9
  93.6 1.9 %collective-permute-start.4 = (f32[2,64,896]{2,1,0:T(8,128)S(1)}, f32[2,64,896]{2,1,0:T(8,128)S(1)}, u32[]{:S(2)}, u32[]{:S(2)}) collective-permute-start(f32[2,64,896]{2,1,0:T(8,128)S(1)} %copy-done.9), channel_id=1, source_target_pairs={{0,3},{1,0},{2,1},{3,2},{4,7},{5,4},{6,5},{7,6},{8,11},{9,8},{10,9... | collective-permute-start | bytes 1376264 | tf_op jit(solution)/shard_map/ppermute | solution.py:229
  95.6 0.0 copy-done.7
  95.6 3.4 %collective-permute-start.6 = (f32[2,64,896]{2,1,0:T(8,128)S(1)}, f32[2,64,896]{2,1,0:T(8,128)S(1)}, u32[]{:S(2)}, u32[]{:S(2)}) collective-permute-start(f32[2,64,896]{2,1,0:T(8,128)S(1)} %copy-done.7), channel_id=1, source_target_pairs={{0,1},{1,2},{2,3},{3,0},{4,5},{5,6},{6,7},{7,4},{8,9},{9,10},{10,1... | collective-permute-start | bytes 1376264 | tf_op jit(solution)/shard_map/ppermute | solution.py:229
  99.0 7.7 %collective-permute-done.4.refs_1_ = f32[2,64,896]{2,1,0:T(8,128)S(1)} collective-permute-done((f32[2,64,896]{2,1,0:T(8,128)S(1)}, f32[2,64,896]{2,1,0:T(8,128)S(1)}, u32[]{:S(2)}, u32[]{:S(2)}) %collective-permute-start.4) | collective-permute-done | bytes 458784 | tf_op jit(solution)/shard_map/ppermute | solution.py:229
  106.7 3.1 %collective-permute-done.6.refs_3_ = f32[2,64,896]{2,1,0:T(8,128)S(1)} collective-permute-done((f32[2,64,896]{2,1,0:T(8,128)S(1)}, f32[2,64,896]{2,1,0:T(8,128)S(1)}, u32[]{:S(2)}, u32[]{:S(2)}) %collective-permute-start.6) | collective-permute-done | bytes 458784 | tf_op jit(solution)/shard_map/ppermute | solution.py:229
  109.8 1.5 %combine.1 = (f32[2,64,512]{2,1,0:T(8,128)}, f32[2,64,768]{2,1,0:T(8,128)}) custom-call(s32[1]{0:T(128)} %bitcast.place.refs_0_, s32[2]{0:T(128)S(1)} %bitcast.20, f32[2,64,896]{2,1,0:T(8,128)S(1)} %get-tuple-element.22.refs_0_, f32[2,64,896]{2,1,0:T(8,128)S(1)} %collective-permute-done.4.refs_1_, f32[2,64,896]{2,1,0:T(8,128)S(1)} %copy-done.3, ...), custom_call_target="tpu_custom_call" | custom-call | bytes 4194304 | tf_op jit(solution)/shard_map/combine/pallas_call | solution.py:290
  111.3 7.5 %all-to-all-done.1 = f32[128,1,1536]{2,1,0:T(1,128)S(1)} async-done(((f32[128,1,1536]{2,1,0:T(1,128)}), f32[128,1,1536]{2,1,0:T(1,128)S(1)}, u32[]{:S(2)}, u32[]{:S(2)}) %all-to-all-start.1) | async-done | bytes 786464 | tf_op jit(solution)/shard_map/all_to_all | solution.py:287
  118.8 0.9 new_slots.1
  (8 shorter events, 0.0 us)
Async XLA Ops:
  2.7 28.8 %copy-start = (f32[2,64,768]{2,1,0:T(8,128)S(1)}, f32[2,64,768]{2,1,0:T(8,128)}, u32[]{:S(2)}) copy-start(f32[2,64,768]{2,1,0:T(8,128)} %refs_2_.3) | copy-start | bytes 1179652
  2.7 11.4 %collective-permute-start = (f32[2,64,896]{2,1,0:T(8,128)}, f32[2,64,896]{2,1,0:T(8,128)S(1)}, u32[]{:S(2)}, u32[]{:S(2)}) collective-permute-start(f32[2,64,896]{2,1,0:T(8,128)} %get-tuple-element.19), channel_id=1, source_target_pairs={{0,1},{1,2},{2,3},{3,0},{4,5},{5,6},{6,7},{7,4},{8,9},{9,10},{10,1... | collective-permute-start | bytes 1376264 | tf_op jit(solution)/shard_map/ppermute | solution.py:229
  6.8 24.7 %copy-start.1 = (f32[2,64,512]{2,1,0:T(8,128)S(1)}, f32[2,64,512]{2,1,0:T(8,128)}, u32[]{:S(2)}) copy-start(f32[2,64,512]{2,1,0:T(8,128)} %refs_3_.3) | copy-start | bytes 786436
  6.8 24.7 %collective-permute-start.1 = (f32[2,64,896]{2,1,0:T(8,128)}, f32[2,64,896]{2,1,0:T(8,128)S(1)}, u32[]{:S(2)}, u32[]{:S(2)}) collective-permute-start(f32[2,64,896]{2,1,0:T(8,128)} %get-tuple-element.20), channel_id=1, source_target_pairs={{0,3},{1,0},{2,1},{3,2},{4,7},{5,4},{6,5},{7,6},{8,11},{9,8},{10,9... | collective-permute-start | bytes 1376264 | tf_op jit(solution)/shard_map/ppermute | solution.py:229
  14.2 17.3 %copy-start.5 = (s32[2,1]{0,1:T(1,128)S(1)}, s32[2,1]{0,1:T(1,128)}, u32[]{:S(2)}) copy-start(s32[2,1]{0,1:T(1,128)} %param.11) | copy-start | bytes 28
  14.2 17.3 %collective-permute-start.3 = (f32[2,64,640]{2,1,0:T(8,128)S(1)}, f32[2,64,640]{2,1,0:T(8,128)S(1)}, u32[]{:S(2)}, u32[]{:S(2)}) collective-permute-start(f32[2,64,640]{2,1,0:T(8,128)S(1)} %slice.4), channel_id=1, source_target_pairs={{0,1},{1,2},{2,3},{3,0},{4,5},{5,6},{6,7},{7,4},{8,9},{9,10},{10,1... | collective-permute-start | bytes 983048 | tf_op jit(solution)/shard_map/ppermute | solution.py:229
  19.5 12.0 %collective-permute-start.2 = (f32[2,64,256]{2,1,0:T(8,128)}, f32[2,64,256]{2,1,0:T(8,128)S(1)}, u32[]{:S(2)}, u32[]{:S(2)}) collective-permute-start(f32[2,64,256]{2,1,0:T(8,128)} %get-tuple-element.21), channel_id=1, source_target_pairs={{0,2},{1,3},{2,0},{3,1},{4,6},{5,7},{6,4},{7,5},{8,10},{9,11},{10,... | collective-permute-start | bytes 393224 | tf_op jit(solution)/shard_map/ppermute | solution.py:229
  33.8 20.4 %copy-start.4 = (f32[2,768,128]{2,1,0:T(8,128)S(1)}, f32[2,768,128]{2,1,0:T(8,128)}, u32[]{:S(2)}) copy-start(f32[2,768,128]{2,1,0:T(8,128)} %weights.1) | copy-start | bytes 2359300
  33.8 45.3 %all-to-all-start = ((f32[128,1,1536]{2,1,0:T(1,128)}), f32[128,1,1536]{2,1,0:T(1,128)}, u32[]{:S(2)}, u32[]{:S(2)}) async-start(f32[128,1,1536]{2,1,0:T(1,128)} %bitcast.2), calls=%async_computation | async-start | bytes 1572864 | tf_op jit(solution)/shard_map/all_to_all | solution.py:256
  56.9 0.8 copy-start.6
  57.7 0.8 copy-start.8
  58.5 2.9 %copy-start.10 = (s32[256,1]{0,1:T(1,128)S(1)}, s32[256,1]{0,1:T(1,128)}, u32[]{:S(2)}) copy-start(s32[256,1]{0,1:T(1,128)} %param.16) | copy-start | bytes 3076
  58.5 14.9 %collective-permute-start.5 = (f32[2,64,896]{2,1,0:T(8,128)}, f32[2,64,896]{2,1,0:T(8,128)S(1)}, u32[]{:S(2)}, u32[]{:S(2)}) collective-permute-start(f32[2,64,896]{2,1,0:T(8,128)} %get-tuple-element.24), channel_id=1, source_target_pairs={{0,2},{1,3},{2,0},{3,1},{4,6},{5,7},{6,4},{7,5},{8,10},{9,11},{10,... | collective-permute-start | bytes 1376264 | tf_op jit(solution)/shard_map/ppermute | solution.py:229
  62.2 0.7 copy-start.11
  73.4 5.7 %copy-start.2 = (f32[2,64,896]{2,1,0:T(8,128)}, f32[2,64,896]{2,1,0:T(8,128)S(1)}, u32[]{:S(2)}) copy-start(f32[2,64,896]{2,1,0:T(8,128)S(1)} %collective-permute-done.5.refs_2_.after) | copy-start | bytes 1376260
  83.2 10.4 %copy-start.9 = (f32[2,64,896]{2,1,0:T(8,128)S(1)}, f32[2,64,896]{2,1,0:T(8,128)}, u32[]{:S(2)}) copy-start(f32[2,64,896]{2,1,0:T(8,128)} %copy-done.8) | copy-start | bytes 1376260
  83.2 12.4 %copy-start.7 = (f32[2,64,896]{2,1,0:T(8,128)S(1)}, f32[2,64,896]{2,1,0:T(8,128)}, u32[]{:S(2)}) copy-start(f32[2,64,896]{2,1,0:T(8,128)} %copy-done.6) | copy-start | bytes 1376260
  83.2 26.6 %copy-start.3 = (f32[2,64,896]{2,1,0:T(8,128)S(1)}, f32[2,64,896]{2,1,0:T(8,128)}, u32[]{:S(2)}) copy-start(f32[2,64,896]{2,1,0:T(8,128)} %copy-done.2) | copy-start | bytes 1376260
  83.2 35.5 %all-to-all-start.1 = ((f32[128,1,1536]{2,1,0:T(1,128)}), f32[128,1,1536]{2,1,0:T(1,128)S(1)}, u32[]{:S(2)}, u32[]{:S(2)}) async-start(f32[128,1,1536]{2,1,0:T(1,128)} %bitcast.21), calls=%async_computation.1 | async-start | bytes 1572864 | tf_op jit(solution)/shard_map/all_to_all | solution.py:287
  93.6 13.0 %collective-permute-start.4 = (f32[2,64,896]{2,1,0:T(8,128)S(1)}, f32[2,64,896]{2,1,0:T(8,128)S(1)}, u32[]{:S(2)}, u32[]{:S(2)}) collective-permute-start(f32[2,64,896]{2,1,0:T(8,128)S(1)} %copy-done.9), channel_id=1, source_target_pairs={{0,3},{1,0},{2,1},{3,2},{4,7},{5,4},{6,5},{7,6},{8,11},{9,8},{10,9... | collective-permute-start | bytes 1376264 | tf_op jit(solution)/shard_map/ppermute | solution.py:229
  95.6 14.2 %collective-permute-start.6 = (f32[2,64,896]{2,1,0:T(8,128)S(1)}, f32[2,64,896]{2,1,0:T(8,128)S(1)}, u32[]{:S(2)}, u32[]{:S(2)}) collective-permute-start(f32[2,64,896]{2,1,0:T(8,128)S(1)} %copy-done.7), channel_id=1, source_target_pairs={{0,1},{1,2},{2,3},{3,0},{4,5},{5,6},{6,7},{7,4},{8,9},{9,10},{10,1... | collective-permute-start | bytes 1376264 | tf_op jit(solution)/shard_map/ppermute | solution.py:229

commit v4 on v3

v4 whole, which is shorter than its diff:
```python
import jax
import jax.numpy as jnp
from jax import lax
from jax.experimental import pallas as pl
from jax.experimental.pallas import tpu as pltpu
from jax.sharding import Mesh, PartitionSpec as P

STEP = 100


beta_one = 0.9
beta_two = 0.999
learn_rate = 0.02
epsilon = 1e-08
decay_rate = 0.1

LANES = 128
PIECES = 4


def halves(x):
    high = x.astype(jnp.bfloat16)
    low = (x - high.astype(jnp.float32)).astype(jnp.bfloat16)
    return high, low


def thirds(x):
    high = x.astype(jnp.bfloat16)
    rest = x - high.astype(jnp.float32)
    middle = rest.astype(jnp.bfloat16)
    low = (rest - middle.astype(jnp.float32)).astype(jnp.bfloat16)
    return high, middle, low


def dot(a, b, dims):
    return lax.dot_general(a, b, (dims, ((), ())), preferred_element_type=jnp.float32)


def dot_split(a, b, dims):
    (ah, al), (bh, bl) = a, b
    return dot(ah, bh, dims) + (dot(ah, bl, dims) + dot(al, bh, dims))


def pack_kernel(counts, acts, grads, out):
    slots, rows, ff = acts.shape
    half = grads.shape[2] // slots
    for s in range(slots):
        live = lax.broadcasted_iota(jnp.int32, (rows, 1), 0) < counts[s]
        for b in range(slots):
            out[slots * b + s, :, :ff] = acts[s]
            out[slots * b + s, :, ff:] = jnp.where(live, grads[s, :, b * half : (b + 1) * half], 0.0)


def rows_of(came, ff):
    n, rows, width = came.shape
    a = came[:, :, :ff].reshape(n * rows, ff)
    g = came[:, :, ff:].reshape(n * rows, width - ff)
    return halves(a), halves(g)


def grad_kernel(came, out):
    ff = out.shape[0] // 2
    a, g = rows_of(came, ff)
    grad = dot_split(a, g, ((0,), (0,)))
    out[:ff] = grad[:, :LANES]
    out[ff:] = grad[:, LANES:]


def swap_kernel(after, slot, weights, out):
    out[...] = weights[1 - slot[0]]


def product_kernel(place, weights, other, came, *refs):
    outs, whole = refs[:-1], refs[-1]
    n, rows, _ = came.shape
    ff = weights.shape[1]
    slot = lax.rem(place[0], 2)
    mine, theirs = weights[slot], other[...]
    first = slot == 0
    w = halves(jnp.concatenate([jnp.where(first, mine, theirs), jnp.where(first, theirs, mine)], axis=1))
    a, g = rows_of(came, ff)
    whole[:, ff:] = dot_split(a, w, ((1,), (0,)))
    whole[:, :ff] = dot_split(g, w, ((1,), (1,)))
    for k, out in enumerate(outs):
        owner = lax.rem(place[0] + k, n)
        out[...] = whole[pl.ds(pl.multiple_of(owner * rows, rows), rows), :]


def combine_kernel(place, counts, *refs):
    parts, outputs, input_grads, whole = refs[:-3], refs[-3], refs[-2], refs[-1]
    n = len(parts)
    slots, rows, ff = input_grads.shape
    half = outputs.shape[2] // slots
    for k in range(n):
        whole[lax.rem(place[0] + n - k, n)] = parts[k][...]
    for s in range(slots):
        live = lax.broadcasted_iota(jnp.int32, (rows, 1), 0) < counts[s]
        input_grads[s] = whole[s, :, :ff] + whole[slots + s, :, :ff]
        for b in range(slots):
            outputs[s, :, b * half : (b + 1) * half] = jnp.where(live, whole[slots * b + s, :, ff:], 0.0)


def place_kernel(rows, out):
    slots, ff, _ = out.shape
    for s in range(slots):
        out[s] = rows[pl.ds(s, ff, stride=slots), :]


def adamw_kernel(after, arrived_in, old_table, new_table, master_in, one_in, two_in,
                 master_out, one_out, two_out, send_out,
                 arrived, master, moment_one, moment_two, new_master, new_one, new_two, send, landed, left):
    def moves(pairs, signals, first=0):
        return [pltpu.make_async_copy(a, b, signals.at[first + i]) for i, (a, b) in enumerate(pairs)]

    def split(a, b):
        part = a.shape[0] // PIECES
        return [(a.at[pl.ds(i * part, part)], b.at[pl.ds(i * part, part)]) for i in range(PIECES)]

    early = moves(split(arrived_in, arrived), landed)
    later = moves([(master_in, master), (one_in, moment_one), (two_in, moment_two)], landed, PIECES)
    for copy in early + later:
        copy.start()
    rows, experts, _ = master.shape
    total = old_table.shape[1]
    slots = 2
    owners = total // slots
    source = lax.broadcasted_iota(jnp.int32, (total, total), 0)
    target = lax.broadcasted_iota(jnp.int32, (total, total), 1)
    wanted = slots * lax.rem(target, owners) + target // owners
    order = (source == wanted).astype(jnp.float32).astype(jnp.bfloat16)
    ids = lax.broadcasted_iota(jnp.int32, (experts, total), 0)

    def onehot(table):
        named = jnp.broadcast_to(table[...].astype(jnp.float32), (8, total)).astype(jnp.bfloat16)
        named = dot(named, order, ((1,), (0,)))[:1].astype(jnp.int32)
        return (ids == named).astype(jnp.float32).astype(jnp.bfloat16)

    old = onehot(old_table)
    new = onehot(new_table)
    for copy in early:
        copy.wait()
    got = jnp.concatenate([arrived[pl.ds(f, total, stride=rows), :] for f in range(rows)], axis=1)
    grad = sum(dot(old, part, ((1,), (0,))) for part in reversed(thirds(got)))
    for copy in later:
        copy.wait()
    updated = []
    for f in range(rows):
        g = grad[:, f * LANES : (f + 1) * LANES]
        first = beta_one * moment_one[f] + (1.0 - beta_one) * g
        second = beta_two * moment_two[f] + (1.0 - beta_two) * g * g
        new_one[f] = first
        new_two[f] = second
        first_hat = first / (1.0 - beta_one**STEP)
        second_hat = second / (1.0 - beta_two**STEP)
        m = master[f]
        m = m - learn_rate * (first_hat / (jnp.sqrt(second_hat) + epsilon) + decay_rate * m)
        new_master[f] = m
        updated.append(m)
    results = moves([(new_master, master_out), (new_one, one_out), (new_two, two_out)], left, PIECES)
    for copy in results:
        copy.start()
    parts = thirds(jnp.concatenate(updated, axis=1))
    picked = sum(dot(new, part, ((0,), (0,))) for part in reversed(parts))
    for f in range(rows):
        for p in range(slots):
            send[pl.ds(f * slots + p, owners, stride=rows * slots), :] = picked[
                p * owners : (p + 1) * owners, f * LANES : (f + 1) * LANES
            ]
    sent = moves(split(send, send_out), left)
    for copy in sent:
        copy.start()
    for copy in results + sent:
        copy.wait()


VMEM = pl.BlockSpec(memory_space=pltpu.VMEM)
SMEM = pl.BlockSpec(memory_space=pltpu.SMEM)
ANY = pl.BlockSpec(memory_space=pl.ANY)
SOME = 24 * 1024 * 1024
MOST = 60 * 1024 * 1024


def kernel(body, out_shape, in_specs, name, flops=0, limit=SOME, spec=VMEM, scratch=()):
    alone = not isinstance(out_shape, tuple)
    return pl.pallas_call(
        body,
        out_shape=out_shape,
        in_specs=in_specs,
        out_specs=spec if alone else (spec,) * len(out_shape),
        scratch_shapes=scratch,
        compiler_params=pltpu.CompilerParams(vmem_limit_bytes=limit),
        cost_estimate=pl.CostEstimate(flops=flops, bytes_accessed=4 << 20, transcendentals=0),
        name=name,
    )


def local(
    activations,
    out_grads,
    counts,
    slot_weights,
    master,
    moment_one,
    moment_two,
    old_table,
    new_table,
):
    f32 = jnp.float32
    dp = ("half", "slot")
    n = lax.axis_size("half") * lax.axis_size("slot")
    owners = lax.axis_size("ep")
    me = lax.axis_index("half") * lax.axis_size("slot") + lax.axis_index("slot")
    slots, tokens, ff = activations.shape
    experts, rows, lanes = master.shape
    width = ff + slots * lanes

    def shape(*dims):
        return jax.ShapeDtypeStruct(dims, f32)

    def scalar(x):
        return x.astype(jnp.int32).reshape(1)

    def exchange(x, axes):
        return lax.all_to_all(x, axes, split_axis=0, concat_axis=0, tiled=True)

    place = scalar(me)
    limits = counts[:, 0]
    packet = shape(tokens, width)
    work = 6 * slots * tokens * n * ff * lanes

    packed = kernel(pack_kernel, shape(n, tokens, width), [SMEM, VMEM, VMEM], "pack", limit=MOST)(
        limits, activations, out_grads
    )
    came = exchange(packed, dp)
    column_grad = kernel(grad_kernel, shape(slots * ff, lanes), [VMEM], "slot_grads", flops=work)(came)
    arrived = exchange(column_grad.reshape(slots * owners, 1, rows * lanes), ("slot", "ep"))

    given = kernel(swap_kernel, shape(ff, lanes), [ANY, SMEM, VMEM], "swap")(
        column_grad, scalar(lax.axis_index("slot")), slot_weights
    )
    other = lax.ppermute(given, "slot", [(0, 1), (1, 0)])
    parts = kernel(
        product_kernel,
        (packet,) * n,
        [SMEM, VMEM, VMEM, VMEM],
        "products",
        flops=2 * work,
        scratch=[pltpu.VMEM((n * tokens, width), f32)],
    )(place, slot_weights, other, came)

    plane = shape(rows, experts, lanes)
    flat = shape(slots * rows * owners, lanes)
    flip = lambda x: jnp.transpose(x, (1, 0, 2))
    new_master, new_one, new_two, send = kernel(
        adamw_kernel,
        (plane, plane, plane, flat),
        [ANY, ANY, VMEM, VMEM, ANY, ANY, ANY],
        "adamw",
        flops=work,
        limit=MOST,
        spec=ANY,
        scratch=[pltpu.VMEM(flat.shape, f32)]
        + [pltpu.VMEM(plane.shape, f32)] * 6
        + [pltpu.VMEM(flat.shape, f32)]
        + [pltpu.SemaphoreType.DMA((PIECES + 3,))] * 2,
    )(
        parts[0],
        arrived.reshape(flat.shape),
        old_table.T,
        new_table.T,
        flip(master),
        flip(moment_one),
        flip(moment_two),
    )
    placed = exchange(send.reshape(owners, 1, slots * rows * lanes), "ep")
    back = [parts[0]] + [
        lax.ppermute(parts[k], dp, [(i, (i + k) % n) for i in range(n)]) for k in range(1, n)
    ]
    outputs, input_grads = kernel(
        combine_kernel,
        (shape(*out_grads.shape), shape(*activations.shape)),
        [SMEM, SMEM] + [VMEM] * n,
        "combine",
        scratch=[pltpu.VMEM((n, tokens, width), f32)],
    )(place, limits, *back)
    new_slots = kernel(place_kernel, shape(*slot_weights.shape), [VMEM], "new_slots")(
        placed.reshape(ff * slots, lanes)
    )
    return (outputs, input_grads, flip(new_master), flip(new_one), flip(new_two), new_slots)


def solution(mesh):
    ep, dp = mesh.devices.shape
    split = Mesh(mesh.devices.reshape(ep, dp // 2, 2), ("ep", "half", "slot"))
    both = ("half", "slot")
    in_specs = (
        P("ep", both, None),
        P("ep", both, None),
        P("ep", both),
        P("ep", None, both),
        P(None, "ep", both),
        P(None, "ep", both),
        P(None, "ep", both),
        P(),
        P(),
    )
    out_specs = (
        P("ep", both, None),
        P("ep", both, None),
        P(None, "ep", both),
        P(None, "ep", both),
        P(None, "ep", both),
        P("ep", None, both),
    )
    return jax.shard_map(local, mesh=split, in_specs=in_specs, out_specs=out_specs, check_vma=False)
```

time: 120 us -> 110 us (0.917)
  blocking collectives: 0 us -> 14.6 us
  waiting for transfers between devices: 43.8 us -> 33.4 us
  starting transfers between devices: 56.3 us -> 49.5 us
  local copies, waits for them, and re-layouts: 3.72 us -> 0.71 us
  Pallas kernels: 13.6 us -> 11 us
  other arithmetic: 1.33 us -> 0 us
    all_to_all x0 -> x1, blocking collectives: none -> 14.6 us  [exchange(): return lax.all_to_all(x, axes, split_axis=0, concat_axis=0, tiled=True)]
    ppermute x7 -> x4, starting transfers between devices: 25.6 us -> 13.6 us  [the longest x3 9.58 us: local(): lax.ppermute(parts[k], dp, [(i, (i + k) % n) for i in range(n)])]
    ppermute x7 -> x4, waiting for transfers between devices: 30.7 us -> 23.2 us  [the longest x1 14.7 us: local(): other = lax.ppermute(given, 'slot', [(0, 1), (1, 0)])]
    all_to_all x2, starting transfers between devices: 30.8 us -> 35.8 us  [exchange(): return lax.all_to_all(x, axes, split_axis=0, concat_axis=0, tiled=True)]
    all_to_all x2, waiting for transfers between devices: 13.1 us -> 10.2 us  [exchange(): return lax.all_to_all(x, axes, split_axis=0, concat_axis=0, tiled=True)]
    pallas_call x4 -> x5, Pallas kernels: 11.2 us -> 8.61 us  [the longest x1 4.15 us: local(): kernel(adamw_kernel, (plane, plane, plane, flat), [ANY, ANY, VMEM, VMEM,...]
    reshape x4 -> x0, local copies, waits for them, and re-layouts: 1.55 us -> none  [the longest x2 0.77 us: local(): old_table.reshape(owners, slots)]
    unnamed x25 -> x8, local copies, waits for them, and re-layouts: 2.15 us -> 0.71 us
  transfers between devices with their start and end apart: 9 -> 6, of which waited for: 7 -> 6; matrix products, arithmetic and copies ran while one was open for 3% -> 0% of each run, Pallas kernels for 3% -> 2%
where the time goes in v4:
time: 110 us
  starting transfers between devices  49.5 us (45%)
  waiting for transfers between devices  33.4 us (30%)
  blocking collectives  14.6 us (13%)
  Pallas kernels  11 us (10%)
    all_to_all x2, starting transfers between devices, exchange(): return lax.all_to_all(x, axes, split_axis=0, concat_axis=0, tiled=True)  35.8 us
    ppermute x1, waiting for transfers between devices, local(): other = lax.ppermute(given, 'slot', [(0, 1), (1, 0)])  14.7 us
    all_to_all x1, blocking collectives, exchange(): return lax.all_to_all(x, axes, split_axis=0, concat_axis=0, tiled=True)  14.6 us
    all_to_all x2, waiting for transfers between devices, exchange(): return lax.all_to_all(x, axes, split_axis=0, concat_axis=0, tiled=True)  10.2 us
    ppermute x3, starting transfers between devices, local(): lax.ppermute(parts[k], dp, [(i, (i + k) % n) for i in range(n)])  9.58 us
    ppermute x3, waiting for transfers between devices, local(): lax.ppermute(parts[k], dp, [(i, (i + k) % n) for i in range(n)])  8.45 us
    pallas_call x1, Pallas kernels, local(): kernel(adamw_kernel, (plane, plane, plane, flat), [ANY, ANY, VMEM, VMEM,...  4.15 us
    ppermute x1, starting transfers between devices, local(): other = lax.ppermute(given, 'slot', [(0, 1), (1, 0)])  4.05 us
  transfers between devices with their start and end apart: 6, of which 6 were waited for; matrix products, arithmetic and copies ran while one was open for 0% of the time, Pallas kernels for 2%

profile of v4, /device:TPU:1, one launch (start us, length us, event | category | flops | bytes accessed | tf_op | source)
XLA Modules:
  0.0 109.9 jit_solution(2361748368529526936)
XLA Ops:
  0.6 2.1 %pack.1 = f32[4,64,1024]{2,1,0:T(8,128)} custom-call(s32[2]{0:T(128)} %bitcast.16, f32[2,64,768]{2,1,0:T(8,128)} %acts.1, f32[2,64,512]{2,1,0:T(8,128)} %grads.1), custom_call_target="tpu_custom_call" | custom-call | bytes 4194304 | tf_op jit(solution)/shard_map/pack/pallas_call | solution.py:231
  2.8 14.6 %all_to_all.15.came = f32[4,64,1024]{2,1,0:T(8,128)S(1)} all-to-all(f32[4,64,1024]{2,1,0:T(8,128)} %pack.1), channel_id=1, replica_groups=mesh['ep'=128,'half'=2,'slot'=2] {'half','slot'}, dimensions={0} | all-to-all | bytes 2097152 | tf_op jit(solution)/shard_map/all_to_all | solution.py:224
  17.3 1.4 %slot_grads.1.after = f32[1536,128]{1,0:T(8,128)} custom-call(f32[4,64,1024]{2,1,0:T(8,128)S(1)} %all_to_all.15.came), custom_call_target="tpu_custom_call" | custom-call | flops 301989888 | bytes 4194304 | tf_op jit(solution)/shard_map/slot_grads/pallas_call | solution.py:235
  18.7 0.0 copy-start.2
  18.7 25.7 %all-to-all-start.1 = ((f32[256,1,768]{2,1,0:T(1,128)}), f32[256,1,768]{2,1,0:T(1,128)}, u32[]{:S(2)}, u32[]{:S(2)}) async-start(f32[256,1,768]{2,1,0:T(1,128)} %bitcast.3), calls=%async_computation.1 | async-start | bytes 1572864 | tf_op jit(solution)/shard_map/all_to_all | solution.py:224
  44.5 0.0 copy-done.2
  44.5 4.0 %collective-permute-start = (f32[768,128]{1,0:T(8,128)S(1)}, f32[768,128]{1,0:T(8,128)S(1)}, u32[]{:S(2)}, u32[]{:S(2)}) collective-permute-start(f32[768,128]{1,0:T(8,128)S(1)} %swap.1), channel_id=1, source_target_pairs={{0,1},{1,0},{2,3},{3,2},{4,5},{5,4},{6,7},{7,6},{8,9},{9,8},{10,11... | collective-permute-start | bytes 1179656 | tf_op jit(solution)/shard_map/ppermute | solution.py:241
  48.6 14.7 %collective-permute-done.other = f32[768,128]{1,0:T(8,128)S(1)} collective-permute-done((f32[768,128]{1,0:T(8,128)S(1)}, f32[768,128]{1,0:T(8,128)S(1)}, u32[]{:S(2)}, u32[]{:S(2)}) %collective-permute-start) | collective-permute-done | bytes 393248 | tf_op jit(solution)/shard_map/ppermute | solution.py:241
  63.4 0.9 products.1
  64.3 0.0 copy-start
  64.3 0.7 copy-done
  65.0 4.6 %all-to-all-done.1 = f32[256,1,768]{2,1,0:T(1,128)} async-done(((f32[256,1,768]{2,1,0:T(1,128)}), f32[256,1,768]{2,1,0:T(1,128)}, u32[]{:S(2)}, u32[]{:S(2)}) %all-to-all-start.1) | async-done | bytes 786464 | tf_op jit(solution)/shard_map/all_to_all | solution.py:224
  69.6 4.1 %adamw.1 = (f32[6,128,128]{2,1,0:T(8,128)}, f32[6,128,128]{2,1,0:T(8,128)}, f32[6,128,128]{2,1,0:T(8,128)}, f32[1536,128]{1,0:T(8,128)}) custom-call(f32[64,1024]{1,0:T(8,128)} %copy-done, f32[1536,128]{1,0:T(8,128)} %bitcast.4.arrived_in, s32[1,256]{1,0:T(1,128)} %bitcast.22, s32[1,256]{1,0:T(1,128)} %bitcast.23, f32[6,128,128]{2,1,0:T(8,128)} %bitcast.19, ...), custom_call_target="tpu_custom_call" | custom-call | flops 301989888 | bytes 4194304 | tf_op jit(solution)/shard_map/adamw/pallas_call | solution.py:254
  73.8 0.0 copy-start.1
  73.8 10.1 %all-to-all-start.2 = ((f32[128,1,1536]{2,1,0:T(1,128)}), f32[128,1,1536]{2,1,0:T(1,128)S(1)}, u32[]{:S(2)}, u32[]{:S(2)}) async-start(f32[128,1,1536]{2,1,0:T(1,128)} %bitcast.18), calls=%async_computation.2 | async-start | bytes 1572864 | tf_op jit(solution)/shard_map/all_to_all | solution.py:224
  83.9 2.2 %collective-permute-start.1 = (f32[64,1024]{1,0:T(8,128)S(1)}, f32[64,1024]{1,0:T(8,128)S(1)}, u32[]{:S(2)}, u32[]{:S(2)}) collective-permute-start(f32[64,1024]{1,0:T(8,128)S(1)} %get-tuple-element.17), channel_id=1, source_target_pairs={{0,1},{1,2},{2,3},{3,0},{4,5},{5,6},{6,7},{7,4},{8,9},{9,10},{10,1... | collective-permute-start | bytes 786440 | tf_op jit(solution)/shard_map/ppermute | solution.py:277
  86.1 0.0 copy-start.3
  86.1 3.7 %collective-permute-start.2 = (f32[64,1024]{1,0:T(8,128)S(1)}, f32[64,1024]{1,0:T(8,128)S(1)}, u32[]{:S(2)}, u32[]{:S(2)}) collective-permute-start(f32[64,1024]{1,0:T(8,128)S(1)} %get-tuple-element.18), channel_id=1, source_target_pairs={{0,2},{1,3},{2,0},{3,1},{4,6},{5,7},{6,4},{7,5},{8,10},{9,11},{10,... | collective-permute-start | bytes 786440 | tf_op jit(solution)/shard_map/ppermute | solution.py:277
  89.8 3.7 %collective-permute-start.3 = (f32[64,1024]{1,0:T(8,128)S(1)}, f32[64,1024]{1,0:T(8,128)S(1)}, u32[]{:S(2)}, u32[]{:S(2)}) collective-permute-start(f32[64,1024]{1,0:T(8,128)S(1)} %get-tuple-element.19), channel_id=1, source_target_pairs={{0,3},{1,0},{2,1},{3,2},{4,7},{5,4},{6,5},{7,6},{8,11},{9,8},{10,9... | collective-permute-start | bytes 786440 | tf_op jit(solution)/shard_map/ppermute | solution.py:277
  93.5 1.0 collective-permute-done.1.refs_1_
  94.5 4.5 %collective-permute-done.2.refs_2_ = f32[64,1024]{1,0:T(8,128)S(1)} collective-permute-done((f32[64,1024]{1,0:T(8,128)S(1)}, f32[64,1024]{1,0:T(8,128)S(1)}, u32[]{:S(2)}, u32[]{:S(2)}) %collective-permute-start.2) | collective-permute-done | bytes 262176 | tf_op jit(solution)/shard_map/ppermute | solution.py:277
  99.0 3.0 %collective-permute-done.3.refs_3_ = f32[64,1024]{1,0:T(8,128)S(1)} collective-permute-done((f32[64,1024]{1,0:T(8,128)S(1)}, f32[64,1024]{1,0:T(8,128)S(1)}, u32[]{:S(2)}, u32[]{:S(2)}) %collective-permute-start.3) | collective-permute-done | bytes 262176 | tf_op jit(solution)/shard_map/ppermute | solution.py:277
  101.9 0.0 copy-done.1
  101.9 0.0 copy-done.3
  101.9 1.5 %combine.1 = (f32[2,64,512]{2,1,0:T(8,128)}, f32[2,64,768]{2,1,0:T(8,128)}) custom-call(s32[1]{0:T(128)} %bitcast.place, s32[2]{0:T(128)S(1)} %bitcast.17, f32[64,1024]{1,0:T(8,128)S(1)} %copy-done.1, f32[64,1024]{1,0:T(8,128)S(1)} %collective-permute-done.1.refs_1_, f32[64,1024]{1,0:T(8,128)S(1)} %collective-permute-done.2.refs_2_, ...), custom_call_target="tpu_custom_call" | custom-call | bytes 4194304 | tf_op jit(solution)/shard_map/combine/pallas_call | solution.py:279
  103.4 5.6 %all-to-all-done.2 = f32[128,1,1536]{2,1,0:T(1,128)S(1)} async-done(((f32[128,1,1536]{2,1,0:T(1,128)}), f32[128,1,1536]{2,1,0:T(1,128)S(1)}, u32[]{:S(2)}, u32[]{:S(2)}) %all-to-all-start.2) | async-done | bytes 786464 | tf_op jit(solution)/shard_map/all_to_all | solution.py:224
  109.0 0.9 new_slots.1
  (1 shorter events, 0.0 us)
Async XLA Ops:
  18.7 25.8 %copy-start.2 = (f32[2,768,128]{2,1,0:T(8,128)S(1)}, f32[2,768,128]{2,1,0:T(8,128)}, u32[]{:S(2)}) copy-start(f32[2,768,128]{2,1,0:T(8,128)} %weights.3) | copy-start | bytes 2359300
  18.7 50.9 %all-to-all-start.1 = ((f32[256,1,768]{2,1,0:T(1,128)}), f32[256,1,768]{2,1,0:T(1,128)}, u32[]{:S(2)}, u32[]{:S(2)}) async-start(f32[256,1,768]{2,1,0:T(1,128)} %bitcast.3), calls=%async_computation.1 | async-start | bytes 1572864 | tf_op jit(solution)/shard_map/all_to_all | solution.py:224
  44.5 18.8 %collective-permute-start = (f32[768,128]{1,0:T(8,128)S(1)}, f32[768,128]{1,0:T(8,128)S(1)}, u32[]{:S(2)}, u32[]{:S(2)}) collective-permute-start(f32[768,128]{1,0:T(8,128)S(1)} %swap.1), channel_id=1, source_target_pairs={{0,1},{1,0},{2,3},{3,2},{4,5},{5,4},{6,7},{7,6},{8,9},{9,8},{10,11... | collective-permute-start | bytes 1179656 | tf_op jit(solution)/shard_map/ppermute | solution.py:241
  64.3 0.7 copy-start
  73.8 28.2 %copy-start.1 = (f32[64,1024]{1,0:T(8,128)S(1)}, f32[64,1024]{1,0:T(8,128)}, u32[]{:S(2)}) copy-start(f32[64,1024]{1,0:T(8,128)} %copy-done) | copy-start | bytes 786436
  73.8 35.2 %all-to-all-start.2 = ((f32[128,1,1536]{2,1,0:T(1,128)}), f32[128,1,1536]{2,1,0:T(1,128)S(1)}, u32[]{:S(2)}, u32[]{:S(2)}) async-start(f32[128,1,1536]{2,1,0:T(1,128)} %bitcast.18), calls=%async_computation.2 | async-start | bytes 1572864 | tf_op jit(solution)/shard_map/all_to_all | solution.py:224
  83.9 10.6 %collective-permute-start.1 = (f32[64,1024]{1,0:T(8,128)S(1)}, f32[64,1024]{1,0:T(8,128)S(1)}, u32[]{:S(2)}, u32[]{:S(2)}) collective-permute-start(f32[64,1024]{1,0:T(8,128)S(1)} %get-tuple-element.17), channel_id=1, source_target_pairs={{0,1},{1,2},{2,3},{3,0},{4,5},{5,6},{6,7},{7,4},{8,9},{9,10},{10,1... | collective-permute-start | bytes 786440 | tf_op jit(solution)/shard_map/ppermute | solution.py:277
  86.1 15.9 %copy-start.3 = (s32[2,1]{0,1:T(1,128)S(1)}, s32[2,1]{0,1:T(1,128)}, u32[]{:S(2)}) copy-start(s32[2,1]{0,1:T(1,128)} %param.11) | copy-start | bytes 28
  86.1 12.9 %collective-permute-start.2 = (f32[64,1024]{1,0:T(8,128)S(1)}, f32[64,1024]{1,0:T(8,128)S(1)}, u32[]{:S(2)}, u32[]{:S(2)}) collective-permute-start(f32[64,1024]{1,0:T(8,128)S(1)} %get-tuple-element.18), channel_id=1, source_target_pairs={{0,2},{1,3},{2,0},{3,1},{4,6},{5,7},{6,4},{7,5},{8,10},{9,11},{10,... | collective-permute-start | bytes 786440 | tf_op jit(solution)/shard_map/ppermute | solution.py:277
  89.8 12.1 %collective-permute-start.3 = (f32[64,1024]{1,0:T(8,128)S(1)}, f32[64,1024]{1,0:T(8,128)S(1)}, u32[]{:S(2)}, u32[]{:S(2)}) collective-permute-start(f32[64,1024]{1,0:T(8,128)S(1)} %get-tuple-element.19), channel_id=1, source_target_pairs={{0,3},{1,0},{2,1},{3,2},{4,7},{5,4},{6,5},{7,6},{8,11},{9,8},{10,9... | collective-permute-start | bytes 786440 | tf_op jit(solution)/shard_map/ppermute | solution.py:277

commit v5 on v4

--- a/solution.py
+++ b/solution.py
@@ -70,7 +70,7 @@
     out[...] = weights[1 - slot[0]]
 
 
-def product_kernel(place, weights, other, came, *refs):
+def product_kernel(after, place, weights, other, came, *refs):
     outs, whole = refs[:-1], refs[-1]
     n, rows, _ = came.shape
     ff = weights.shape[1]
@@ -106,9 +106,9 @@
         out[s] = rows[pl.ds(s, ff, stride=slots), :]
 
 
-def adamw_kernel(after, arrived_in, old_table, new_table, master_in, one_in, two_in,
+def adamw_kernel(after, arrived_in, old_in, new_in, master_in, one_in, two_in,
                  master_out, one_out, two_out, send_out,
-                 arrived, master, moment_one, moment_two, new_master, new_one, new_two, send, landed, left):
+                 arrived, old_table, new_table, master, moment_one, moment_two, new_master, new_one, new_two, send, landed, left):
     def moves(pairs, signals, first=0):
         return [pltpu.make_async_copy(a, b, signals.at[first + i]) for i, (a, b) in enumerate(pairs)]
 
@@ -116,9 +116,10 @@
         part = a.shape[0] // PIECES
         return [(a.at[pl.ds(i * part, part)], b.at[pl.ds(i * part, part)]) for i in range(PIECES)]
 
+    tables = moves([(old_in, old_table), (new_in, new_table)], landed, PIECES + 3)
     early = moves(split(arrived_in, arrived), landed)
     later = moves([(master_in, master), (one_in, moment_one), (two_in, moment_two)], landed, PIECES)
-    for copy in early + later:
+    for copy in tables + early + later:
         copy.start()
     rows, experts, _ = master.shape
     total = old_table.shape[1]
@@ -135,6 +136,8 @@
         named = dot(named, order, ((1,), (0,)))[:1].astype(jnp.int32)
         return (ids == named).astype(jnp.float32).astype(jnp.bfloat16)
 
+    for copy in tables:
+        copy.wait()
     old = onehot(old_table)
     new = onehot(new_table)
     for copy in early:
@@ -177,6 +180,7 @@
 SMEM = pl.BlockSpec(memory_space=pltpu.SMEM)
 ANY = pl.BlockSpec(memory_space=pl.ANY)
 SOME = 24 * 1024 * 1024
+MUCH = 52 * 1024 * 1024
 MOST = 60 * 1024 * 1024
 
 
@@ -239,32 +243,24 @@
         column_grad, scalar(lax.axis_index("slot")), slot_weights
     )
     other = lax.ppermute(given, "slot", [(0, 1), (1, 0)])
-    parts = kernel(
-        product_kernel,
-        (packet,) * n,
-        [SMEM, VMEM, VMEM, VMEM],
-        "products",
-        flops=2 * work,
-        scratch=[pltpu.VMEM((n * tokens, width), f32)],
-    )(place, slot_weights, other, came)
-
     plane = shape(rows, experts, lanes)
     flat = shape(slots * rows * owners, lanes)
     flip = lambda x: jnp.transpose(x, (1, 0, 2))
     new_master, new_one, new_two, send = kernel(
         adamw_kernel,
         (plane, plane, plane, flat),
-        [ANY, ANY, VMEM, VMEM, ANY, ANY, ANY],
+        [ANY] * 7,
         "adamw",
         flops=work,
-        limit=MOST,
+        limit=MUCH,
         spec=ANY,
         scratch=[pltpu.VMEM(flat.shape, f32)]
+        + [pltpu.VMEM((1, slots * owners), jnp.int32)] * 2
         + [pltpu.VMEM(plane.shape, f32)] * 6
         + [pltpu.VMEM(flat.shape, f32)]
-        + [pltpu.SemaphoreType.DMA((PIECES + 3,))] * 2,
+        + [pltpu.SemaphoreType.DMA((PIECES + 5,))] * 2,
     )(
-        parts[0],
+        other,
         arrived.reshape(flat.shape),
         old_table.T,
         new_table.T,
@@ -273,6 +269,15 @@
         flip(moment_two),
     )
     placed = exchange(send.reshape(owners, 1, slots * rows * lanes), "ep")
+    parts = kernel(
+        product_kernel,
+        (packet,) * n,
+        [ANY, SMEM, VMEM, VMEM, VMEM],
+        "products",
+        flops=2 * work,
+        scratch=[pltpu.VMEM((n * tokens, width), f32)],
+    )(send, place, slot_weights, other, came)
+
     back = [parts[0]] + [
         lax.ppermute(parts[k], dp, [(i, (i + k) % n) for i in range(n)]) for k in range(1, n)
     ]

time: 110 us -> 109 us (level)
  starting transfers between devices: 49.5 us -> 48.1 us
    all_to_all x2, starting transfers between devices: 35.8 us -> 34.4 us  [exchange(): return lax.all_to_all(x, axes, split_axis=0, concat_axis=0, tiled=True)]
where the time goes in v5:
time: 109 us
  starting transfers between devices  48.1 us (44%)
  waiting for transfers between devices  32.9 us (30%)
  blocking collectives  14.6 us (13%)
  Pallas kernels  10.4 us (10%)
  local copies, waits for them, and re-layouts  1.69 us (2%)
    all_to_all x2, starting transfers between devices, exchange(): return lax.all_to_all(x, axes, split_axis=0, concat_axis=0, tiled=True)  34.4 us
    ppermute x1, waiting for transfers between devices, local(): other = lax.ppermute(given, 'slot', [(0, 1), (1, 0)])  14.7 us
    all_to_all x1, blocking collectives, exchange(): return lax.all_to_all(x, axes, split_axis=0, concat_axis=0, tiled=True)  14.6 us
    all_to_all x2, waiting for transfers between devices, exchange(): return lax.all_to_all(x, axes, split_axis=0, concat_axis=0, tiled=True)  9.82 us
    ppermute x3, starting transfers between devices, local(): lax.ppermute(parts[k], dp, [(i, (i + k) % n) for i in range(n)])  9.58 us
    ppermute x3, waiting for transfers between devices, local(): lax.ppermute(parts[k], dp, [(i, (i + k) % n) for i in range(n)])  8.44 us
    ppermute x1, starting transfers between devices, local(): other = lax.ppermute(given, 'slot', [(0, 1), (1, 0)])  4.18 us
    pallas_call x1, Pallas kernels, local(): kernel(adamw_kernel, (plane, plane, plane, flat), [ANY] * 7, 'adamw', flo...  3.49 us
  transfers between devices with their start and end apart: 6, of which 6 were waited for; matrix products, arithmetic and copies ran while one was open for 0% of the time, Pallas kernels for 2%

profile of v5, /device:TPU:1, one launch (start us, length us, event | category | flops | bytes accessed | tf_op | source)
XLA Modules:
  0.0 108.5 jit_solution(557376468745150718)
XLA Ops:
  0.6 2.1 %pack.1 = f32[4,64,1024]{2,1,0:T(8,128)} custom-call(s32[2]{0:T(128)} %bitcast.20, f32[2,64,768]{2,1,0:T(8,128)} %acts.1, f32[2,64,512]{2,1,0:T(8,128)} %grads.1), custom_call_target="tpu_custom_call" | custom-call | bytes 4194304 | tf_op jit(solution)/shard_map/pack/pallas_call | solution.py:235
  2.8 14.6 %all_to_all.15.came = f32[4,64,1024]{2,1,0:T(8,128)S(1)} all-to-all(f32[4,64,1024]{2,1,0:T(8,128)} %pack.1), channel_id=1, replica_groups=mesh['ep'=128,'half'=2,'slot'=2] {'half','slot'}, dimensions={0} | all-to-all | bytes 2097152 | tf_op jit(solution)/shard_map/all_to_all | solution.py:228
  17.4 1.4 %slot_grads.1.after = f32[1536,128]{1,0:T(8,128)} custom-call(f32[4,64,1024]{2,1,0:T(8,128)S(1)} %all_to_all.15.came), custom_call_target="tpu_custom_call" | custom-call | flops 301989888 | bytes 4194304 | tf_op jit(solution)/shard_map/slot_grads/pallas_call | solution.py:239
  18.8 0.0 copy-start
  18.8 25.7 %all-to-all-start.1 = ((f32[256,1,768]{2,1,0:T(1,128)}), f32[256,1,768]{2,1,0:T(1,128)}, u32[]{:S(2)}, u32[]{:S(2)}) async-start(f32[256,1,768]{2,1,0:T(1,128)} %bitcast.3), calls=%async_computation.1 | async-start | bytes 1572864 | tf_op jit(solution)/shard_map/all_to_all | solution.py:228
  44.5 0.0 copy-done
  44.5 0.0 copy-start.4
  44.5 0.0 copy-start.5
  44.5 0.0 copy-start.6
  44.6 0.0 copy-start.9
  44.6 4.2 %collective-permute-start = (f32[768,128]{1,0:T(8,128)S(1)}, f32[768,128]{1,0:T(8,128)S(1)}, u32[]{:S(2)}, u32[]{:S(2)}) collective-permute-start(f32[768,128]{1,0:T(8,128)S(1)} %swap.1), channel_id=1, source_target_pairs={{0,1},{1,0},{2,3},{3,2},{4,5},{5,4},{6,7},{7,6},{8,9},{9,8},{10,11... | collective-permute-start | bytes 1179656 | tf_op jit(solution)/shard_map/ppermute | solution.py:245
  48.8 14.7 %collective-permute-done.after.other = f32[768,128]{1,0:T(8,128)S(1)} collective-permute-done((f32[768,128]{1,0:T(8,128)S(1)}, f32[768,128]{1,0:T(8,128)S(1)}, u32[]{:S(2)}, u32[]{:S(2)}) %collective-permute-start) | collective-permute-done | bytes 393248 | tf_op jit(solution)/shard_map/ppermute | solution.py:245
  63.4 0.0 copy-start.2
  63.5 6.2 %all-to-all-done.1 = f32[256,1,768]{2,1,0:T(1,128)} async-done(((f32[256,1,768]{2,1,0:T(1,128)}), f32[256,1,768]{2,1,0:T(1,128)}, u32[]{:S(2)}, u32[]{:S(2)}) %all-to-all-start.1) | async-done | bytes 786464 | tf_op jit(solution)/shard_map/all_to_all | solution.py:228
  69.6 0.0 copy-start.8
  69.6 0.0 copy-done.4
  69.6 0.0 copy-done.5
  69.6 0.0 copy-done.6
  69.6 0.0 copy-done.9
  69.6 0.7 copy-done.8
  70.3 3.5 %adamw.1 = (f32[6,128,128]{2,1,0:T(8,128)}, f32[6,128,128]{2,1,0:T(8,128)}, f32[6,128,128]{2,1,0:T(8,128)}, f32[1536,128]{1,0:T(8,128)}) custom-call(f32[768,128]{1,0:T(8,128)S(1)} %collective-permute-done.after.other, f32[1536,128]{1,0:T(8,128)} %bitcast.4.arrived_in, s32[1,256]{1,0:T(1,128)S(1)} %bitcast.22, s32[1,256]{1,0:T(1,128)S(1)} %bitcast.23, ...), custom_call_target="tpu_custom_call" | custom-call | flops 301989888 | bytes 4194304 | tf_op jit(solution)/shard_map/adamw/pallas_call | solution.py:249
  73.8 0.0 copy-done.2
  73.8 0.0 copy-start.1
  73.8 8.6 %all-to-all-start.2 = ((f32[128,1,1536]{2,1,0:T(1,128)}), f32[128,1,1536]{2,1,0:T(1,128)S(1)}, u32[]{:S(2)}, u32[]{:S(2)}) async-start(f32[128,1,1536]{2,1,0:T(1,128)} %bitcast.16), calls=%async_computation.2 | async-start | bytes 1572864 | tf_op jit(solution)/shard_map/all_to_all | solution.py:228
  82.5 0.0 copy-done.1
  82.5 0.0 copy-start.3
  82.5 1.0 copy-done.3
  83.5 0.9 products.1
  84.4 2.2 %collective-permute-start.1 = (f32[64,1024]{1,0:T(8,128)S(1)}, f32[64,1024]{1,0:T(8,128)S(1)}, u32[]{:S(2)}, u32[]{:S(2)}) collective-permute-start(f32[64,1024]{1,0:T(8,128)S(1)} %get-tuple-element.18), channel_id=1, source_target_pairs={{0,1},{1,2},{2,3},{3,0},{4,5},{5,6},{6,7},{7,4},{8,9},{9,10},{10,1... | collective-permute-start | bytes 786440 | tf_op jit(solution)/shard_map/ppermute | solution.py:282
  86.6 3.7 %collective-permute-start.2 = (f32[64,1024]{1,0:T(8,128)S(1)}, f32[64,1024]{1,0:T(8,128)S(1)}, u32[]{:S(2)}, u32[]{:S(2)}) collective-permute-start(f32[64,1024]{1,0:T(8,128)S(1)} %get-tuple-element.19), channel_id=1, source_target_pairs={{0,2},{1,3},{2,0},{3,1},{4,6},{5,7},{6,4},{7,5},{8,10},{9,11},{10,... | collective-permute-start | bytes 786440 | tf_op jit(solution)/shard_map/ppermute | solution.py:282
  90.3 0.0 copy-start.7
  90.3 3.7 %collective-permute-start.3 = (f32[64,1024]{1,0:T(8,128)S(1)}, f32[64,1024]{1,0:T(8,128)S(1)}, u32[]{:S(2)}, u32[]{:S(2)}) collective-permute-start(f32[64,1024]{1,0:T(8,128)S(1)} %get-tuple-element.20), channel_id=1, source_target_pairs={{0,3},{1,0},{2,1},{3,2},{4,7},{5,4},{6,5},{7,6},{8,11},{9,8},{10,9... | collective-permute-start | bytes 786440 | tf_op jit(solution)/shard_map/ppermute | solution.py:282
  94.0 1.0 collective-permute-done.1.refs_1_
  95.0 4.5 %collective-permute-done.2.refs_2_ = f32[64,1024]{1,0:T(8,128)S(1)} collective-permute-done((f32[64,1024]{1,0:T(8,128)S(1)}, f32[64,1024]{1,0:T(8,128)S(1)}, u32[]{:S(2)}, u32[]{:S(2)}) %collective-permute-start.2) | collective-permute-done | bytes 262176 | tf_op jit(solution)/shard_map/ppermute | solution.py:282
  99.5 3.0 %collective-permute-done.3.refs_3_ = f32[64,1024]{1,0:T(8,128)S(1)} collective-permute-done((f32[64,1024]{1,0:T(8,128)S(1)}, f32[64,1024]{1,0:T(8,128)S(1)}, u32[]{:S(2)}, u32[]{:S(2)}) %collective-permute-start.3) | collective-permute-done | bytes 262176 | tf_op jit(solution)/shard_map/ppermute | solution.py:282
  102.4 0.0 copy-done.7
  102.4 1.5 %combine.1 = (f32[2,64,512]{2,1,0:T(8,128)}, f32[2,64,768]{2,1,0:T(8,128)}) custom-call(s32[1]{0:T(128)} %bitcast.place, s32[2]{0:T(128)S(1)} %bitcast.21, f32[64,1024]{1,0:T(8,128)S(1)} %get-tuple-element.17.refs_0_, f32[64,1024]{1,0:T(8,128)S(1)} %collective-permute-done.1.refs_1_, f32[64,1024]{1,0:T(8,128)S(1)} %collective-permute-done.2.refs_2_, ...), custom_call_target="tpu_custom_call" | custom-call | bytes 4194304 | tf_op jit(solution)/shard_map/combine/pallas_call | solution.py:284
  103.9 3.7 %all-to-all-done.2 = f32[128,1,1536]{2,1,0:T(1,128)S(1)} async-done(((f32[128,1,1536]{2,1,0:T(1,128)}), f32[128,1,1536]{2,1,0:T(1,128)S(1)}, u32[]{:S(2)}, u32[]{:S(2)}) %all-to-all-start.2) | async-done | bytes 786464 | tf_op jit(solution)/shard_map/all_to_all | solution.py:228
  107.6 0.9 new_slots.1
  (1 shorter events, 0.0 us)
Async XLA Ops:
  18.8 25.8 %copy-start = (f32[2,768,128]{2,1,0:T(8,128)S(1)}, f32[2,768,128]{2,1,0:T(8,128)}, u32[]{:S(2)}) copy-start(f32[2,768,128]{2,1,0:T(8,128)} %weights.3) | copy-start | bytes 2359300
  18.8 50.8 %all-to-all-start.1 = ((f32[256,1,768]{2,1,0:T(1,128)}), f32[256,1,768]{2,1,0:T(1,128)}, u32[]{:S(2)}, u32[]{:S(2)}) async-start(f32[256,1,768]{2,1,0:T(1,128)} %bitcast.3), calls=%async_computation.1 | async-start | bytes 1572864 | tf_op jit(solution)/shard_map/all_to_all | solution.py:228
  44.5 25.1 %copy-start.4 = (f32[128,6,128]{2,0,1:T(8,128)S(1)}, f32[128,6,128]{2,0,1:T(8,128)}, u32[]{:S(2)}) copy-start(f32[128,6,128]{2,0,1:T(8,128)} %param.13) | copy-start | bytes 1179652
  44.5 25.1 %copy-start.5 = (f32[128,6,128]{2,0,1:T(8,128)S(1)}, f32[128,6,128]{2,0,1:T(8,128)}, u32[]{:S(2)}) copy-start(f32[128,6,128]{2,0,1:T(8,128)} %param.14) | copy-start | bytes 1179652
  44.5 25.1 %copy-start.6 = (f32[128,6,128]{2,0,1:T(8,128)S(1)}, f32[128,6,128]{2,0,1:T(8,128)}, u32[]{:S(2)}) copy-start(f32[128,6,128]{2,0,1:T(8,128)} %param.15) | copy-start | bytes 1179652
  44.6 25.1 %copy-start.9 = (s32[256,1]{0,1:T(1,128)S(1)}, s32[256,1]{0,1:T(1,128)}, u32[]{:S(2)}) copy-start(s32[256,1]{0,1:T(1,128)} %param.17) | copy-start | bytes 3076
  44.6 18.8 %collective-permute-start = (f32[768,128]{1,0:T(8,128)S(1)}, f32[768,128]{1,0:T(8,128)S(1)}, u32[]{:S(2)}, u32[]{:S(2)}) collective-permute-start(f32[768,128]{1,0:T(8,128)S(1)} %swap.1), channel_id=1, source_target_pairs={{0,1},{1,0},{2,3},{3,2},{4,5},{5,4},{6,7},{7,6},{8,9},{9,8},{10,11... | collective-permute-start | bytes 1179656 | tf_op jit(solution)/shard_map/ppermute | solution.py:245
  63.4 10.3 %copy-start.2 = (f32[768,128]{1,0:T(8,128)}, f32[768,128]{1,0:T(8,128)S(1)}, u32[]{:S(2)}) copy-start(f32[768,128]{1,0:T(8,128)S(1)} %collective-permute-done.after.other) | copy-start | bytes 1179652
  69.6 0.7 copy-start.8
  73.8 8.7 %copy-start.1 = (f32[1536,128]{1,0:T(8,128)S(1)}, f32[1536,128]{1,0:T(8,128)}, u32[]{:S(2)}) copy-start(f32[1536,128]{1,0:T(8,128)} %get-tuple-element.16.after) | copy-start | bytes 2359300
  73.8 33.8 %all-to-all-start.2 = ((f32[128,1,1536]{2,1,0:T(1,128)}), f32[128,1,1536]{2,1,0:T(1,128)S(1)}, u32[]{:S(2)}, u32[]{:S(2)}) async-start(f32[128,1,1536]{2,1,0:T(1,128)} %bitcast.16), calls=%async_computation.2 | async-start | bytes 1572864 | tf_op jit(solution)/shard_map/all_to_all | solution.py:228
  82.5 1.0 copy-start.3
  84.4 10.6 %collective-permute-start.1 = (f32[64,1024]{1,0:T(8,128)S(1)}, f32[64,1024]{1,0:T(8,128)S(1)}, u32[]{:S(2)}, u32[]{:S(2)}) collective-permute-start(f32[64,1024]{1,0:T(8,128)S(1)} %get-tuple-element.18), channel_id=1, source_target_pairs={{0,1},{1,2},{2,3},{3,0},{4,5},{5,6},{6,7},{7,4},{8,9},{9,10},{10,1... | collective-permute-start | bytes 786440 | tf_op jit(solution)/shard_map/ppermute | solution.py:282
  86.6 12.9 %collective-permute-start.2 = (f32[64,1024]{1,0:T(8,128)S(1)}, f32[64,1024]{1,0:T(8,128)S(1)}, u32[]{:S(2)}, u32[]{:S(2)}) collective-permute-start(f32[64,1024]{1,0:T(8,128)S(1)} %get-tuple-element.19), channel_id=1, source_target_pairs={{0,2},{1,3},{2,0},{3,1},{4,6},{5,7},{6,4},{7,5},{8,10},{9,11},{10,... | collective-permute-start | bytes 786440 | tf_op jit(solution)/shard_map/ppermute | solution.py:282
  90.3 12.2 %copy-start.7 = (s32[2,1]{0,1:T(1,128)S(1)}, s32[2,1]{0,1:T(1,128)}, u32[]{:S(2)}) copy-start(s32[2,1]{0,1:T(1,128)} %param.11) | copy-start | bytes 28
  90.3 12.1 %collective-permute-start.3 = (f32[64,1024]{1,0:T(8,128)S(1)}, f32[64,1024]{1,0:T(8,128)S(1)}, u32[]{:S(2)}, u32[]{:S(2)}) collective-permute-start(f32[64,1024]{1,0:T(8,128)S(1)} %get-tuple-element.20), channel_id=1, source_target_pairs={{0,3},{1,0},{2,1},{3,2},{4,7},{5,4},{6,5},{7,6},{8,11},{9,8},{10,9... | collective-permute-start | bytes 786440 | tf_op jit(solution)/shard_map/ppermute | solution.py:282

commit v6 on v4

--- a/solution.py
+++ b/solution.py
@@ -106,9 +106,9 @@
         out[s] = rows[pl.ds(s, ff, stride=slots), :]
 
 
-def adamw_kernel(after, arrived_in, old_table, new_table, master_in, one_in, two_in,
+def adamw_kernel(after, arrived_in, old_in, new_in, master_in, one_in, two_in,
                  master_out, one_out, two_out, send_out,
-                 arrived, master, moment_one, moment_two, new_master, new_one, new_two, send, landed, left):
+                 arrived, old_table, new_table, master, moment_one, moment_two, new_master, new_one, new_two, send, landed, left):
     def moves(pairs, signals, first=0):
         return [pltpu.make_async_copy(a, b, signals.at[first + i]) for i, (a, b) in enumerate(pairs)]
 
@@ -116,9 +116,10 @@
         part = a.shape[0] // PIECES
         return [(a.at[pl.ds(i * part, part)], b.at[pl.ds(i * part, part)]) for i in range(PIECES)]
 
+    tables = moves([(old_in, old_table), (new_in, new_table)], landed, PIECES + 3)
     early = moves(split(arrived_in, arrived), landed)
     later = moves([(master_in, master), (one_in, moment_one), (two_in, moment_two)], landed, PIECES)
-    for copy in early + later:
+    for copy in tables + early + later:
         copy.start()
     rows, experts, _ = master.shape
     total = old_table.shape[1]
@@ -135,6 +136,8 @@
         named = dot(named, order, ((1,), (0,)))[:1].astype(jnp.int32)
         return (ids == named).astype(jnp.float32).astype(jnp.bfloat16)
 
+    for copy in tables:
+        copy.wait()
     old = onehot(old_table)
     new = onehot(new_table)
     for copy in early:
@@ -254,15 +257,16 @@
     new_master, new_one, new_two, send = kernel(
         adamw_kernel,
         (plane, plane, plane, flat),
-        [ANY, ANY, VMEM, VMEM, ANY, ANY, ANY],
+        [ANY] * 7,
         "adamw",
         flops=work,
         limit=MOST,
         spec=ANY,
         scratch=[pltpu.VMEM(flat.shape, f32)]
+        + [pltpu.VMEM((1, slots * owners), jnp.int32)] * 2
         + [pltpu.VMEM(plane.shape, f32)] * 6
         + [pltpu.VMEM(flat.shape, f32)]
-        + [pltpu.SemaphoreType.DMA((PIECES + 3,))] * 2,
+        + [pltpu.SemaphoreType.DMA((PIECES + 5,))] * 2,
     )(
         parts[0],
         arrived.reshape(flat.shape),

time: 110 us -> 110 us (level)
  no operation moved by 1% of the time
where the time goes in v6:
time: 110 us; the launch traced here: 109 us
  starting transfers between devices  49.5 us (45%)
  waiting for transfers between devices  33.4 us (30%)
  blocking collectives  14.6 us (13%)
  Pallas kernels  10.4 us (9%)
    all_to_all x2, starting transfers between devices, exchange(): return lax.all_to_all(x, axes, split_axis=0, concat_axis=0, tiled=True)  35.8 us
    ppermute x1, waiting for transfers between devices, local(): other = lax.ppermute(given, 'slot', [(0, 1), (1, 0)])  14.7 us
    all_to_all x1, blocking collectives, exchange(): return lax.all_to_all(x, axes, split_axis=0, concat_axis=0, tiled=True)  14.6 us
    all_to_all x2, waiting for transfers between devices, exchange(): return lax.all_to_all(x, axes, split_axis=0, concat_axis=0, tiled=True)  10.2 us
    ppermute x3, starting transfers between devices, local(): lax.ppermute(parts[k], dp, [(i, (i + k) % n) for i in range(n)])  9.58 us
    ppermute x3, waiting for transfers between devices, local(): lax.ppermute(parts[k], dp, [(i, (i + k) % n) for i in range(n)])  8.45 us
    ppermute x1, starting transfers between devices, local(): other = lax.ppermute(given, 'slot', [(0, 1), (1, 0)])  4.05 us
    pallas_call x1, Pallas kernels, local(): kernel(adamw_kernel, (plane, plane, plane, flat), [ANY] * 7, 'adamw', flo...  3.51 us
  transfers between devices with their start and end apart: 6, of which 6 were waited for; matrix products, arithmetic and copies ran while one was open for 0% of the time, Pallas kernels for 2%

profile of v6, /device:TPU:1, one launch (start us, length us, event | category | flops | bytes accessed | tf_op | source)
XLA Modules:
  0.0 109.3 jit_solution(5088743205488328265)
XLA Ops:
  0.6 2.1 %pack.1 = f32[4,64,1024]{2,1,0:T(8,128)} custom-call(s32[2]{0:T(128)} %bitcast.16, f32[2,64,768]{2,1,0:T(8,128)} %acts.1, f32[2,64,512]{2,1,0:T(8,128)} %grads.1), custom_call_target="tpu_custom_call" | custom-call | bytes 4194304 | tf_op jit(solution)/shard_map/pack/pallas_call | solution.py:234
  2.8 14.6 %all_to_all.15.came = f32[4,64,1024]{2,1,0:T(8,128)S(1)} all-to-all(f32[4,64,1024]{2,1,0:T(8,128)} %pack.1), channel_id=1, replica_groups=mesh['ep'=128,'half'=2,'slot'=2] {'half','slot'}, dimensions={0} | all-to-all | bytes 2097152 | tf_op jit(solution)/shard_map/all_to_all | solution.py:227
  17.3 1.4 %slot_grads.1.after = f32[1536,128]{1,0:T(8,128)} custom-call(f32[4,64,1024]{2,1,0:T(8,128)S(1)} %all_to_all.15.came), custom_call_target="tpu_custom_call" | custom-call | flops 301989888 | bytes 4194304 | tf_op jit(solution)/shard_map/slot_grads/pallas_call | solution.py:238
  18.7 0.0 copy-start.2
  18.7 25.7 %all-to-all-start.1 = ((f32[256,1,768]{2,1,0:T(1,128)}), f32[256,1,768]{2,1,0:T(1,128)}, u32[]{:S(2)}, u32[]{:S(2)}) async-start(f32[256,1,768]{2,1,0:T(1,128)} %bitcast.3), calls=%async_computation.1 | async-start | bytes 1572864 | tf_op jit(solution)/shard_map/all_to_all | solution.py:227
  44.5 0.0 copy-done.2
  44.5 4.0 %collective-permute-start = (f32[768,128]{1,0:T(8,128)S(1)}, f32[768,128]{1,0:T(8,128)S(1)}, u32[]{:S(2)}, u32[]{:S(2)}) collective-permute-start(f32[768,128]{1,0:T(8,128)S(1)} %swap.1), channel_id=1, source_target_pairs={{0,1},{1,0},{2,3},{3,2},{4,5},{5,4},{6,7},{7,6},{8,9},{9,8},{10,11... | collective-permute-start | bytes 1179656 | tf_op jit(solution)/shard_map/ppermute | solution.py:244
  48.6 14.7 %collective-permute-done.other = f32[768,128]{1,0:T(8,128)S(1)} collective-permute-done((f32[768,128]{1,0:T(8,128)S(1)}, f32[768,128]{1,0:T(8,128)S(1)}, u32[]{:S(2)}, u32[]{:S(2)}) %collective-permute-start) | collective-permute-done | bytes 393248 | tf_op jit(solution)/shard_map/ppermute | solution.py:244
  63.4 0.9 products.1
  64.3 0.0 copy-start
  64.3 0.7 copy-done
  65.0 4.6 %all-to-all-done.1 = f32[256,1,768]{2,1,0:T(1,128)} async-done(((f32[256,1,768]{2,1,0:T(1,128)}), f32[256,1,768]{2,1,0:T(1,128)}, u32[]{:S(2)}, u32[]{:S(2)}) %all-to-all-start.1) | async-done | bytes 786464 | tf_op jit(solution)/shard_map/all_to_all | solution.py:227
  69.6 3.5 %adamw.1 = (f32[6,128,128]{2,1,0:T(8,128)}, f32[6,128,128]{2,1,0:T(8,128)}, f32[6,128,128]{2,1,0:T(8,128)}, f32[1536,128]{1,0:T(8,128)}) custom-call(f32[64,1024]{1,0:T(8,128)} %copy-done, f32[1536,128]{1,0:T(8,128)} %bitcast.4.arrived_in, s32[1,256]{1,0:T(1,128)} %bitcast.22, s32[1,256]{1,0:T(1,128)} %bitcast.23, f32[6,128,128]{2,1,0:T(8,128)} %bitcast.19, ...), custom_call_target="tpu_custom_call" | custom-call | flops 301989888 | bytes 4194304 | tf_op jit(solution)/shard_map/adamw/pallas_call | solution.py:257
  73.1 0.0 copy-start.1
  73.1 10.1 %all-to-all-start.2 = ((f32[128,1,1536]{2,1,0:T(1,128)}), f32[128,1,1536]{2,1,0:T(1,128)S(1)}, u32[]{:S(2)}, u32[]{:S(2)}) async-start(f32[128,1,1536]{2,1,0:T(1,128)} %bitcast.18), calls=%async_computation.2 | async-start | bytes 1572864 | tf_op jit(solution)/shard_map/all_to_all | solution.py:227
  83.2 2.2 %collective-permute-start.1 = (f32[64,1024]{1,0:T(8,128)S(1)}, f32[64,1024]{1,0:T(8,128)S(1)}, u32[]{:S(2)}, u32[]{:S(2)}) collective-permute-start(f32[64,1024]{1,0:T(8,128)S(1)} %get-tuple-element.17), channel_id=1, source_target_pairs={{0,1},{1,2},{2,3},{3,0},{4,5},{5,6},{6,7},{7,4},{8,9},{9,10},{10,1... | collective-permute-start | bytes 786440 | tf_op jit(solution)/shard_map/ppermute | solution.py:281
  85.4 0.0 copy-start.3
  85.4 3.7 %collective-permute-start.2 = (f32[64,1024]{1,0:T(8,128)S(1)}, f32[64,1024]{1,0:T(8,128)S(1)}, u32[]{:S(2)}, u32[]{:S(2)}) collective-permute-start(f32[64,1024]{1,0:T(8,128)S(1)} %get-tuple-element.18), channel_id=1, source_target_pairs={{0,2},{1,3},{2,0},{3,1},{4,6},{5,7},{6,4},{7,5},{8,10},{9,11},{10,... | collective-permute-start | bytes 786440 | tf_op jit(solution)/shard_map/ppermute | solution.py:281
  89.1 3.7 %collective-permute-start.3 = (f32[64,1024]{1,0:T(8,128)S(1)}, f32[64,1024]{1,0:T(8,128)S(1)}, u32[]{:S(2)}, u32[]{:S(2)}) collective-permute-start(f32[64,1024]{1,0:T(8,128)S(1)} %get-tuple-element.19), channel_id=1, source_target_pairs={{0,3},{1,0},{2,1},{3,2},{4,7},{5,4},{6,5},{7,6},{8,11},{9,8},{10,9... | collective-permute-start | bytes 786440 | tf_op jit(solution)/shard_map/ppermute | solution.py:281
  92.8 1.0 collective-permute-done.1.refs_1_
  93.8 4.5 %collective-permute-done.2.refs_2_ = f32[64,1024]{1,0:T(8,128)S(1)} collective-permute-done((f32[64,1024]{1,0:T(8,128)S(1)}, f32[64,1024]{1,0:T(8,128)S(1)}, u32[]{:S(2)}, u32[]{:S(2)}) %collective-permute-start.2) | collective-permute-done | bytes 262176 | tf_op jit(solution)/shard_map/ppermute | solution.py:281
  98.3 3.0 %collective-permute-done.3.refs_3_ = f32[64,1024]{1,0:T(8,128)S(1)} collective-permute-done((f32[64,1024]{1,0:T(8,128)S(1)}, f32[64,1024]{1,0:T(8,128)S(1)}, u32[]{:S(2)}, u32[]{:S(2)}) %collective-permute-start.3) | collective-permute-done | bytes 262176 | tf_op jit(solution)/shard_map/ppermute | solution.py:281
  101.3 0.0 copy-done.1
  101.3 0.0 copy-done.3
  101.3 1.5 %combine.1 = (f32[2,64,512]{2,1,0:T(8,128)}, f32[2,64,768]{2,1,0:T(8,128)}) custom-call(s32[1]{0:T(128)} %bitcast.place, s32[2]{0:T(128)S(1)} %bitcast.17, f32[64,1024]{1,0:T(8,128)S(1)} %copy-done.1, f32[64,1024]{1,0:T(8,128)S(1)} %collective-permute-done.1.refs_1_, f32[64,1024]{1,0:T(8,128)S(1)} %collective-permute-done.2.refs_2_, ...), custom_call_target="tpu_custom_call" | custom-call | bytes 4194304 | tf_op jit(solution)/shard_map/combine/pallas_call | solution.py:283
  102.8 5.6 %all-to-all-done.2 = f32[128,1,1536]{2,1,0:T(1,128)S(1)} async-done(((f32[128,1,1536]{2,1,0:T(1,128)}), f32[128,1,1536]{2,1,0:T(1,128)S(1)}, u32[]{:S(2)}, u32[]{:S(2)}) %all-to-all-start.2) | async-done | bytes 786464 | tf_op jit(solution)/shard_map/all_to_all | solution.py:227
  108.4 0.9 new_slots.1
  (1 shorter events, 0.0 us)
Async XLA Ops:
  18.7 25.8 %copy-start.2 = (f32[2,768,128]{2,1,0:T(8,128)S(1)}, f32[2,768,128]{2,1,0:T(8,128)}, u32[]{:S(2)}) copy-start(f32[2,768,128]{2,1,0:T(8,128)} %weights.3) | copy-start | bytes 2359300
  18.7 50.9 %all-to-all-start.1 = ((f32[256,1,768]{2,1,0:T(1,128)}), f32[256,1,768]{2,1,0:T(1,128)}, u32[]{:S(2)}, u32[]{:S(2)}) async-start(f32[256,1,768]{2,1,0:T(1,128)} %bitcast.3), calls=%async_computation.1 | async-start | bytes 1572864 | tf_op jit(solution)/shard_map/all_to_all | solution.py:227
  44.5 18.8 %collective-permute-start = (f32[768,128]{1,0:T(8,128)S(1)}, f32[768,128]{1,0:T(8,128)S(1)}, u32[]{:S(2)}, u32[]{:S(2)}) collective-permute-start(f32[768,128]{1,0:T(8,128)S(1)} %swap.1), channel_id=1, source_target_pairs={{0,1},{1,0},{2,3},{3,2},{4,5},{5,4},{6,7},{7,6},{8,9},{9,8},{10,11... | collective-permute-start | bytes 1179656 | tf_op jit(solution)/shard_map/ppermute | solution.py:244
  64.3 0.7 copy-start
  73.1 28.2 %copy-start.1 = (f32[64,1024]{1,0:T(8,128)S(1)}, f32[64,1024]{1,0:T(8,128)}, u32[]{:S(2)}) copy-start(f32[64,1024]{1,0:T(8,128)} %copy-done) | copy-start | bytes 786436
  73.1 35.2 %all-to-all-start.2 = ((f32[128,1,1536]{2,1,0:T(1,128)}), f32[128,1,1536]{2,1,0:T(1,128)S(1)}, u32[]{:S(2)}, u32[]{:S(2)}) async-start(f32[128,1,1536]{2,1,0:T(1,128)} %bitcast.18), calls=%async_computation.2 | async-start | bytes 1572864 | tf_op jit(solution)/shard_map/all_to_all | solution.py:227
  83.2 10.6 %collective-permute-start.1 = (f32[64,1024]{1,0:T(8,128)S(1)}, f32[64,1024]{1,0:T(8,128)S(1)}, u32[]{:S(2)}, u32[]{:S(2)}) collective-permute-start(f32[64,1024]{1,0:T(8,128)S(1)} %get-tuple-element.17), channel_id=1, source_target_pairs={{0,1},{1,2},{2,3},{3,0},{4,5},{5,6},{6,7},{7,4},{8,9},{9,10},{10,1... | collective-permute-start | bytes 786440 | tf_op jit(solution)/shard_map/ppermute | solution.py:281
  85.4 15.9 %copy-start.3 = (s32[2,1]{0,1:T(1,128)S(1)}, s32[2,1]{0,1:T(1,128)}, u32[]{:S(2)}) copy-start(s32[2,1]{0,1:T(1,128)} %param.11) | copy-start | bytes 28
  85.4 12.9 %collective-permute-start.2 = (f32[64,1024]{1,0:T(8,128)S(1)}, f32[64,1024]{1,0:T(8,128)S(1)}, u32[]{:S(2)}, u32[]{:S(2)}) collective-permute-start(f32[64,1024]{1,0:T(8,128)S(1)} %get-tuple-element.18), channel_id=1, source_target_pairs={{0,2},{1,3},{2,0},{3,1},{4,6},{5,7},{6,4},{7,5},{8,10},{9,11},{10,... | collective-permute-start | bytes 786440 | tf_op jit(solution)/shard_map/ppermute | solution.py:281
  89.1 12.1 %collective-permute-start.3 = (f32[64,1024]{1,0:T(8,128)S(1)}, f32[64,1024]{1,0:T(8,128)S(1)}, u32[]{:S(2)}, u32[]{:S(2)}) collective-permute-start(f32[64,1024]{1,0:T(8,128)S(1)} %get-tuple-element.19), channel_id=1, source_target_pairs={{0,3},{1,0},{2,1},{3,2},{4,7},{5,4},{6,5},{7,6},{8,11},{9,8},{10,9... | collective-permute-start | bytes 786440 | tf_op jit(solution)/shard_map/ppermute | solution.py:281

commit v7 on v6

--- a/solution.py
+++ b/solution.py
@@ -71,7 +71,8 @@
 
 
 def product_kernel(place, weights, other, came, *refs):
-    outs, whole = refs[:-1], refs[-1]
+    outs, done, whole = refs[:-2], refs[-2], refs[-1]
+    done[...] = jnp.zeros_like(done)
     n, rows, _ = came.shape
     ff = weights.shape[1]
     slot = lax.rem(place[0], 2)
@@ -242,9 +243,9 @@
         column_grad, scalar(lax.axis_index("slot")), slot_weights
     )
     other = lax.ppermute(given, "slot", [(0, 1), (1, 0)])
-    parts = kernel(
+    *parts, done = kernel(
         product_kernel,
-        (packet,) * n,
+        (packet,) * n + (shape(8, lanes),),
         [SMEM, VMEM, VMEM, VMEM],
         "products",
         flops=2 * work,
@@ -268,7 +269,7 @@
         + [pltpu.VMEM(flat.shape, f32)]
         + [pltpu.SemaphoreType.DMA((PIECES + 5,))] * 2,
     )(
-        parts[0],
+        done,
         arrived.reshape(flat.shape),
         old_table.T,
         new_table.T,

time: 110 us -> 110 us (level)
  no operation moved by 1% of the time
where the time goes in v7:
time: 110 us; the launch traced here: 109 us
  starting transfers between devices  49.2 us (45%)
  waiting for transfers between devices  33.5 us (30%)
  blocking collectives  14.6 us (13%)
  Pallas kernels  10.4 us (9%)
    all_to_all x2, starting transfers between devices, exchange(): return lax.all_to_all(x, axes, split_axis=0, concat_axis=0, tiled=True)  35.6 us
    ppermute x1, waiting for transfers between devices, local(): other = lax.ppermute(given, 'slot', [(0, 1), (1, 0)])  14.7 us
    all_to_all x1, blocking collectives, exchange(): return lax.all_to_all(x, axes, split_axis=0, concat_axis=0, tiled=True)  14.6 us
    all_to_all x2, waiting for transfers between devices, exchange(): return lax.all_to_all(x, axes, split_axis=0, concat_axis=0, tiled=True)  10.3 us
    ppermute x3, starting transfers between devices, local(): lax.ppermute(parts[k], dp, [(i, (i + k) % n) for i in range(n)])  9.59 us
    ppermute x3, waiting for transfers between devices, local(): lax.ppermute(parts[k], dp, [(i, (i + k) % n) for i in range(n)])  8.42 us
    ppermute x1, starting transfers between devices, local(): other = lax.ppermute(given, 'slot', [(0, 1), (1, 0)])  4.05 us
    pallas_call x1, Pallas kernels, local(): kernel(adamw_kernel, (plane, plane, plane, flat), [ANY] * 7, 'adamw', flo...  3.51 us
  transfers between devices with their start and end apart: 6, of which 6 were waited for; matrix products, arithmetic and copies ran while one was open for 0% of the time, Pallas kernels for 2%

profile of v7, /device:TPU:1, one launch (start us, length us, event | category | flops | bytes accessed | tf_op | source)
XLA Modules:
  0.0 109.0 jit_solution(9259269982083674099)
XLA Ops:
  0.6 2.1 %pack.1 = f32[4,64,1024]{2,1,0:T(8,128)} custom-call(s32[2]{0:T(128)} %bitcast.16, f32[2,64,768]{2,1,0:T(8,128)} %acts.1, f32[2,64,512]{2,1,0:T(8,128)} %grads.1), custom_call_target="tpu_custom_call" | custom-call | bytes 4194304 | tf_op jit(solution)/shard_map/pack/pallas_call | solution.py:235
  2.8 14.6 %all_to_all.15.came = f32[4,64,1024]{2,1,0:T(8,128)S(1)} all-to-all(f32[4,64,1024]{2,1,0:T(8,128)} %pack.1), channel_id=1, replica_groups=mesh['ep'=128,'half'=2,'slot'=2] {'half','slot'}, dimensions={0} | all-to-all | bytes 2097152 | tf_op jit(solution)/shard_map/all_to_all | solution.py:228
  17.3 1.4 %slot_grads.1.after = f32[1536,128]{1,0:T(8,128)} custom-call(f32[4,64,1024]{2,1,0:T(8,128)S(1)} %all_to_all.15.came), custom_call_target="tpu_custom_call" | custom-call | flops 301989888 | bytes 4194304 | tf_op jit(solution)/shard_map/slot_grads/pallas_call | solution.py:239
  18.7 0.0 copy-start
  18.7 25.7 %all-to-all-start.1 = ((f32[256,1,768]{2,1,0:T(1,128)}), f32[256,1,768]{2,1,0:T(1,128)}, u32[]{:S(2)}, u32[]{:S(2)}) async-start(f32[256,1,768]{2,1,0:T(1,128)} %bitcast.3), calls=%async_computation.1 | async-start | bytes 1572864 | tf_op jit(solution)/shard_map/all_to_all | solution.py:228
  44.5 0.0 copy-done
  44.5 4.0 %collective-permute-start = (f32[768,128]{1,0:T(8,128)S(1)}, f32[768,128]{1,0:T(8,128)S(1)}, u32[]{:S(2)}, u32[]{:S(2)}) collective-permute-start(f32[768,128]{1,0:T(8,128)S(1)} %swap.1), channel_id=1, source_target_pairs={{0,1},{1,0},{2,3},{3,2},{4,5},{5,4},{6,7},{7,6},{8,9},{9,8},{10,11... | collective-permute-start | bytes 1179656 | tf_op jit(solution)/shard_map/ppermute | solution.py:245
  48.6 14.7 %collective-permute-done.other = f32[768,128]{1,0:T(8,128)S(1)} collective-permute-done((f32[768,128]{1,0:T(8,128)S(1)}, f32[768,128]{1,0:T(8,128)S(1)}, u32[]{:S(2)}, u32[]{:S(2)}) %collective-permute-start) | collective-permute-done | bytes 393248 | tf_op jit(solution)/shard_map/ppermute | solution.py:245
  63.3 0.9 products.1
  64.2 0.0 copy-start.1
  64.3 0.6 copy-done.1
  64.8 4.7 %all-to-all-done.1 = f32[256,1,768]{2,1,0:T(1,128)} async-done(((f32[256,1,768]{2,1,0:T(1,128)}), f32[256,1,768]{2,1,0:T(1,128)}, u32[]{:S(2)}, u32[]{:S(2)}) %all-to-all-start.1) | async-done | bytes 786464 | tf_op jit(solution)/shard_map/all_to_all | solution.py:228
  69.6 3.5 %adamw.1 = (f32[6,128,128]{2,1,0:T(8,128)}, f32[6,128,128]{2,1,0:T(8,128)}, f32[6,128,128]{2,1,0:T(8,128)}, f32[1536,128]{1,0:T(8,128)}) custom-call(f32[8,128]{1,0:T(8,128)} %copy-done.1, f32[1536,128]{1,0:T(8,128)} %bitcast.4.arrived_in, s32[1,256]{1,0:T(1,128)} %bitcast.22, s32[1,256]{1,0:T(1,128)} %bitcast.23, f32[6,128,128]{2,1,0:T(8,128)} %bitcast.19, ...), custom_call_target="tpu_custom_call" | custom-call | flops 301989888 | bytes 4194304 | tf_op jit(solution)/shard_map/adamw/pallas_call | solution.py:258
  73.1 9.8 %all-to-all-start.2 = ((f32[128,1,1536]{2,1,0:T(1,128)}), f32[128,1,1536]{2,1,0:T(1,128)S(1)}, u32[]{:S(2)}, u32[]{:S(2)}) async-start(f32[128,1,1536]{2,1,0:T(1,128)} %bitcast.18), calls=%async_computation.2 | async-start | bytes 1572864 | tf_op jit(solution)/shard_map/all_to_all | solution.py:228
  83.0 2.2 %collective-permute-start.1 = (f32[64,1024]{1,0:T(8,128)S(1)}, f32[64,1024]{1,0:T(8,128)S(1)}, u32[]{:S(2)}, u32[]{:S(2)}) collective-permute-start(f32[64,1024]{1,0:T(8,128)S(1)} %get-tuple-element.18), channel_id=1, source_target_pairs={{0,1},{1,2},{2,3},{3,0},{4,5},{5,6},{6,7},{7,4},{8,9},{9,10},{10,1... | collective-permute-start | bytes 786440 | tf_op jit(solution)/shard_map/ppermute | solution.py:282
  85.2 3.7 %collective-permute-start.2 = (f32[64,1024]{1,0:T(8,128)S(1)}, f32[64,1024]{1,0:T(8,128)S(1)}, u32[]{:S(2)}, u32[]{:S(2)}) collective-permute-start(f32[64,1024]{1,0:T(8,128)S(1)} %get-tuple-element.19), channel_id=1, source_target_pairs={{0,2},{1,3},{2,0},{3,1},{4,6},{5,7},{6,4},{7,5},{8,10},{9,11},{10,... | collective-permute-start | bytes 786440 | tf_op jit(solution)/shard_map/ppermute | solution.py:282
  88.9 0.0 copy-start.2
  88.9 3.7 %collective-permute-start.3 = (f32[64,1024]{1,0:T(8,128)S(1)}, f32[64,1024]{1,0:T(8,128)S(1)}, u32[]{:S(2)}, u32[]{:S(2)}) collective-permute-start(f32[64,1024]{1,0:T(8,128)S(1)} %get-tuple-element.20), channel_id=1, source_target_pairs={{0,3},{1,0},{2,1},{3,2},{4,7},{5,4},{6,5},{7,6},{8,11},{9,8},{10,9... | collective-permute-start | bytes 786440 | tf_op jit(solution)/shard_map/ppermute | solution.py:282
  92.6 1.0 collective-permute-done.1.refs_1_
  93.6 4.5 %collective-permute-done.2.refs_2_ = f32[64,1024]{1,0:T(8,128)S(1)} collective-permute-done((f32[64,1024]{1,0:T(8,128)S(1)}, f32[64,1024]{1,0:T(8,128)S(1)}, u32[]{:S(2)}, u32[]{:S(2)}) %collective-permute-start.2) | collective-permute-done | bytes 262176 | tf_op jit(solution)/shard_map/ppermute | solution.py:282
  98.1 2.9 %collective-permute-done.3.refs_3_ = f32[64,1024]{1,0:T(8,128)S(1)} collective-permute-done((f32[64,1024]{1,0:T(8,128)S(1)}, f32[64,1024]{1,0:T(8,128)S(1)}, u32[]{:S(2)}, u32[]{:S(2)}) %collective-permute-start.3) | collective-permute-done | bytes 262176 | tf_op jit(solution)/shard_map/ppermute | solution.py:282
  101.0 0.0 copy-done.2
  101.0 1.5 %combine.1 = (f32[2,64,512]{2,1,0:T(8,128)}, f32[2,64,768]{2,1,0:T(8,128)}) custom-call(s32[1]{0:T(128)} %bitcast.place, s32[2]{0:T(128)S(1)} %bitcast.17, f32[64,1024]{1,0:T(8,128)S(1)} %get-tuple-element.17.refs_0_, f32[64,1024]{1,0:T(8,128)S(1)} %collective-permute-done.1.refs_1_, f32[64,1024]{1,0:T(8,128)S(1)} %collective-permute-done.2.refs_2_, ...), custom_call_target="tpu_custom_call" | custom-call | bytes 4194304 | tf_op jit(solution)/shard_map/combine/pallas_call | solution.py:284
  102.5 5.6 %all-to-all-done.2 = f32[128,1,1536]{2,1,0:T(1,128)S(1)} async-done(((f32[128,1,1536]{2,1,0:T(1,128)}), f32[128,1,1536]{2,1,0:T(1,128)S(1)}, u32[]{:S(2)}, u32[]{:S(2)}) %all-to-all-start.2) | async-done | bytes 786464 | tf_op jit(solution)/shard_map/all_to_all | solution.py:228
  108.1 0.9 new_slots.1
  (1 shorter events, 0.0 us)
Async XLA Ops:
  18.7 25.8 %copy-start = (f32[2,768,128]{2,1,0:T(8,128)S(1)}, f32[2,768,128]{2,1,0:T(8,128)}, u32[]{:S(2)}) copy-start(f32[2,768,128]{2,1,0:T(8,128)} %weights.3) | copy-start | bytes 2359300
  18.7 50.8 %all-to-all-start.1 = ((f32[256,1,768]{2,1,0:T(1,128)}), f32[256,1,768]{2,1,0:T(1,128)}, u32[]{:S(2)}, u32[]{:S(2)}) async-start(f32[256,1,768]{2,1,0:T(1,128)} %bitcast.3), calls=%async_computation.1 | async-start | bytes 1572864 | tf_op jit(solution)/shard_map/all_to_all | solution.py:228
  44.5 18.8 %collective-permute-start = (f32[768,128]{1,0:T(8,128)S(1)}, f32[768,128]{1,0:T(8,128)S(1)}, u32[]{:S(2)}, u32[]{:S(2)}) collective-permute-start(f32[768,128]{1,0:T(8,128)S(1)} %swap.1), channel_id=1, source_target_pairs={{0,1},{1,0},{2,3},{3,2},{4,5},{5,4},{6,7},{7,6},{8,9},{9,8},{10,11... | collective-permute-start | bytes 1179656 | tf_op jit(solution)/shard_map/ppermute | solution.py:245
  64.2 0.6 copy-start.1
  73.1 35.0 %all-to-all-start.2 = ((f32[128,1,1536]{2,1,0:T(1,128)}), f32[128,1,1536]{2,1,0:T(1,128)S(1)}, u32[]{:S(2)}, u32[]{:S(2)}) async-start(f32[128,1,1536]{2,1,0:T(1,128)} %bitcast.18), calls=%async_computation.2 | async-start | bytes 1572864 | tf_op jit(solution)/shard_map/all_to_all | solution.py:228
  83.0 10.6 %collective-permute-start.1 = (f32[64,1024]{1,0:T(8,128)S(1)}, f32[64,1024]{1,0:T(8,128)S(1)}, u32[]{:S(2)}, u32[]{:S(2)}) collective-permute-start(f32[64,1024]{1,0:T(8,128)S(1)} %get-tuple-element.18), channel_id=1, source_target_pairs={{0,1},{1,2},{2,3},{3,0},{4,5},{5,6},{6,7},{7,4},{8,9},{9,10},{10,1... | collective-permute-start | bytes 786440 | tf_op jit(solution)/shard_map/ppermute | solution.py:282
  85.2 12.9 %collective-permute-start.2 = (f32[64,1024]{1,0:T(8,128)S(1)}, f32[64,1024]{1,0:T(8,128)S(1)}, u32[]{:S(2)}, u32[]{:S(2)}) collective-permute-start(f32[64,1024]{1,0:T(8,128)S(1)} %get-tuple-element.19), channel_id=1, source_target_pairs={{0,2},{1,3},{2,0},{3,1},{4,6},{5,7},{6,4},{7,5},{8,10},{9,11},{10,... | collective-permute-start | bytes 786440 | tf_op jit(solution)/shard_map/ppermute | solution.py:282
  88.9 12.1 %copy-start.2 = (s32[2,1]{0,1:T(1,128)S(1)}, s32[2,1]{0,1:T(1,128)}, u32[]{:S(2)}) copy-start(s32[2,1]{0,1:T(1,128)} %param.11) | copy-start | bytes 28
  88.9 12.1 %collective-permute-start.3 = (f32[64,1024]{1,0:T(8,128)S(1)}, f32[64,1024]{1,0:T(8,128)S(1)}, u32[]{:S(2)}, u32[]{:S(2)}) collective-permute-start(f32[64,1024]{1,0:T(8,128)S(1)} %get-tuple-element.20), channel_id=1, source_target_pairs={{0,3},{1,0},{2,1},{3,2},{4,7},{5,4},{6,5},{7,6},{8,11},{9,8},{10,9... | collective-permute-start | bytes 786440 | tf_op jit(solution)/shard_map/ppermute | solution.py:282
